TPU v7x, 32 devices: a whole 2x2x4 slice. The times are simulated.
32 devices in a mesh: ctx: 4 (over y, core), ep: 8 (over z, x).
Axes of the slice: x: 2, y: 2, z: 4, core: 2. Of those that a mesh axis runs over, the one named last changes fastest.
Arguments:
- resid: bfloat16 [4096, 2048], P(('ctx', 'ep')), may hold values from -12 to 12
- mixed_qkv: bfloat16 [4096, 4096], P(('ctx', 'ep')), may hold values from -6 to 6
- out_gate: bfloat16 [4096, 2048], P(('ctx', 'ep')), may hold values from -6 to 6
- beta: float32 [16, 4096], P(None, ('ctx', 'ep')), may hold values from 0.001 to 0.95
- log_decay: float32 [16, 4096], P(None, ('ctx', 'ep')), may hold values from -1 to 0
- conv_weight: float32 [4, 4096], replicated, may hold values from -3 to 3
- head_gain: float32 [128], replicated, may hold values from 0.25 to 1.75
- moe_gain: float32 [2048], replicated, may hold values from 0.25 to 1.75
- routes: int32 [4096, 3], P(('ctx', 'ep')), may hold values from 0 to 7, all different within a row; in each aligned block of 128 rows (0 to 127, 128 to 255, ...) at most 60 rows name the same one
- route_gates: float32 [4096, 3], P(('ctx', 'ep')), may hold values from 0.1 to 1
- w_in: bfloat16 [8, 2048, 1024], P('ep', 'ctx'), may hold values from -0.125 to 0.125
- w_out: bfloat16 [8, 512, 2048], P('ep', None, 'ctx'), may hold values from -0.25 to 0.25
Outputs:
- mixer_out: bfloat16 [4096, 2048], P(('ctx', 'ep'))
- layer_out: bfloat16 [4096, 2048], P(('ctx', 'ep'))
Inputs may be any that keep to these rules, and one draw needn't show every extreme that they name: `routes`: in the rows of one device no expert is named more than 60 times, a bound that some block reaches.
All inputs are finite; a program needn't handle non-finite values.
Results may differ from a plain program's by a relative error of at most 0.0037.
Values may be sent and summed in bfloat16 or wider, within the bound.
No kernel may reach another device: no remote copies, remote signals or barrier semaphores. Data moves between devices by JAX's collectives and lax.ppermute only.
A program may use at most 320 MiB of HBM per device.

v0:
```python
import jax
import jax.numpy as jnp
from jax import lax
from jax.sharding import PartitionSpec as P

HK = 8
VALUE_HEAD_SET = 16
DK = 128
DV = 128
MOE_H = 512
CONV = 4
TOPK = 3
TOK_DEV = 128


precise = lax.Precision.HIGHEST


def from_behind(value, axis, steps):
    count = lax.axis_size(axis)
    leading, last = (max(0, -steps), min(count, count - steps))
    return lax.ppermute(value, axis, [(source, source + steps) for source in range(leading, last)])


def entering(value, axis, join, neutral, backward):
    count, mine = (lax.axis_size(axis), lax.axis_index(axis))
    pieces = jax.tree.map(lambda part: lax.all_gather(part, axis), value)
    if backward:
        pieces = jax.tree.map(lambda part: part[::-1], pieces)
        mine = count - 1 - mine
    so_far = jax.tree.map(
        lambda part, zero: jnp.full_like(part, 0) + jnp.asarray(zero, part.dtype), value, neutral
    )

    def lap(position, so_far):
        longer = join(so_far, jax.tree.map(lambda part: part[position], pieces))
        return jax.tree.map(lambda new, old: jnp.where(position < mine, new, old), longer, so_far)

    return lax.fori_loop(0, count - 1, lap, so_far)


def short_conv(padded, conv_weight, row_count):
    qkv_data = padded.astype(jnp.float32)
    conv_sum = jnp.zeros((row_count, qkv_data.shape[1]), jnp.float32)
    for offset in range(conv_weight.shape[0]):
        conv_sum = conv_sum + qkv_data[offset : offset + row_count] * conv_weight[offset]
    return jax.nn.silu(conv_sum)


def local_terms(conv_out, beta, log_decay):
    row_count = conv_out.shape[0]
    head_group = VALUE_HEAD_SET // HK
    queries = conv_out[:, : HK * DK].reshape(row_count, HK, DK)
    keys_hat = conv_out[:, HK * DK : 2 * HK * DK].reshape(row_count, HK, DK)
    values = conv_out[:, 2 * HK * DK :].reshape(row_count, VALUE_HEAD_SET, DV)
    queries = (
        queries
        * lax.rsqrt(jnp.sum(queries * queries, axis=-1, keepdims=True) + 1e-06)
        * DK ** (-0.5)
    )
    keys_hat = keys_hat * lax.rsqrt(jnp.sum(keys_hat * keys_hat, axis=-1, keepdims=True) + 1e-06)
    queries = jnp.repeat(queries, head_group, axis=1).transpose(1, 0, 2)
    keys_hat = jnp.repeat(keys_hat, head_group, axis=1).transpose(1, 0, 2)
    values = values.transpose(1, 0, 2)
    cumulative = jnp.cumsum(log_decay, axis=1)
    positions = jnp.arange(row_count)
    strict_mask = (positions[:, None] > positions[None, :])[None]
    causal_mask = (positions[:, None] >= positions[None, :])[None]
    log_gap = cumulative[:, :, None] - cumulative[:, None, :]
    fading = jnp.where(causal_mask, jnp.exp(jnp.where(causal_mask, log_gap, 0.0)), 0.0)
    key_key = jnp.einsum("htd,hsd->hts", keys_hat, keys_hat, precision=precise)
    mixing = jnp.where(strict_mask, beta[:, :, None] * fading * key_key, 0.0)
    identity_t = jnp.eye(row_count, dtype=jnp.float32)
    weights_solved = lax.linalg.triangular_solve(
        identity_t[None] + mixing, identity_t[None] * beta[:, :, None], left_side=True, lower=True
    )
    block_fade = jnp.exp(cumulative)
    tail_fade = jnp.exp(cumulative[:, -1:] - cumulative)
    fresh_vals = jnp.einsum("hts,hsv->htv", weights_solved, values, precision=precise)
    carried = jnp.einsum(
        "hts,hsk->htk", weights_solved, block_fade[:, :, None] * keys_hat, precision=precise
    )
    faded_keys = tail_fade[:, :, None] * keys_hat
    transition = block_fade[:, -1][:, None, None] * jnp.eye(DK, dtype=jnp.float32)[
        None
    ] - jnp.einsum("htj,htk->hjk", carried, faded_keys, precision=precise)
    state_add = jnp.einsum("htv,htk->hvk", fresh_vals, faded_keys, precision=precise)
    scores = fading * jnp.einsum("htd,hsd->hts", queries, keys_hat, precision=precise)
    return (queries, block_fade, scores, fresh_vals, carried, transition, state_add)


def head_outputs(queries, block_fade, scores, fresh_vals, carried, start_state):
    new_vals = fresh_vals - jnp.einsum("htk,hvk->htv", carried, start_state, precision=precise)
    from_state = jnp.einsum("htk,hvk->htv", queries, start_state, precision=precise)
    return block_fade[:, :, None] * from_state + jnp.einsum(
        "hts,hsv->htv", scores, new_vals, precision=precise
    )


def gated_norm(head_out, out_gate, head_gain):
    row_count = head_out.shape[1]
    per_token = head_out.transpose(1, 0, 2)
    scaled = (
        per_token
        * lax.rsqrt(jnp.mean(per_token * per_token, axis=-1, keepdims=True) + 1e-06)
        * head_gain
    )
    gate_vals = out_gate.astype(jnp.float32).reshape(row_count, VALUE_HEAD_SET, DV)
    return (
        (scaled * jax.nn.silu(gate_vals))
        .reshape(row_count, VALUE_HEAD_SET * DV)
        .astype(jnp.bfloat16)
    )


def compose(earlier, later):
    first_map, first_add = earlier
    second_map, second_add = later
    joined_map = jnp.einsum("hij,hjk->hik", first_map, second_map, precision=precise)
    joined_add = jnp.einsum("hvj,hjk->hvk", first_add, second_map, precision=precise) + second_add
    return (joined_map, joined_add)


def compose_back(higher, lower):
    return compose(lower, higher)


def expert_mlp(token_rows, weight_in, weight_out):
    projected = jnp.dot(token_rows, weight_in, preferred_element_type=jnp.float32)
    activated = (jax.nn.silu(projected[:, :MOE_H]) * projected[:, MOE_H:]).astype(jnp.bfloat16)
    return jnp.dot(activated, weight_out, preferred_element_type=jnp.float32).astype(jnp.bfloat16)


def shards(
    resid,
    mixed_qkv,
    out_gate,
    beta,
    log_decay,
    conv_weight,
    head_gain,
    moe_gain,
    routes,
    route_gates,
    w_in,
    w_out,
):
    row_count = mixed_qkv.shape[0]
    rim_rows = from_behind(mixed_qkv[row_count - CONV + 1 :], ("ctx", "ep"), 1)
    conv_out = short_conv(jnp.concatenate([rim_rows, mixed_qkv], axis=0), conv_weight, row_count)
    queries, block_fade, scores, fresh_vals, carried, transition, state_add = local_terms(
        conv_out, beta, log_decay
    )
    neutral = (
        jnp.broadcast_to(jnp.eye(DK, dtype=jnp.float32)[None], transition.shape),
        jnp.zeros_like(state_add),
    )
    within_group = entering((transition, state_add), "ep", compose, neutral, False)
    through_own = compose(within_group, (transition, state_add))
    after_own = entering((transition, state_add), "ep", compose_back, neutral, True)
    group_whole = compose(through_own, after_own)
    before_group = entering(group_whole, "ctx", compose, neutral, False)
    start_state = compose(before_group, within_group)[1]
    head_out = head_outputs(queries, block_fade, scores, fresh_vals, carried, start_state)
    mixer_out = gated_norm(head_out, out_gate, head_gain)
    residual_mid = resid.astype(jnp.float32) + mixer_out.astype(jnp.float32)
    moe_input = (
        residual_mid
        * lax.rsqrt(jnp.mean(residual_mid * residual_mid, axis=-1, keepdims=True) + 1e-06)
        * moe_gain
    ).astype(jnp.bfloat16)
    expert_count = lax.axis_size("ep")
    capacity = max(2, (5 * TOK_DEV * TOPK + 4 * expert_count - 1) // (4 * expert_count))
    slot_count = expert_count * capacity
    width = moe_input.shape[1]
    flat_routes = routes.reshape(-1)
    one_hot = (flat_routes[:, None] == jnp.arange(expert_count)[None, :]).astype(jnp.int32)
    earlier_same = jnp.cumsum(one_hot, axis=0) - one_hot
    slot_rank = jnp.sum(earlier_same * one_hot, axis=1)
    slot_ids = flat_routes * capacity + slot_rank
    selector = (slot_ids[None, :] == jnp.arange(slot_count)[:, None]).astype(jnp.int32)
    selector = jnp.sum(selector.reshape(slot_count, row_count, TOPK), axis=2).astype(jnp.bfloat16)
    send_rows = jnp.dot(selector, moe_input, preferred_element_type=jnp.float32).astype(
        jnp.bfloat16
    )
    send_rows = send_rows.reshape(expert_count, capacity, width)
    whole_in, whole_out = (
        lax.all_gather(w_in, "ctx", axis=1, tiled=True),
        lax.all_gather(w_out, "ctx", axis=2, tiled=True),
    )
    slot_rows = lax.all_to_all(send_rows, "ep", split_axis=0, concat_axis=0, tiled=True)
    flat_rows = slot_rows.reshape(-1, width)
    result_rows = expert_mlp(flat_rows, whole_in[0], whole_out[0]).reshape(slot_rows.shape)
    returned = lax.all_to_all(result_rows, "ep", split_axis=0, concat_axis=0, tiled=True)
    returned_flat = returned.reshape(slot_count, width)
    picked_rows = returned_flat[slot_ids].reshape(row_count, TOPK, width)
    combined = jnp.einsum("tk,tkd->td", route_gates, picked_rows.astype(jnp.float32))
    layer_out = (residual_mid + combined).astype(jnp.bfloat16)
    return (mixer_out, layer_out)


def solution(mesh):
    return jax.shard_map(
        shards,
        mesh=mesh,
        in_specs=(
            P(("ctx", "ep"), None),
            P(("ctx", "ep"), None),
            P(("ctx", "ep"), None),
            P(None, ("ctx", "ep")),
            P(None, ("ctx", "ep")),
            P(),
            P(),
            P(),
            P(("ctx", "ep"), None),
            P(("ctx", "ep"), None),
            P("ep", "ctx", None),
            P("ep", None, "ctx"),
        ),
        out_specs=(P(("ctx", "ep"), None), P(("ctx", "ep"), None)),
        check_vma=False,
    )
```

profile of v0, /device:TPU:0, one launch (start us, length us, event | category | flops | bytes accessed | tf_op | source)
XLA Modules:
  0.0 816.0 jit_solution(8747101318717336057)
XLA Ops:
  8.1 4.8 collective-permute-start
  18.2 4.6 divide_multiply_fusion
  28.0 158.6 %custom-call.3 = f32[16,1,128,128]{2,3,1,0:T(8,128)} custom-call(f32[16,1,128,128]{3,2,1,0:T(8,128)} %fusion.39), custom_call_target="InvertDiagBlocksLowerTriangular" | custom-call | tf_op jit(solution)/shard_map/triangular_solve | solution.py:74
  204.3 119.3 %all-gather.17.cloned.1.call-done = f32[128,128,128]{2,1,0:T(8,128)} async-done(((f32[16,128,128]{2,1,0:T(8,128)}), f32[128,128,128]{2,1,0:T(8,128)}) %all-gather.17.cloned.1.call-update) | async-done | bytes 8388624 | tf_op jit(solution)/shard_map/all_gather | solution.py:27
  323.6 7.7 rev.7
  331.4 117.5 %all-gather.15.cloned.1.call-done = f32[128,128,128]{2,1,0:T(8,128)} async-done(((f32[16,128,128]{2,1,0:T(8,128)}), f32[128,128,128]{2,1,0:T(8,128)}) %all-gather.15.cloned.1.call-update) | async-done | bytes 8388624 | tf_op jit(solution)/shard_map/all_gather | solution.py:27
  448.9 7.7 rev.6
  456.7 71.4 %while.46 = (s32[]{:T(128)}, f32[16,128,128]{1,2,0:T(8,128)S(1)}, f32[16,128,128]{1,2,0:T(8,128)}, s32[]{:T(128)}, f32[8,16,128,128]{3,2,1,0:T(8,128)}, /*index=5*/f32[8,16,128,128]{3,2,1,0:T(8,128)}, s32[]{:T(128)}, s32[]{:T(128)}) while((s32[]{:T(128)}, f32[16,128,128]{1,2,0:T(8,128)S(1)}, f32[16,128,128]{1,2,0:T(8,128)}, ...), condition=%wide.region_4.5_spmd.clone, body=%wide.region_3.4_spmd.clone.sunk | while | flops 806617088 | bytes 17828460 | solution.py:39
  469.8 4.1 fusion.118
  480.0 4.1 fusion.118
  490.2 4.1 fusion.118
  500.4 4.1 fusion.118
  510.6 4.1 fusion.118
  528.1 4.8 convolution_add_fusion.2
  533.0 37.2 %while.47 = (s32[]{:T(128)}, f32[16,128,128]{2,1,0:T(8,128)S(1)}, f32[16,128,128]{2,1,0:T(8,128)S(1)}, s32[]{:T(128)}, f32[8,16,128,128]{3,2,1,0:T(8,128)}, /*in...) while((s32[]{:T(128)}, f32[16,128,128]{2,1,0:T(8,128)S(1)}, f32[16,128,128]{2,1,0:T(8,128)S(1)}, ...), condition=%wide.region_6.7_spmd.clone, body=%wide.region_5.6_spmd.clone.sunk | while | flops 806354944 | bytes 10486890 | solution.py:39
  592.2 14.2 %all-gather.21.cloned.1.call-done = f32[64,128,128]{2,1,0:T(8,128)} async-done(((f32[16,128,128]{2,1,0:T(8,128)}), f32[64,128,128]{2,1,0:T(8,128)}) %all-gather.21.cloned.1.call-update) | async-done | bytes 4194320 | tf_op jit(solution)/shard_map/all_gather | solution.py:27
  606.4 35.9 %all-gather.19.cloned.1.call-done = f32[64,128,128]{2,1,0:T(8,128)} async-done(((f32[16,128,128]{2,1,0:T(8,128)}), f32[64,128,128]{2,1,0:T(8,128)}) %all-gather.19.cloned.1.call-update) | async-done | bytes 4194320 | tf_op jit(solution)/shard_map/all_gather | solution.py:27
  642.3 21.3 %while.48 = (s32[]{:T(128)}, f32[16,128,128]{1,2,0:T(8,128)}, s32[]{:T(128)}, f32[4,16,128,128]{3,2,1,0:T(8,128)}, f32[4,16,128,128]{3,2,1,0:T(8,128)}, /*index=5*/s32[]{:T(128)}, s32[]{:T(128)}) while((s32[]{:T(128)}, f32[16,128,128]{1,2,0:T(8,128)}, s32[]{:T(128)}, f32[4,16,128,128]{3,2,1,0:T(8,128)}, ...), condition=%wide.region_8.9_spmd.clone, body=%wide.region_7.8_spmd.clone.sunk | while | flops 403701760 | bytes 11536483 | solution.py:39
  652.3 4.2 fusion.125
  677.5 5.8 all-to-all-start
  683.8 48.2 %all-to-all-done = bf16[8,60,2048]{2,1,0:T(8,128)(2,1)S(1)} async-done(((bf16[8,60,2048]{2,1,0:T(8,128)(2,1)}), bf16[8,60,2048]{2,1,0:T(8,128)(2,1)S(1)}, u32[]{:S(2)}, u32[]{:S(2)}) %all-to-all-start) | async-done | bytes 1966112 | tf_op jit(solution)/shard_map/all_to_all | solution.py:191
  733.5 6.3 fusion.28
  744.7 4.7 all-to-all-start.1
  749.9 47.5 %all-to-all-done.1 = bf16[8,60,2048]{2,1,0:T(8,128)(2,1)} async-done(((bf16[8,60,2048]{2,1,0:T(8,128)(2,1)}), bf16[8,60,2048]{2,1,0:T(8,128)(2,1)}, u32[]{:S(2)}, u32[]{:S(2)}) %all-to-all-start.1) | async-done | bytes 1966112 | tf_op jit(solution)/shard_map/all_to_all | solution.py:194
  (203 shorter events, 187.6 us)
Async XLA Ops:
  7.2 316.5 %all-gather.17.cloned.1.call-start = ((), (), s32[]{:S(2)}) async-start(), calls=%async_computation.5 | async-start | bytes 9437184 | tf_op jit(solution)/shard_map/all_gather | solution.py:27
  8.1 8.8 %collective-permute-start = (bf16[3,4096]{1,0:T(4,128)(2,1)S(1)}, bf16[3,4096]{1,0:T(4,128)(2,1)S(1)}, u32[]{:S(2)}, u32[]{:S(2)}) collective-permute-start(bf16[3,4096]{1,0:T(4,128)(2,1)S(1)} %slice.60), channel_id=1, source_target_pairs={{0,1},{1,2},{2,3},{3,4},{4,5},{5,6},{6,7},{7,8},{8,9},{9,10},{10,1... | collective-permute-start | bytes 73736 | tf_op jit(solution)/shard_map/ppermute | solution.py:22
  24.7 3.4 copy-start.11
  24.7 165.3 %slice-start = ((f32[128,4096]{0,1:T(8,128)}), f32[128,2048]{0,1:T(8,128)S(1)}, s32[]{:S(2)}) async-start(f32[128,4096]{0,1:T(8,128)} %copy-done.2), calls=%async_computation.8 | async-start | bytes 2097152 | tf_op jit(solution)/shard_map/slice | solution.py:55
  195.3 3.7 copy-start.13
  198.2 250.7 %all-gather.15.cloned.1.call-start = ((), (), s32[]{:S(2)}) async-start(), calls=%async_computation.4 | async-start | bytes 9437184 | tf_op jit(solution)/shard_map/all_gather | solution.py:27
  204.1 402.3 %all-gather.21.cloned.1.call-start = ((), (), s32[]{:S(2)}) async-start(), calls=%async_computation.7 | async-start | bytes 5242880 | tf_op jit(solution)/shard_map/all_gather | solution.py:27
  528.1 4.9 copy-start.1
  573.6 68.8 %all-gather.19.cloned.1.call-start = ((), (), s32[]{:S(2)}) async-start(), calls=%async_computation.6 | async-start | bytes 5242880 | tf_op jit(solution)/shard_map/all_gather | solution.py:27
  576.9 2.8 copy-start.19
  579.0 5.3 copy-start.16
  579.0 154.5 %all-gather.11.cloned.1.call-start = ((), (), s32[]{:S(2)}) async-start(), calls=%async_computation.2 | async-start | bytes 5242880 | tf_op jit(solution)/shard_map/all_gather | solution.py:188
  580.2 7.4 copy-start.12
  585.3 5.6 copy-start
  663.7 3.5 copy-start.4
  667.2 2.4 copy-start.6
  667.2 2.4 copy-start.8
  669.5 2.3 copy-start.15
  671.9 2.0 copy-start.14
  674.9 132.6 %copy-start.9 = (bf16[128,2048]{1,0:T(8,128)(2,1)}, bf16[128,2048]{1,0:T(8,128)(2,1)S(1)}, u32[]{:S(2)}) copy-start(bf16[128,2048]{1,0:T(8,128)(2,1)S(1)} %copy.117) | copy-start | bytes 1572868
  677.5 54.5 %all-to-all-start = ((bf16[8,60,2048]{2,1,0:T(8,128)(2,1)}), bf16[8,60,2048]{2,1,0:T(8,128)(2,1)S(1)}, u32[]{:S(2)}, u32[]{:S(2)}) async-start(bf16[8,60,2048]{2,1,0:T(8,128)(2,1)} %reshape.207), calls=%async_computation | async-start | bytes 4194304 | tf_op jit(solution)/shard_map/all_to_all | solution.py:191
  683.2 56.5 %all-gather.13.cloned.1.call-start = ((), (), s32[]{:S(2)}) async-start(), calls=%async_computation.3 | async-start | bytes 2621440 | tf_op jit(solution)/shard_map/all_gather | solution.py:189
  744.7 4.9 copy-start.20
  744.7 52.6 %all-to-all-start.1 = ((bf16[8,60,2048]{2,1,0:T(8,128)(2,1)}), bf16[8,60,2048]{2,1,0:T(8,128)(2,1)}, u32[]{:S(2)}, u32[]{:S(2)}) async-start(bf16[8,60,2048]{2,1,0:T(8,128)(2,1)} %reshape.209), calls=%async_computation.1 | async-start | bytes 4194304 | tf_op jit(solution)/shard_map/all_to_all | solution.py:194
  (8 other events, 11.1 us)
Sparse Core Ops, SparseCore 0:
  198.4 125.2 all-gather.16
  325.8 123.1 all-gather.14
  573.7 32.6 all-gather.20
  607.8 34.4 all-gather.18
  643.7 34.4 all-gather.10
  685.3 23.0 all-gather.12
where the time goes:
time: 827 us; the launch traced here: 816 us
  waiting for transfers between devices  384 us (46%)
  other arithmetic  171 us (21%)
  matrix products  154 us (19%)
  local copies, waits for them, and re-layouts  75.2 us (9%)
  starting transfers between devices  16.2 us (2%)
  between operations  15.2 us (2%)
    all_gather x4, waiting for transfers between devices, entering(): pieces = jax.tree.map(lambda part: lax.all_gather(part, axis), value)  287 us
    another operation x1, other arithmetic, local_terms(): lax.linalg.triangular_solve(identity_t[None] + mixing, identity_t[None] *...  159 us
    dot_general x20, matrix products, compose(): jnp.einsum('hvj,hjk->hvk', first_add, second_map, precision=precise)  71.8 us
    all_to_all x1, waiting for transfers between devices, shards(): lax.all_to_all(send_rows, 'ep', split_axis=0, concat_axis=0, tiled=True)  48.2 us
    all_to_all x1, waiting for transfers between devices, shards(): lax.all_to_all(result_rows, 'ep', split_axis=0, concat_axis=0, tiled=True)  47.5 us
    dot_general x16, matrix products, compose(): jnp.einsum('hij,hjk->hik', first_map, second_map, precision=precise)  44.3 us
  transfers between devices with their start and end apart: 9, of which 6 were waited for; matrix products, arithmetic and copies ran while one was open for 9% of the time, Pallas kernels for 0%

commit v1 on v0

v1 whole, which is shorter than its diff:
```python
import functools

import jax
import jax.numpy as jnp
from jax import lax
from jax.experimental import pallas as pl
from jax.experimental.pallas import tpu as pltpu
from jax.sharding import PartitionSpec as P

HK = 8
VALUE_HEAD_SET = 16
DK = 128
DV = 128
MOE_H = 512
CONV = 4
TOPK = 3
TOK_DEV = 128
GROUP = VALUE_HEAD_SET // HK
HALO = 8
STEP_KEYS = 2

f32 = jnp.float32
bf16 = jnp.bfloat16
VMEM_LIMIT = 48 << 20


def round_up(value, multiple):
    return (value + multiple - 1) // multiple * multiple


def dot(lhs, rhs):
    return jnp.dot(lhs, rhs, preferred_element_type=f32)


def dot_nt(lhs, rhs):
    return lax.dot_general(lhs, rhs, (((1,), (1,)), ((), ())), preferred_element_type=f32)


def halves(value):
    high = value.astype(bf16)
    return high, (value - high.astype(f32)).astype(bf16)


def one_pass(lhs, rhs):
    return dot(lhs.astype(bf16), rhs.astype(bf16))


def three_pass(lhs, rhs):
    (lhs_high, lhs_low), (rhs_high, rhs_low) = halves(lhs), halves(rhs)
    return dot(lhs_high, rhs_high) + (dot(lhs_high, rhs_low) + dot(lhs_low, rhs_high))


def three_pass_nt(lhs, rhs):
    (lhs_high, lhs_low), (rhs_high, rhs_low) = lhs, rhs
    return dot_nt(lhs_high, rhs_high) + (dot_nt(lhs_high, rhs_low) + dot_nt(lhs_low, rhs_high))


def silu(value):
    return value * jax.nn.sigmoid(value)


def conv_silu(ref, halo_ref, weight_ref):
    rows = ref.shape[0]
    padded = jnp.concatenate([halo_ref[...].astype(f32), ref[...].astype(f32)], axis=0)
    total = padded[HALO:] * weight_ref[CONV - 1 : CONV, :]
    for tap in range(CONV - 1):
        start = HALO - (CONV - 1) + tap
        total = total + padded[start : start + rows] * weight_ref[tap : tap + 1, :]
    return silu(total)


def local_kernel(
    splits,
    part,
    part_rows,
    q_ref,
    k_ref,
    v_ref,
    qh_ref,
    kh_ref,
    vh_ref,
    qw_ref,
    kw_ref,
    vw_ref,
    beta_ref,
    decay_ref,
    send_ref,
    own_ref,
    reader_ref,
):
    rows = q_ref.shape[0]
    queries, keys, values = (
        conv_silu(q_ref, qh_ref, qw_ref),
        conv_silu(k_ref, kh_ref, kw_ref),
        conv_silu(v_ref, vh_ref, vw_ref),
    )
    row_ids = lax.broadcasted_iota(jnp.int32, (rows, rows), 0)
    col_ids = lax.broadcasted_iota(jnp.int32, (rows, rows), 1)
    strict, causal, diagonal = row_ids > col_ids, row_ids >= col_ids, row_ids == col_ids
    identity = jnp.where(diagonal, 1.0, 0.0).astype(f32)

    query_hats, key_hats, grams, scores_raw = [], [], [], []
    for key in range(STEP_KEYS):
        span = slice(key * DK, (key + 1) * DK)
        query, key_rows = queries[:, span], keys[:, span]
        query = (
            query
            * lax.rsqrt(jnp.sum(query * query, axis=1, keepdims=True) + 1e-06)
            * DK ** (-0.5)
        )
        key_rows = key_rows * lax.rsqrt(
            jnp.sum(key_rows * key_rows, axis=1, keepdims=True) + 1e-06
        )
        query_hats.append(query)
        key_hats.append(key_rows)
        query_parts, key_parts = halves(query), halves(key_rows)
        grams.append(three_pass_nt(key_parts, key_parts))
        scores_raw.append(three_pass_nt(query_parts, key_parts))

    heads = range(STEP_KEYS * GROUP)
    lower, betas, fades, tails, fadings, wholes = [], [], [], [], [], []
    for head in heads:
        key = head // GROUP
        beta_row = beta_ref[key, head % GROUP : head % GROUP + 1, :]
        decay_row = decay_ref[key, head % GROUP : head % GROUP + 1, :]
        beta_col = jnp.sum(jnp.where(diagonal, beta_row, 0.0), axis=1, keepdims=True)
        decay_col = jnp.sum(jnp.where(diagonal, decay_row, 0.0), axis=1, keepdims=True)
        cum_col = jnp.sum(jnp.where(causal, decay_row, 0.0), axis=1, keepdims=True)
        cum_row = jnp.sum(jnp.where(row_ids <= col_ids, decay_col, 0.0), axis=0, keepdims=True)
        last = jnp.sum(decay_row, axis=1, keepdims=True)
        fading = jnp.where(causal, jnp.exp(jnp.where(causal, cum_col - cum_row, 0.0)), 0.0)
        lower.append(jnp.where(strict, beta_col * fading * grams[key], 0.0))
        betas.append(beta_col)
        fades.append(jnp.exp(cum_col))
        tails.append(jnp.exp(jnp.minimum(last - cum_col, 0.0)))
        fadings.append(fading)

    solved = [
        jnp.where(row_ids // 2 == col_ids // 2, identity - lower[head], 0.0) for head in heads
    ]
    size = 2
    while size < rows:
        joins = (row_ids // (2 * size) == col_ids // (2 * size)) & (
            row_ids // size != col_ids // size
        )
        parts = [solved[head].astype(bf16) for head in heads]
        inner = [
            dot(parts[head], jnp.where(joins, lower[head], 0.0).astype(bf16)) for head in heads
        ]
        solved = [solved[head] - dot(inner[head].astype(bf16), parts[head]) for head in heads]
        size *= 2
    residues = [
        (identity - solved[head]) - three_pass(lower[head], solved[head]) for head in heads
    ]
    solved = [solved[head] + one_pass(solved[head], residues[head]) for head in heads]

    for head in heads:
        key = head // GROUP
        value_span = slice(head * DV, (head + 1) * DV)
        fresh_carried = three_pass(
            solved[head],
            jnp.concatenate(
                [
                    betas[head] * values[:, value_span],
                    (betas[head] * fades[head]) * key_hats[key],
                ],
                axis=1,
            ),
        )
        sums = three_pass(fresh_carried.T, tails[head] * key_hats[key])
        transition, state_add = sums[DV:], sums[:DV]
        for split in range(splits):
            send_ref[head, split, :DK, :] = transition.astype(bf16)
            added = state_add[split * part : (split + 1) * part].astype(bf16)
            if part == part_rows:
                send_ref[head, split, DK:, :] = added
            else:
                send_ref[head, split, DK:, :] = jnp.concatenate(
                    [added, jnp.zeros((part_rows - part, DK), bf16)], axis=0
                )
        mixed = three_pass(fadings[head] * scores_raw[key], fresh_carried)
        own_ref[head] = mixed[:, :DV]
        reader_ref[head] = fades[head] * query_hats[key] - mixed[:, DV:]


def local_terms(mixed_qkv, halo, conv_weight, beta, log_decay, splits, part_rows):
    rows = mixed_qkv.shape[0]
    key_cols, value_cols = STEP_KEYS * DK, STEP_KEYS * GROUP * DV
    steps = HK // STEP_KEYS
    value_from = 2 * HK * DK // value_cols
    part = DV // splits
    col_maps = (
        (key_cols, lambda i: (0, i)),
        (key_cols, lambda i: (0, steps + i)),
        (value_cols, lambda i: (0, value_from + i)),
    )
    specs = [
        pl.BlockSpec((height, width), index)
        for height in (rows, HALO, CONV)
        for width, index in col_maps
    ]
    per_head = pl.BlockSpec((STEP_KEYS, GROUP, rows), lambda i: (i, 0, 0))
    step_heads = STEP_KEYS * GROUP
    return pl.pallas_call(
        functools.partial(local_kernel, splits, part, part_rows),
        grid=(steps,),
        in_specs=specs + [per_head, per_head],
        out_specs=[
            pl.BlockSpec((step_heads, splits, DK + part_rows, DK), lambda i: (i, 0, 0, 0)),
            pl.BlockSpec((step_heads, rows, DV), lambda i: (i, 0, 0)),
            pl.BlockSpec((step_heads, rows, DK), lambda i: (i, 0, 0)),
        ],
        out_shape=[
            jax.ShapeDtypeStruct((VALUE_HEAD_SET, splits, DK + part_rows, DK), bf16),
            jax.ShapeDtypeStruct((VALUE_HEAD_SET, rows, DV), f32),
            jax.ShapeDtypeStruct((VALUE_HEAD_SET, rows, DK), f32),
        ],
        compiler_params=pltpu.CompilerParams(
            dimension_semantics=("arbitrary",), vmem_limit_bytes=VMEM_LIMIT
        ),
        name="local_terms",
    )(
        *[mixed_qkv] * 3,
        *[halo] * 3,
        *[conv_weight] * 3,
        beta.reshape(HK, GROUP, rows),
        log_decay.reshape(HK, GROUP, rows),
    )


def scan_kernel(fade_ref, sums_ref, start_ref, state_ref):
    step, block = pl.program_id(0), sums_ref.shape[0]

    @pl.when(step == 0)
    def _():
        state_ref[...] = jnp.zeros_like(state_ref)

    state = state_ref[...]
    for place in range(block):
        high, low = halves(state)
        start_ref[place] = high
        transition = sums_ref[place, :DK, :]
        moved = dot(high, transition) + dot(low, transition)
        added = sums_ref[place, DK:, :].astype(f32)
        state = (fade_ref[step * block + place] * state - moved) + added
    state_ref[...] = state


def scan_states(fade, sums):
    count, height = sums.shape[:2]
    part_rows = height - DK
    block = 8
    return pl.pallas_call(
        scan_kernel,
        grid_spec=pltpu.PrefetchScalarGridSpec(
            num_scalar_prefetch=1,
            grid=(count // block,),
            in_specs=[pl.BlockSpec((block, height, DK), lambda i, fade: (i, 0, 0))],
            out_specs=pl.BlockSpec((block, part_rows, DK), lambda i, fade: (i, 0, 0)),
            scratch_shapes=[pltpu.VMEM((part_rows, DK), f32)],
        ),
        out_shape=jax.ShapeDtypeStruct((count, part_rows, DK), bf16),
        compiler_params=pltpu.CompilerParams(
            dimension_semantics=("arbitrary",), vmem_limit_bytes=VMEM_LIMIT
        ),
        name="scan_states",
    )(fade, sums)


def route_kernel(capacity, routes_ref, gates_ref, select_ref, gather_ref):
    rows = routes_ref.shape[1]
    experts = select_ref.shape[0] // capacity
    expert_ids = lax.broadcasted_iota(jnp.int32, (experts, rows), 0)
    chosen = jnp.zeros((experts, rows), jnp.bool_)
    gates = jnp.zeros((experts, rows), f32)
    for choice in range(TOPK):
        named = routes_ref[choice : choice + 1, :] == expert_ids
        chosen = chosen | named
        gates = gates + jnp.where(named, gates_ref[choice : choice + 1, :], 0.0)
    earlier = lax.broadcasted_iota(jnp.int32, (rows, rows), 0) < lax.broadcasted_iota(
        jnp.int32, (rows, rows), 1
    )
    rank = dot(
        jnp.where(chosen, 1.0, 0.0).astype(bf16), jnp.where(earlier, 1.0, 0.0).astype(bf16)
    )
    slot = jnp.where(chosen, rank, -1.0).astype(jnp.int32)
    slot_ids = lax.broadcasted_iota(jnp.int32, (capacity, rows), 0)
    for expert in range(experts):
        span = slice(expert * capacity, (expert + 1) * capacity)
        taken = slot_ids == slot[expert : expert + 1, :]
        select_ref[span, :] = jnp.where(taken, 1.0, 0.0).astype(bf16)
        gather_ref[span, :] = jnp.where(taken, gates[expert : expert + 1, :], 0.0)


def route_tables(routes, route_gates, experts, capacity):
    rows = routes.shape[0]
    slots = experts * capacity
    return pl.pallas_call(
        functools.partial(route_kernel, capacity),
        out_shape=[
            jax.ShapeDtypeStruct((slots, rows), bf16),
            jax.ShapeDtypeStruct((slots, rows), f32),
        ],
        name="route_tables",
    )(routes.T, route_gates.T)


def mixer_kernel(
    own_ref,
    reader_ref,
    state_ref,
    gate_ref,
    resid_ref,
    head_gain_ref,
    moe_gain_ref,
    select_ref,
    mixer_ref,
    middle_ref,
    rows_ref,
):
    squares = None
    for head in range(VALUE_HEAD_SET):
        span = slice(head * DV, (head + 1) * DV)
        state = state_ref[head]
        high, low = halves(reader_ref[head])
        head_out = own_ref[head] + (dot_nt(high, state) + dot_nt(low, state))
        scaled = (
            head_out
            * lax.rsqrt(jnp.mean(head_out * head_out, axis=1, keepdims=True) + 1e-06)
            * head_gain_ref[...]
        )
        mixed = (scaled * silu(gate_ref[:, span].astype(f32))).astype(bf16)
        mixer_ref[:, span] = mixed
        middle = resid_ref[:, span].astype(f32) + mixed.astype(f32)
        middle_ref[:, span] = middle
        part = jnp.sum(middle * middle, axis=1, keepdims=True)
        squares = part if squares is None else squares + part
    width = resid_ref.shape[1]
    moe_input = (
        middle_ref[...] * lax.rsqrt(squares / width + 1e-06) * moe_gain_ref[...]
    ).astype(bf16)
    rows_ref[...] = dot(select_ref[...], moe_input).astype(bf16)


def mixer(own, reader, state, out_gate, resid, head_gain, moe_gain, select):
    rows, width = resid.shape
    return pl.pallas_call(
        mixer_kernel,
        out_shape=[
            jax.ShapeDtypeStruct((rows, width), bf16),
            jax.ShapeDtypeStruct((rows, width), f32),
            jax.ShapeDtypeStruct((select.shape[0], width), bf16),
        ],
        compiler_params=pltpu.CompilerParams(vmem_limit_bytes=VMEM_LIMIT),
        name="mixer",
    )(own, reader, state, out_gate, resid, head_gain[None], moe_gain[None], select)


def expert_kernel(rows_ref, win_ref, wout_ref, out_ref):
    projected = dot(rows_ref[...], win_ref[...])
    activated = (silu(projected[:, :MOE_H]) * projected[:, MOE_H:]).astype(bf16)
    cols = wout_ref.shape[2]
    for part in range(wout_ref.shape[0]):
        out_ref[:, part * cols : (part + 1) * cols] = dot(activated, wout_ref[part]).astype(bf16)


def expert_mlp(rows, whole_in, whole_out):
    count, width = rows.shape
    block = min(count, 256)
    return pl.pallas_call(
        expert_kernel,
        grid=(count // block,),
        in_specs=[
            pl.BlockSpec((block, width), lambda i: (i, 0)),
            pl.BlockSpec(whole_in.shape, lambda i: (0, 0)),
            pl.BlockSpec(whole_out.shape, lambda i: (0, 0, 0)),
        ],
        out_specs=pl.BlockSpec((block, width), lambda i: (i, 0)),
        out_shape=jax.ShapeDtypeStruct((count, width), bf16),
        compiler_params=pltpu.CompilerParams(
            dimension_semantics=("arbitrary",), vmem_limit_bytes=VMEM_LIMIT
        ),
        name="expert_mlp",
    )(rows, whole_in, whole_out)


def combine_kernel(gather_ref, rows_ref, middle_ref, out_ref):
    high, low = halves(gather_ref[...].T)
    out_ref[...] = (
        middle_ref[...] + (dot(high, rows_ref[...]) + dot(low, rows_ref[...]))
    ).astype(bf16)


def combine(gather, rows, middle):
    return pl.pallas_call(
        combine_kernel,
        out_shape=jax.ShapeDtypeStruct(middle.shape, bf16),
        compiler_params=pltpu.CompilerParams(vmem_limit_bytes=VMEM_LIMIT),
        name="combine",
    )(gather, rows, middle)


def shards(
    resid,
    mixed_qkv,
    out_gate,
    beta,
    log_decay,
    conv_weight,
    head_gain,
    moe_gain,
    routes,
    route_gates,
    w_in,
    w_out,
):
    every = ("ctx", "ep")
    count = lax.axis_size("ctx") * lax.axis_size("ep")
    experts = lax.axis_size("ep")
    splits = count // VALUE_HEAD_SET
    part = DV // splits
    part_rows = round_up(part, 16)
    capacity = round_up(
        max(2, (5 * TOK_DEV * TOPK + 4 * experts - 1) // (4 * experts)), 16
    )
    rows = mixed_qkv.shape[0]

    halo = lax.ppermute(
        mixed_qkv[rows - HALO :], every, [(source, source + 1) for source in range(count - 1)]
    )
    whole_in = lax.all_gather(w_in[0], "ctx", axis=0, tiled=True)
    whole_out = lax.all_gather(w_out[0], "ctx", axis=0)
    fades = lax.all_gather(jnp.exp(jnp.sum(log_decay, axis=1)), every)
    my_head = lax.axis_index(every) // splits
    fade = lax.dynamic_index_in_dim(fades, my_head, axis=1, keepdims=False)

    send, own, reader = local_terms(
        mixed_qkv, halo, conv_weight, beta, log_decay, splits, part_rows
    )
    sums = lax.all_to_all(
        send.reshape(count, DK + part_rows, DK), every, split_axis=0, concat_axis=0, tiled=True
    )
    starts = scan_states(fade, sums)
    states = lax.all_to_all(starts, every, split_axis=0, concat_axis=0, tiled=True)
    states = states[:, :part].reshape(VALUE_HEAD_SET, DV, DK)

    select, gather = route_tables(routes, route_gates, experts, capacity)
    mixer_out, middle, send_rows = mixer(
        own, reader, states, out_gate, resid, head_gain, moe_gain, select
    )
    expert_in = lax.all_to_all(send_rows, "ep", split_axis=0, concat_axis=0, tiled=True)
    expert_out = expert_mlp(expert_in, whole_in, whole_out)
    returned = lax.all_to_all(expert_out, "ep", split_axis=0, concat_axis=0, tiled=True)
    return mixer_out, combine(gather, returned, middle)


def solution(mesh):
    split_rows, split_cols = P(("ctx", "ep"), None), P(None, ("ctx", "ep"))
    return jax.shard_map(
        shards,
        mesh=mesh,
        in_specs=(
            split_rows,
            split_rows,
            split_rows,
            split_cols,
            split_cols,
            P(),
            P(),
            P(),
            split_rows,
            split_rows,
            P("ep", "ctx", None),
            P("ep", None, "ctx"),
        ),
        out_specs=(split_rows, split_rows),
        check_vma=False,
    )
```

time: 827 us -> 255 us (0.31); the launches traced: 816 us -> 254 us
  waiting for transfers between devices: 384 us -> 66 us
  other arithmetic: 171 us -> 0.11 us
  matrix products: 154 us -> 0 us
  blocking collectives: 0 us -> 109 us
  local copies, waits for them, and re-layouts: 75.2 us -> 9.97 us
  Pallas kernels: 0 us -> 35.4 us
    all_gather x6 -> x2, waiting for transfers between devices: 287 us -> 0.04 us  [the longest x1 0.02 us: shards(): whole_out = lax.all_gather(w_out[0], 'ctx', axis=0)]
    another operation x4 -> x0, other arithmetic: 160 us -> none  [the longest x1 159 us: local_terms(): lax.linalg.triangular_solve(identity_t[None] + mixing, identity_t[None] *...]
    dot_general x49 -> x0, matrix products: 150 us -> none  [the longest x20 71.8 us: compose(): jnp.einsum('hvj,hjk->hvk', first_add, second_map, precision=precise)]
    unnamed x0 -> x1, blocking collectives: none -> 56.7 us
    all_to_all x0 -> x1, blocking collectives: none -> 51.9 us  [shards(): lax.all_to_all(expert_out, 'ep', split_axis=0, concat_axis=0, tiled=True)]
    pallas_call x0 -> x6, Pallas kernels: none -> 35.4 us  [the longest x1 16.7 us: local_terms(): pl.pallas_call(functools.partial(local_kernel, splits, part, part_rows),...]
    all_to_all x1 -> x2, waiting for transfers between devices: 47.5 us -> 14.7 us  [the longest x1 14.7 us: shards(): lax.all_to_all(starts, every, split_axis=0, concat_axis=0, tiled=True)]
    dynamic_slice x20 -> x1, local copies, waits for them, and re-layouts: 16.4 us -> 0.18 us  [shards(): fade = lax.dynamic_index_in_dim(fades, my_head, axis=1, keepdims=False)]
  transfers between devices with their start and end apart: 9 -> 6, of which waited for: 6 -> 3; matrix products, arithmetic and copies ran while one was open for 9% -> 1% of each run, Pallas kernels for 0% -> 11%
where the time goes in v1:
time: 255 us; the launch traced here: 254 us
  blocking collectives  109 us (43%)
  waiting for transfers between devices  66 us (26%)
  Pallas kernels  35.4 us (14%)
  starting transfers between devices  19.6 us (8%)
  between operations  14.2 us (6%)
  local copies, waits for them, and re-layouts  9.97 us (4%)
    unnamed x1, blocking collectives  56.7 us
    all_to_all x1, blocking collectives, shards(): lax.all_to_all(expert_out, 'ep', split_axis=0, concat_axis=0, tiled=True)  51.9 us
    all_to_all x1, waiting for transfers between devices, shards(): lax.all_to_all(send_rows, 'ep', split_axis=0, concat_axis=0, tiled=True)  47.9 us
    pallas_call x1, Pallas kernels, local_terms(): pl.pallas_call(functools.partial(local_kernel, splits, part, part_rows),...  16.7 us
    all_to_all x1, waiting for transfers between devices, shards(): lax.all_to_all(starts, every, split_axis=0, concat_axis=0, tiled=True)  14.7 us
    unnamed x32, local copies, waits for them, and re-layouts  8.86 us
    all_to_all x1, starting transfers between devices, shards(): lax.all_to_all(send.reshape(count, DK + part_rows, DK), every, split_axis...  6.76 us
    pallas_call x1, Pallas kernels, expert_mlp(): pl.pallas_call(expert_kernel, grid=(count // block,), in_specs=[pl.BlockS...  6.63 us
  transfers between devices with their start and end apart: 6, of which 3 were waited for; matrix products, arithmetic and copies ran while one was open for 1% of the time, Pallas kernels for 11%

profile of v1, /device:TPU:0, one launch (start us, length us, event | category | flops | bytes accessed | tf_op | source)
XLA Modules:
  0.0 253.9 jit_solution(3749588641500281966)
XLA Ops:
  7.9 0.8 slice.3
  8.7 4.8 %collective-permute-start = (bf16[8,4096]{1,0:T(8,128)(2,1)S(1)}, bf16[8,4096]{1,0:T(8,128)(2,1)S(1)}, u32[]{:S(2)}, u32[]{:S(2)}) collective-permute-start(bf16[8,4096]{1,0:T(8,128)(2,1)S(1)} %slice.3), channel_id=1, source_target_pairs={{0,1},{1,2},{2,3},{3,4},{4,5},{5,6},{6,7},{7,8},{8,9},{9,10},{10,1... | collective-permute-start | bytes 196616 | tf_op jit(solution)/shard_map/ppermute | solution.py:428
  13.6 1.9 collective-permute-done.qh_ref.kh_ref.vh_ref
  15.5 1.2 copy-done
  16.7 0.8 copy-done.5
  18.2 0.7 copy-done.12
  18.9 16.7 %local_terms.1 = (bf16[16,2,192,128]{3,2,1,0:T(8,128)(2,1)}, f32[16,128,128]{2,1,0:T(8,128)S(1)}, f32[16,128,128]{2,1,0:T(8,128)S(1)}) custom-call(bf16[128,4096]{1,0:T(8,128)(2,1)S(1)} %copy-done, bf16[128,4096]{1,0:T(8,128)(2,1)S(1)} %copy-done, bf16[128,4096]{1,0:T(8,128)(2,1)S(1)} %copy-done, ...), custom_call_target="tpu_custom_call" | custom-call | tf_op jit(solution)/shard_map/local_terms/pallas_call | solution.py:204
  35.7 1.0 copy-done.1
  36.7 6.8 %all-to-all-start = ((bf16[32,192,128]{2,1,0:T(8,128)(2,1)}), bf16[32,192,128]{2,1,0:T(8,128)(2,1)S(1)}, u32[]{:S(2)}, u32[]{:S(2)}) async-start(bf16[32,192,128]{2,1,0:T(8,128)(2,1)} %bitcast.2), calls=%async_computation | async-start | bytes 3145728 | tf_op jit(solution)/shard_map/all_to_all | solution.py:440
  44.6 56.7 %all-reduce.1 = f32[32,16]{1,0:T(8,128)S(1)} all-reduce(f32[32,16]{1,0:T(8,128)S(1)} %reshape.32), channel_id=2, replica_groups=mesh['ctx'=4,'ep'=8] {'ctx','ep'}, use_global_device_ids=true, to_apply=%add | all-reduce | flops 512 | bytes 4096
  101.5 5.6 %scan_states.1 = bf16[32,64,128]{2,1,0:T(8,128)(2,1)} custom-call(f32[32]{0:T(128)S(1)} %dynamic-slice_reduce_fusion.fade_ref, bf16[32,192,128]{2,1,0:T(8,128)(2,1)S(1)} %all-to-all-done.sums_ref), custom_call_target="tpu_custom_call" | custom-call | tf_op jit(solution)/shard_map/scan_states/pallas_call | solution.py:253
  107.1 4.3 %all-to-all-start.1 = ((bf16[32,64,128]{2,1,0:T(8,128)(2,1)}), bf16[32,64,128]{2,1,0:T(8,128)(2,1)S(1)}, u32[]{:S(2)}, u32[]{:S(2)}) async-start(bf16[32,64,128]{2,1,0:T(8,128)(2,1)} %scan_states.1), calls=%async_computation.1 | async-start | bytes 1048576 | tf_op jit(solution)/shard_map/all_to_all | solution.py:444
  111.4 1.6 route_tables.1
  113.1 14.7 %all-to-all-done.1 = bf16[32,64,128]{2,1,0:T(8,128)(2,1)S(1)} async-done(((bf16[32,64,128]{2,1,0:T(8,128)(2,1)}), bf16[32,64,128]{2,1,0:T(8,128)(2,1)S(1)}, u32[]{:S(2)}, u32[]{:S(2)}) %all-to-all-start.1) | async-done | bytes 524320 | tf_op jit(solution)/shard_map/all_to_all | solution.py:444
  127.8 1.2 copy-done.2
  129.0 1.0 copy-done.7
  130.1 0.9 copy-done.9
  131.0 3.3 %mixer.1 = (bf16[128,2048]{1,0:T(8,128)(2,1)}, f32[128,2048]{1,0:T(8,128)S(1)}, bf16[512,2048]{1,0:T(8,128)(2,1)}) custom-call(f32[16,128,128]{2,1,0:T(8,128)S(1)} %get-tuple-element.10.own_ref, f32[16,128,128]{2,1,0:T(8,128)S(1)} %copy-done.2, bf16[16,128,128]{2,1,0:T(8,128)(2,1)S(1)} %bitcast.16, bf16[128,2048]{1,0:T(8,128)(2,1)S(1)} %copy-done.6, ...), custom_call_target="tpu_custom_call" | custom-call | tf_op jit(solution)/shard_map/mixer/pallas_call | solution.py:347
  134.3 1.1 copy-done.3
  135.3 3.6 %all-to-all-start.2 = ((bf16[8,64,2048]{2,1,0:T(8,128)(2,1)}), bf16[8,64,2048]{2,1,0:T(8,128)(2,1)S(1)}, u32[]{:S(2)}, u32[]{:S(2)}) async-start(bf16[8,64,2048]{2,1,0:T(8,128)(2,1)} %bitcast.22), calls=%async_computation.2 | async-start | bytes 4194304 | tf_op jit(solution)/shard_map/all_to_all | solution.py:451
  139.0 47.9 %all-to-all-done.2 = bf16[8,64,2048]{2,1,0:T(8,128)(2,1)S(1)} async-done(((bf16[8,64,2048]{2,1,0:T(8,128)(2,1)}), bf16[8,64,2048]{2,1,0:T(8,128)(2,1)S(1)}, u32[]{:S(2)}, u32[]{:S(2)}) %all-to-all-start.2) | async-done | bytes 2097184 | tf_op jit(solution)/shard_map/all_to_all | solution.py:451
  186.9 6.6 %expert_mlp.1 = bf16[512,2048]{1,0:T(8,128)(2,1)S(1)} custom-call(bf16[512,2048]{1,0:T(8,128)(2,1)S(1)} %bitcast.13, bf16[2048,1024]{1,0:T(8,128)(2,1)} %bitcast.21, bf16[4,512,512]{2,1,0:T(8,128)(2,1)} %all-gather.5.cloned.1.call-done.wout_ref), custom_call_target="tpu_custom_call" | custom-call | tf_op jit(solution)/shard_map/expert_mlp/pallas_call | solution.py:370
  193.6 51.9 %all_to_all.32 = bf16[8,64,2048]{2,1,0:T(8,128)(2,1)S(1)} all-to-all(bf16[8,64,2048]{2,1,0:T(8,128)(2,1)S(1)} %bitcast.14), channel_id=1, replica_groups=mesh['ctx'=4,'ep'=8] {'ep'}, dimensions={0} | all-to-all | bytes 4194304 | tf_op jit(solution)/shard_map/all_to_all | solution.py:453
  245.5 1.6 combine.1
  (34 shorter events, 2.7 us)
Async XLA Ops:
  7.2 131.8 %all-gather.5.cloned.1.call-start = ((), (), s32[]{:S(2)}) async-start(), calls=%async_computation.4 | async-start | bytes 2621440 | tf_op jit(solution)/shard_map/all_gather | solution.py:432
  8.7 6.7 %collective-permute-start = (bf16[8,4096]{1,0:T(8,128)(2,1)S(1)}, bf16[8,4096]{1,0:T(8,128)(2,1)S(1)}, u32[]{:S(2)}, u32[]{:S(2)}) collective-permute-start(bf16[8,4096]{1,0:T(8,128)(2,1)S(1)} %slice.3), channel_id=1, source_target_pairs={{0,1},{1,2},{2,3},{3,4},{4,5},{5,6},{6,7},{7,8},{8,9},{9,10},{10,1... | collective-permute-start | bytes 196616 | tf_op jit(solution)/shard_map/ppermute | solution.py:428
  15.5 1.2 copy-start
  16.7 0.8 copy-start.5
  17.5 0.7 copy-start.10
  18.2 0.7 copy-start.12
  35.7 1.0 copy-start.1
  36.7 7.6 %copy-start.11 = (f32[16,128]{1,0:T(8,128)S(1)}, f32[16,128]{1,0:T(8,128)}, u32[]{:S(2)}) copy-start(f32[16,128]{1,0:T(8,128)} %param.16) | copy-start | bytes 24580
  36.7 64.8 %all-to-all-start = ((bf16[32,192,128]{2,1,0:T(8,128)(2,1)}), bf16[32,192,128]{2,1,0:T(8,128)(2,1)S(1)}, u32[]{:S(2)}, u32[]{:S(2)}) async-start(bf16[32,192,128]{2,1,0:T(8,128)(2,1)} %bitcast.2), calls=%async_computation | async-start | bytes 3145728 | tf_op jit(solution)/shard_map/all_to_all | solution.py:440
  43.5 84.3 %copy-start.6 = (bf16[128,2048]{1,0:T(8,128)(2,1)S(1)}, bf16[128,2048]{1,0:T(8,128)(2,1)}, u32[]{:S(2)}) copy-start(bf16[128,2048]{1,0:T(8,128)(2,1)} %gate_ref.1) | copy-start | bytes 1572868
  43.5 84.3 %copy-start.13 = (f32[2048]{0:T(1024)S(1)}, f32[2048]{0:T(1024)}, u32[]{:S(2)}) copy-start(f32[2048]{0:T(1024)} %param.19) | copy-start | bytes 24580
  43.5 84.3 %copy-start.14 = (f32[128]{0:T(128)S(1)}, f32[128]{0:T(128)}, u32[]{:S(2)}) copy-start(f32[128]{0:T(128)} %param.18) | copy-start | bytes 1540
  43.5 95.5 %all-gather.7.cloned.1.call-start = ((), (), s32[]{:S(2)}) async-start(), calls=%async_computation.5 | async-start | bytes 5242880 | tf_op jit(solution)/shard_map/all_gather | solution.py:431
  107.1 20.7 %all-to-all-start.1 = ((bf16[32,64,128]{2,1,0:T(8,128)(2,1)}), bf16[32,64,128]{2,1,0:T(8,128)(2,1)S(1)}, u32[]{:S(2)}, u32[]{:S(2)}) async-start(bf16[32,64,128]{2,1,0:T(8,128)(2,1)} %scan_states.1), calls=%async_computation.1 | async-start | bytes 1048576 | tf_op jit(solution)/shard_map/all_to_all | solution.py:444
  127.8 1.2 copy-start.2
  129.0 1.0 copy-start.7
  130.1 0.9 copy-start.9
  134.3 1.1 copy-start.3
  135.3 51.6 %all-to-all-start.2 = ((bf16[8,64,2048]{2,1,0:T(8,128)(2,1)}), bf16[8,64,2048]{2,1,0:T(8,128)(2,1)S(1)}, u32[]{:S(2)}, u32[]{:S(2)}) async-start(bf16[8,64,2048]{2,1,0:T(8,128)(2,1)} %bitcast.22), calls=%async_computation.2 | async-start | bytes 4194304 | tf_op jit(solution)/shard_map/all_to_all | solution.py:451
  193.5 51.9 %copy-start.4 = (f32[128,2048]{1,0:T(8,128)S(1)}, f32[128,2048]{1,0:T(8,128)}, u32[]{:S(2)}) copy-start(f32[128,2048]{1,0:T(8,128)} %copy-done.3) | copy-start | bytes 3145732
  193.6 51.9 %copy-start.8 = (f32[512,128]{1,0:T(8,128)S(1)}, f32[512,128]{1,0:T(8,128)}, u32[]{:S(2)}) copy-start(f32[512,128]{1,0:T(8,128)} %get-tuple-element.15.gather_ref) | copy-start | bytes 786436
Sparse Core Ops, SparseCore 0:
  9.6 25.2 all-gather.4
  45.9 43.2 all-gather.6

commit v2 on v1

v2 whole, which is shorter than its diff:
```python
import functools

import jax
import jax.numpy as jnp
from jax import lax
from jax.experimental import pallas as pl
from jax.experimental.pallas import tpu as pltpu
from jax.sharding import Mesh
from jax.sharding import PartitionSpec as P

HK = 8
VALUE_HEAD_SET = 16
DK = 128
DV = 128
MOE_H = 512
CONV = 4
TOPK = 3
TOK_DEV = 128
GROUP = VALUE_HEAD_SET // HK
HALO = 8
STEP_KEYS = 2
FADE_ROWS = 16

f32 = jnp.float32
bf16 = jnp.bfloat16


def round_up(value, multiple):
    return (value + multiple - 1) // multiple * multiple


def hbm(*arrays):
    return [pltpu.with_memory_space_constraint(array, pltpu.HBM) for array in arrays]


def dot(lhs, rhs):
    return jnp.dot(lhs, rhs, preferred_element_type=f32)


def dot_nt(lhs, rhs):
    return lax.dot_general(lhs, rhs, (((1,), (1,)), ((), ())), preferred_element_type=f32)


def halves(value):
    high = value.astype(bf16)
    return high, (value - high.astype(f32)).astype(bf16)


def one_pass(lhs, rhs):
    return dot(lhs.astype(bf16), rhs.astype(bf16))


def three_pass(lhs, rhs):
    (lhs_high, lhs_low), (rhs_high, rhs_low) = halves(lhs), halves(rhs)
    return dot(lhs_high, rhs_high) + (dot(lhs_high, rhs_low) + dot(lhs_low, rhs_high))


def three_pass_nt(lhs, rhs):
    (lhs_high, lhs_low), (rhs_high, rhs_low) = lhs, rhs
    return dot_nt(lhs_high, rhs_high) + (dot_nt(lhs_high, rhs_low) + dot_nt(lhs_low, rhs_high))


def silu(value):
    return value * jax.nn.sigmoid(value)


def conv_silu(ref, halo_ref, weight_ref):
    rows = ref.shape[0]
    padded = jnp.concatenate([halo_ref[...].astype(f32), ref[...].astype(f32)], axis=0)
    total = padded[HALO:] * weight_ref[CONV - 1 : CONV, :]
    for tap in range(CONV - 1):
        start = HALO - (CONV - 1) + tap
        total = total + padded[start : start + rows] * weight_ref[tap : tap + 1, :]
    return silu(total)


def fade_tile(fade):
    left = jnp.broadcast_to(fade, (FADE_ROWS, DK))
    row_ids = lax.broadcasted_iota(jnp.int32, (FADE_ROWS, DK), 0)
    tile = jnp.zeros((FADE_ROWS, DK), f32)
    for term in range(3):
        part = left.astype(bf16).astype(f32)
        tile = jnp.where(row_ids == term, part, tile)
        left = left - part
    return tile.astype(bf16)


def key_rows_hat(key_rows):
    return key_rows * lax.rsqrt(jnp.sum(key_rows * key_rows, axis=1, keepdims=True) + 1e-06)


def decay_terms(decay_row, masks):
    diagonal, causal, upper = masks
    decay_col = jnp.sum(jnp.where(diagonal, decay_row, 0.0), axis=1, keepdims=True)
    cum_col = jnp.sum(jnp.where(causal, decay_row, 0.0), axis=1, keepdims=True)
    cum_row = jnp.sum(jnp.where(upper, decay_col, 0.0), axis=0, keepdims=True)
    fading = jnp.where(causal, jnp.exp(jnp.where(causal, cum_col - cum_row, 0.0)), 0.0)
    return cum_col, fading


def square_ids(rows):
    return (
        lax.broadcasted_iota(jnp.int32, (rows, rows), 0),
        lax.broadcasted_iota(jnp.int32, (rows, rows), 1),
    )


def local_kernel(
    splits,
    part,
    part_rows,
    k_ref,
    v_ref,
    kh_ref,
    vh_ref,
    kw_ref,
    vw_ref,
    beta_ref,
    decay_ref,
    send_ref,
    hat_ref,
    fresh_ref,
):
    rows = k_ref.shape[0]
    keys, values = conv_silu(k_ref, kh_ref, kw_ref), conv_silu(v_ref, vh_ref, vw_ref)
    row_ids, col_ids = square_ids(rows)
    strict, causal, diagonal = row_ids > col_ids, row_ids >= col_ids, row_ids == col_ids
    masks = diagonal, causal, row_ids <= col_ids
    identity = jnp.where(diagonal, 1.0, 0.0).astype(f32)

    key_hats, grams = [], []
    for key in range(STEP_KEYS):
        key_hat = key_rows_hat(keys[:, key * DK : (key + 1) * DK])
        hat_ref[key] = key_hat
        key_hats.append(key_hat)
        parts = halves(key_hat)
        grams.append(three_pass_nt(parts, parts))

    heads = range(STEP_KEYS * GROUP)
    lower, betas, fades, tails, wholes = [], [], [], [], []
    for head in heads:
        key, member = head // GROUP, head % GROUP
        beta_row = beta_ref[key, member : member + 1, :]
        decay_row = decay_ref[key, member : member + 1, :]
        beta_col = jnp.sum(jnp.where(diagonal, beta_row, 0.0), axis=1, keepdims=True)
        cum_col, fading = decay_terms(decay_row, masks)
        last = jnp.sum(decay_row, axis=1, keepdims=True)
        lower.append(jnp.where(strict, beta_col * fading * grams[key], 0.0))
        betas.append(beta_col)
        fades.append(jnp.exp(cum_col))
        tails.append(jnp.exp(jnp.minimum(last - cum_col, 0.0)))
        wholes.append(jnp.exp(last))

    solved = [
        jnp.where(row_ids // 2 == col_ids // 2, identity - lower[head], 0.0) for head in heads
    ]
    size = 2
    while size < rows:
        joins = (row_ids // (2 * size) == col_ids // (2 * size)) & (
            row_ids // size != col_ids // size
        )
        parts = [solved[head].astype(bf16) for head in heads]
        inner = [
            dot(parts[head], jnp.where(joins, lower[head], 0.0).astype(bf16)) for head in heads
        ]
        solved = [solved[head] - dot(inner[head].astype(bf16), parts[head]) for head in heads]
        size *= 2
    residues = [
        (identity - solved[head]) - three_pass(lower[head], solved[head]) for head in heads
    ]
    solved = [solved[head] + one_pass(solved[head], residues[head]) for head in heads]

    for head in heads:
        key = head // GROUP
        value_span = slice(head * DV, (head + 1) * DV)
        fresh_carried = three_pass(
            solved[head],
            jnp.concatenate(
                [
                    betas[head] * values[:, value_span],
                    (betas[head] * fades[head]) * key_hats[key],
                ],
                axis=1,
            ),
        )
        fresh_ref[head] = fresh_carried
        sums = three_pass(fresh_carried.T, tails[head] * key_hats[key])
        transition, state_add = sums[DV:].astype(bf16), sums[:DV].astype(bf16)
        fade_rows = fade_tile(wholes[head])
        for split in range(splits):
            send_ref[head, split, :DK, :] = transition
            for core in range(2):
                place = 2 * split + core
                added = state_add[place * part : (place + 1) * part]
                if part < part_rows:
                    added = jnp.concatenate(
                        [added, jnp.zeros((part_rows - part, DK), bf16)], axis=0
                    )
                send_ref[head, split, pl.ds(DK + core * part_rows, part_rows), :] = added
            send_ref[head, split, pl.ds(DK + 2 * part_rows, FADE_ROWS), :] = fade_rows


def local_terms(mixed_qkv, halo, conv_weight, beta, log_decay, splits, part, part_rows):
    rows = mixed_qkv.shape[0]
    key_cols, value_cols = STEP_KEYS * DK, STEP_KEYS * GROUP * DV
    steps = HK // STEP_KEYS
    value_from = 2 * HK * DK // value_cols
    height = DK + 2 * part_rows + FADE_ROWS
    col_maps = (
        (key_cols, lambda i: (0, steps + i)),
        (value_cols, lambda i: (0, value_from + i)),
    )
    specs = [
        pl.BlockSpec((tall, width), index)
        for tall in (rows, HALO, CONV)
        for width, index in col_maps
    ]
    per_key = pl.BlockSpec((STEP_KEYS, GROUP, rows), lambda i: (i, 0, 0))
    step_heads = STEP_KEYS * GROUP
    return pl.pallas_call(
        functools.partial(local_kernel, splits, part, part_rows),
        grid=(steps,),
        in_specs=specs + [per_key, per_key],
        out_specs=[
            pl.BlockSpec((step_heads, splits, height, DK), lambda i: (i, 0, 0, 0)),
            pl.BlockSpec((STEP_KEYS, rows, DK), lambda i: (i, 0, 0)),
            pl.BlockSpec((step_heads, rows, DV + DK), lambda i: (i, 0, 0)),
        ],
        out_shape=[
            pltpu.HBM((VALUE_HEAD_SET, splits, height, DK), bf16),
            pltpu.HBM((HK, rows, DK), f32),
            pltpu.HBM((VALUE_HEAD_SET, rows, DV + DK), f32),
        ],
        compiler_params=pltpu.CompilerParams(
            dimension_semantics=("arbitrary",), vmem_limit_bytes=24 << 20
        ),
        name="local_terms",
    )(
        *hbm(mixed_qkv, mixed_qkv),
        halo,
        halo,
        *hbm(conv_weight, conv_weight, beta, log_decay),
    )


def reader_kernel(
    q_ref, qh_ref, qw_ref, hat_ref, decay_ref, fresh_ref, own_ref, reader_ref
):
    rows = q_ref.shape[0]
    queries = conv_silu(q_ref, qh_ref, qw_ref)
    row_ids, col_ids = square_ids(rows)
    masks = row_ids == col_ids, row_ids >= col_ids, row_ids <= col_ids
    for key in range(STEP_KEYS):
        query = key_rows_hat(queries[:, key * DK : (key + 1) * DK]) * DK ** (-0.5)
        raw = three_pass_nt(halves(query), halves(hat_ref[key]))
        for member in range(GROUP):
            head = key * GROUP + member
            cum_col, fading = decay_terms(decay_ref[key, member : member + 1, :], masks)
            mixed = three_pass(fading * raw, fresh_ref[head])
            own_ref[head] = mixed[:, :DV]
            reader_ref[head] = jnp.exp(cum_col) * query - mixed[:, DV:]


def reader_terms(mixed_qkv, halo, conv_weight, log_decay, hats, fresh):
    rows = mixed_qkv.shape[0]
    key_cols, step_heads = STEP_KEYS * DK, STEP_KEYS * GROUP
    per_head = pl.BlockSpec((step_heads, rows, DK), lambda i: (i, 0, 0))
    return pl.pallas_call(
        reader_kernel,
        grid=(HK // STEP_KEYS,),
        in_specs=[pl.BlockSpec((tall, key_cols), lambda i: (0, i)) for tall in (rows, HALO, CONV)]
        + [
            pl.BlockSpec((STEP_KEYS, rows, DK), lambda i: (i, 0, 0)),
            pl.BlockSpec((STEP_KEYS, GROUP, rows), lambda i: (i, 0, 0)),
            pl.BlockSpec((step_heads, rows, DV + DK), lambda i: (i, 0, 0)),
        ],
        out_specs=[per_head, per_head],
        out_shape=[pltpu.HBM((VALUE_HEAD_SET, rows, DK), f32)] * 2,
        compiler_params=pltpu.CompilerParams(
            dimension_semantics=("arbitrary",), vmem_limit_bytes=24 << 20
        ),
        name="reader_terms",
    )(*hbm(mixed_qkv), halo, *hbm(conv_weight, hats, log_decay, fresh))


def scan_kernel(core_ref, near_ref, far_ref, start_ref, state_ref):
    step, core = pl.program_id(0), core_ref[0]
    block, part_rows = start_ref.shape[:2]

    @pl.when(step == 0)
    def _():
        state_ref[...] = jnp.zeros_like(state_ref)

    is_near = step % 2 == core
    added_at = pl.multiple_of(DK + core * part_rows, 16)
    state = state_ref[...]
    for place in range(block):

        def pick(span):
            return jnp.where(is_near, near_ref[place, span, :], far_ref[place, span, :])

        high, low = halves(state)
        start_ref[place] = high
        transition = pick(slice(0, DK))
        moved = dot(high, transition) + dot(low, transition)
        added = pick(pl.ds(added_at, part_rows)).astype(f32)
        terms = pick(slice(DK + 2 * part_rows, DK + 2 * part_rows + FADE_ROWS)).astype(f32)
        fade = terms[0:1] + (terms[1:2] + terms[2:3])
        state = (fade * state - moved) + added
    state_ref[...] = state


def scan_states(core, near, far, block, part_rows):
    chips, height = near.shape[:2]
    both = pl.BlockSpec((block, height, DK), lambda i, core: (i // 2, 0, 0))
    return pl.pallas_call(
        scan_kernel,
        grid_spec=pltpu.PrefetchScalarGridSpec(
            num_scalar_prefetch=1,
            grid=(2 * chips // block,),
            in_specs=[both, both],
            out_specs=pl.BlockSpec((block, part_rows, DK), lambda i, core: (i, 0, 0)),
            scratch_shapes=[pltpu.VMEM((part_rows, DK), f32)],
        ),
        out_shape=pltpu.HBM((2 * chips, part_rows, DK), bf16),
        compiler_params=pltpu.CompilerParams(
            dimension_semantics=("arbitrary",), vmem_limit_bytes=16 << 20
        ),
        name="scan_states",
    )(core, near, far)


def route_kernel(capacity, routes_ref, gates_ref, select_ref, gather_ref):
    rows = routes_ref.shape[1]
    experts = select_ref.shape[0] // capacity
    expert_ids = lax.broadcasted_iota(jnp.int32, (experts, rows), 0)
    chosen = jnp.zeros((experts, rows), jnp.bool_)
    gates = jnp.zeros((experts, rows), f32)
    for choice in range(TOPK):
        named = routes_ref[choice : choice + 1, :] == expert_ids
        chosen = chosen | named
        gates = gates + jnp.where(named, gates_ref[choice : choice + 1, :], 0.0)
    earlier = lax.broadcasted_iota(jnp.int32, (rows, rows), 0) < lax.broadcasted_iota(
        jnp.int32, (rows, rows), 1
    )
    rank = dot(
        jnp.where(chosen, 1.0, 0.0).astype(bf16), jnp.where(earlier, 1.0, 0.0).astype(bf16)
    )
    slot = jnp.where(chosen, rank, -1.0).astype(jnp.int32)
    slot_ids = lax.broadcasted_iota(jnp.int32, (capacity, rows), 0)
    for expert in range(experts):
        span = slice(expert * capacity, (expert + 1) * capacity)
        taken = slot_ids == slot[expert : expert + 1, :]
        select_ref[span, :] = jnp.where(taken, 1.0, 0.0).astype(bf16)
        gather_ref[span, :] = jnp.where(taken, gates[expert : expert + 1, :], 0.0)


def route_tables(routes, route_gates, experts, capacity):
    rows = routes.shape[0]
    slots = experts * capacity
    return pl.pallas_call(
        functools.partial(route_kernel, capacity),
        out_shape=[
            jax.ShapeDtypeStruct((slots, rows), bf16),
            jax.ShapeDtypeStruct((slots, rows), f32),
        ],
        name="route_tables",
    )(routes.T, route_gates.T)


def mixer_kernel(
    own_ref,
    reader_ref,
    state_ref,
    gate_ref,
    resid_ref,
    head_gain_ref,
    moe_gain_ref,
    select_ref,
    mixer_ref,
    middle_ref,
    rows_ref,
    squares_ref,
):
    step, heads = pl.program_id(0), own_ref.shape[0]
    squares = jnp.where(step == 0, jnp.zeros_like(squares_ref), squares_ref[...])
    for head in range(heads):
        span = slice(head * DV, (head + 1) * DV)
        if len(state_ref.shape) == 3:
            state = state_ref[head]
        else:
            state = jnp.concatenate([state_ref[0, core, head] for core in range(2)], axis=0)
        high, low = halves(reader_ref[head])
        head_out = own_ref[head] + (dot_nt(high, state) + dot_nt(low, state))
        scaled = (
            head_out
            * lax.rsqrt(jnp.mean(head_out * head_out, axis=1, keepdims=True) + 1e-06)
            * head_gain_ref[...]
        )
        mixed = (scaled * silu(gate_ref[:, span].astype(f32))).astype(bf16)
        mixer_ref[:, span] = mixed
        middle = resid_ref[:, span].astype(f32) + mixed.astype(f32)
        middle_ref[step * heads + head] = middle
        squares = squares + jnp.sum(middle * middle, axis=1, keepdims=True)
    squares_ref[...] = squares

    @pl.when(step == pl.num_programs(0) - 1)
    def _():
        scale = lax.rsqrt(squares / moe_gain_ref.shape[1] + 1e-06)
        select = select_ref[...]
        for head in range(VALUE_HEAD_SET):
            span = slice(head * DV, (head + 1) * DV)
            moe_input = (middle_ref[head] * scale * moe_gain_ref[:, span]).astype(bf16)
            rows_ref[:, span] = dot(select, moe_input).astype(bf16)


def mixer(own, reader, state, out_gate, resid, head_gain, moe_gain, select):
    rows, width = resid.shape
    heads = 4
    per_head = pl.BlockSpec((heads, rows, DV), lambda i: (i, 0, 0))
    columns = pl.BlockSpec((rows, heads * DV), lambda i: (0, i))
    if state.ndim == 3:
        state_spec = pl.BlockSpec((heads, DV, DK), lambda i: (i, 0, 0))
    else:
        block = state.shape[2] // heads
        state_spec = pl.BlockSpec(
            (1, 2, heads) + state.shape[3:], lambda i: (i // block, 0, i % block, 0, 0)
        )

    def whole(*shape):
        return pl.BlockSpec(shape, lambda i: (0,) * len(shape))

    return pl.pallas_call(
        mixer_kernel,
        grid=(VALUE_HEAD_SET // heads,),
        in_specs=[
            per_head,
            per_head,
            state_spec,
            columns,
            columns,
            whole(1, DV),
            whole(1, width),
            whole(*select.shape),
        ],
        out_specs=[
            columns,
            whole(VALUE_HEAD_SET, rows, DV),
            whole(select.shape[0], width),
        ],
        out_shape=[
            pltpu.HBM((rows, width), bf16),
            jax.ShapeDtypeStruct((VALUE_HEAD_SET, rows, DV), f32),
            pltpu.HBM((select.shape[0], width), bf16),
        ],
        scratch_shapes=[pltpu.VMEM((rows, 1), f32)],
        compiler_params=pltpu.CompilerParams(
            dimension_semantics=("arbitrary",), vmem_limit_bytes=24 << 20
        ),
        name="mixer",
    )(
        *hbm(own, reader),
        state,
        *hbm(out_gate, resid),
        head_gain[None],
        moe_gain[None],
        *hbm(select),
    )


def expert_in_kernel(order_ref, rows_ref, *refs):
    in_refs, result_ref = refs[:-1], refs[-1]
    projected = None
    for place, ref in enumerate(in_refs):
        depth = ref.shape[0]
        start = pl.multiple_of(order_ref[place] * depth, depth)
        term = dot(rows_ref[:, pl.ds(start, depth)], ref[...])
        projected = term if projected is None else projected + term
    result_ref[...] = (silu(projected[:, :MOE_H]) * projected[:, MOE_H:]).astype(bf16)


def expert_out_kernel(order_ref, activated_ref, *refs):
    out_refs, result_ref = refs[:-1], refs[-1]
    activated = activated_ref[...]
    for place, ref in enumerate(out_refs):
        cols = ref.shape[1]
        start = pl.multiple_of(order_ref[place] * cols, cols)
        result_ref[:, pl.ds(start, cols)] = dot(activated, ref[...]).astype(bf16)


def expert_call(kernel, name, order, rows, parts, width):
    count = rows.shape[0]
    block = min(count, 256)
    return pl.pallas_call(
        kernel,
        grid_spec=pltpu.PrefetchScalarGridSpec(
            num_scalar_prefetch=1,
            grid=(count // block,),
            in_specs=[pl.BlockSpec((block, rows.shape[1]), lambda i, order: (i, 0))]
            + [pl.BlockSpec(part.shape, lambda i, order: (0, 0)) for part in parts],
            out_specs=pl.BlockSpec((block, width), lambda i, order: (i, 0)),
        ),
        out_shape=jax.ShapeDtypeStruct((count, width), bf16),
        compiler_params=pltpu.CompilerParams(
            dimension_semantics=("arbitrary",), vmem_limit_bytes=24 << 20
        ),
        name=name,
    )(order, rows, *hbm(*parts))


def expert_in(order, rows, parts):
    rows = rows.reshape(-1, rows.shape[-1])
    return expert_call(expert_in_kernel, "expert_in", order, rows, parts, MOE_H)


def expert_out(order, activated, parts, width):
    return expert_call(expert_out_kernel, "expert_out", order, activated, parts, width)


def combine_kernel(gather_ref, rows_ref, middle_ref, out_ref):
    high, low = halves(gather_ref[...].T)
    for head in range(middle_ref.shape[0]):
        span = slice(head * DV, (head + 1) * DV)
        rows = rows_ref[:, span]
        out_ref[:, span] = (middle_ref[head] + (dot(high, rows) + dot(low, rows))).astype(bf16)


def combine(gather, rows, middle):
    count, width = middle.shape[1], rows.shape[1]
    return pl.pallas_call(
        combine_kernel,
        out_shape=pltpu.HBM((count, width), bf16),
        compiler_params=pltpu.CompilerParams(vmem_limit_bytes=24 << 20),
        name="combine",
    )(gather, rows, middle)


def after(value, earlier):
    return lax.optimization_barrier((value, earlier))[0]


def across_halves(value, flip):
    pairs = [
        (core * 2 + half, half * 2 + (core ^ flip)) for core in range(2) for half in range(2)
    ]
    return lax.ppermute(value, ("core", "half"), pairs)


def along_y(value, y_count):
    moved = [value]
    for shift in range(1, y_count):
        pairs = [(source, (source + shift) % y_count) for source in range(y_count)]
        moved.append(lax.ppermute(value, "y", pairs))
    return moved


def shards(
    resid,
    mixed_qkv,
    out_gate,
    beta,
    log_decay,
    conv_weight,
    head_gain,
    moe_gain,
    routes,
    route_gates,
    w_in,
    w_out,
):
    every = ("y", "core", "half", "rest")
    y_count, rest_count = lax.axis_size("y"), lax.axis_size("rest")
    count = lax.axis_size(every)
    experts = 2 * rest_count
    chips, block = count // 2, 2 * rest_count
    splits = chips // VALUE_HEAD_SET
    part = DV // (2 * splits)
    part_rows = round_up(part, 16)
    capacity = round_up(
        max(2, (5 * TOK_DEV * TOPK + 4 * experts - 1) // (4 * experts)), 16
    )
    rows = mixed_qkv.shape[0]
    beta, log_decay = (value.reshape(HK, GROUP, rows) for value in (beta, log_decay))
    tie = lax.optimization_barrier

    halo = lax.ppermute(
        mixed_qkv[rows - HALO :], every, [(source, source + 1) for source in range(count - 1)]
    )
    in_first = across_halves(after(w_in[0], halo), 0)
    send, hats, fresh = local_terms(
        mixed_qkv, halo, conv_weight, beta, log_decay, splits, part, part_rows
    )

    near = lax.all_to_all(
        send.reshape(chips, -1, DK),
        ("y", "half", "rest"),
        split_axis=0,
        concat_axis=0,
        tiled=True,
    )
    hats, in_first = tie((hats, in_first))
    own, reader = reader_terms(mixed_qkv, halo, conv_weight, log_decay, hats, fresh)
    select, gather = route_tables(routes, route_gates, experts, capacity)
    in_first = along_y(after(in_first, own), y_count)
    out_first = across_halves(after(w_out[0], send), 0)
    near, in_first, out_first, own, reader, select = tie(
        (near, in_first, out_first, own, reader, select)
    )

    in_second = across_halves(after(w_in[0], near), 1)
    far = lax.ppermute(near, "core", [(0, 1), (1, 0)])
    core = lax.axis_index("core").astype(jnp.int32).reshape(1)
    starts = scan_states(core, near, far, block, part_rows)
    states = lax.all_to_all(starts, every, split_axis=0, concat_axis=0, tiled=True)
    out_first = along_y(out_first, y_count)
    states, in_second, out_first = tie((states, in_second, out_first))

    states = states.reshape(y_count, 2, block, part_rows, DK)
    if part < part_rows or splits > 1:
        states = states[:, :, :, :part].transpose(0, 2, 1, 3, 4)
        states = states.reshape(VALUE_HEAD_SET, DV, DK)
    mixer_out, middle, send_rows = mixer(
        own, reader, states, out_gate, resid, head_gain, moe_gain, select
    )
    in_second = along_y(after(in_second, send_rows), y_count)
    out_second = across_halves(after(w_out[0], send_rows), 1)
    out_second = along_y(out_second, y_count)
    exchange = functools.partial(
        lax.all_to_all, axis_name=("core", "rest"), split_axis=0, concat_axis=0, tiled=True
    )
    y_index, half = lax.axis_index("y"), lax.axis_index("half")
    order = jnp.stack(
        [
            (y_index - shift) % y_count * 2 + (half ^ flip)
            for flip in range(2)
            for shift in range(y_count)
        ]
    )
    activated = expert_in(order, exchange(send_rows), in_first + in_second)
    expert_rows = expert_out(order, activated, out_first + out_second, send_rows.shape[1])
    return mixer_out, combine(gather, exchange(expert_rows), middle)


def solution(mesh):
    ctx_count, ep_count = mesh.shape["ctx"], mesh.shape["ep"]
    names = ("y", "core", "half", "rest")
    fine = Mesh(mesh.devices.reshape(ctx_count // 2, 2, 2, ep_count // 2), names)
    split_rows, split_cols = P(names, None), P(None, names)
    ctx, ep = names[:2], names[2:]
    return jax.shard_map(
        shards,
        mesh=fine,
        in_specs=(
            split_rows,
            split_rows,
            split_rows,
            split_cols,
            split_cols,
            P(),
            P(),
            P(),
            split_rows,
            split_rows,
            P(ep, ctx, None),
            P(ep, None, ctx),
        ),
        out_specs=(split_rows, split_rows),
        check_vma=False,
    )
```

time: 255 us -> 203 us (0.80)
  blocking collectives: 109 us -> 31.5 us
  starting transfers between devices: 19.6 us -> 54.8 us
  between operations: 14.2 us -> 0.72 us
  Pallas kernels: 35.4 us -> 44.4 us
  local copies, waits for them, and re-layouts: 9.97 us -> 1.67 us
    unnamed x1 -> x0, blocking collectives: 56.7 us -> none
    ppermute x0 -> x9, waiting for transfers between devices: none -> 46.4 us  [the longest x4 24.9 us: across_halves(): return lax.ppermute(value, ('core', 'half'), pairs)]
    ppermute x0 -> x9, starting transfers between devices: none -> 35 us  [the longest x1 18.7 us: shards(): far = lax.ppermute(near, 'core', [(0, 1), (1, 0)])]
    all_to_all x2, waiting for transfers between devices: 47.9 us -> 15.1 us  [the longest x1 13.7 us: shards(): lax.all_to_all(send.reshape(chips, -1, DK), ('y', 'half', 'rest'), split_...]
    all_to_all x1, blocking collectives: 51.9 us -> 31.5 us  [shards(): return (mixer_out, combine(gather, exchange(expert_rows), middle))]
    pallas_call x3 -> x5, Pallas kernels: 11.5 us -> 23.5 us  [the longest x2 8.78 us: expert_call(): pl.pallas_call(kernel, grid_spec=pltpu.PrefetchScalarGridSpec(num_scalar_...]
    all_to_all x1, waiting for transfers between devices: 14.7 us -> 5.05 us  [shards(): lax.all_to_all(starts, every, split_axis=0, concat_axis=0, tiled=True)]
    unnamed x32 -> x12, local copies, waits for them, and re-layouts: 8.86 us -> 0.83 us
  transfers between devices with their start and end apart: 6 -> 13, of which waited for: 3 -> 8; matrix products, arithmetic and copies ran while one was open for 1% -> 0% of each run, Pallas kernels for 11% -> 16%
where the time goes in v2:
time: 203 us; the launch traced here: 202 us
  waiting for transfers between devices  68.4 us (34%)
  starting transfers between devices  54.8 us (27%)
  Pallas kernels  44.4 us (22%)
  blocking collectives  31.5 us (16%)
    all_to_all x1, blocking collectives, shards(): return (mixer_out, combine(gather, exchange(expert_rows), middle))  31.5 us
    ppermute x4, waiting for transfers between devices, across_halves(): return lax.ppermute(value, ('core', 'half'), pairs)  24.9 us
    ppermute x4, waiting for transfers between devices, along_y(): moved.append(lax.ppermute(value, 'y', pairs))  19.1 us
    ppermute x1, starting transfers between devices, shards(): far = lax.ppermute(near, 'core', [(0, 1), (1, 0)])  18.7 us
    pallas_call x1, Pallas kernels, local_terms(): pl.pallas_call(functools.partial(local_kernel, splits, part, part_rows),...  14.2 us
    all_to_all x1, waiting for transfers between devices, shards(): lax.all_to_all(send.reshape(chips, -1, DK), ('y', 'half', 'rest'), split_...  13.7 us
    ppermute x4, starting transfers between devices, across_halves(): return lax.ppermute(value, ('core', 'half'), pairs)  10.7 us
    pallas_call x2, Pallas kernels, expert_call(): pl.pallas_call(kernel, grid_spec=pltpu.PrefetchScalarGridSpec(num_scalar_...  8.78 us
  transfers between devices with their start and end apart: 13, of which 8 were waited for; matrix products, arithmetic and copies ran while one was open for 0% of the time, Pallas kernels for 16%

profile of v2, /device:TPU:0, one launch (start us, length us, event | category | flops | bytes accessed | tf_op | source)
XLA Modules:
  0.0 201.6 jit_solution(6829354235812359746)
XLA Ops:
  1.5 4.8 %collective-permute-start = (bf16[8,4096]{1,0:T(8,128)(2,1)S(1)}, bf16[8,4096]{1,0:T(8,128)(2,1)S(1)}, u32[]{:S(2)}, u32[]{:S(2)}) collective-permute-start(bf16[8,4096]{1,0:T(8,128)(2,1)S(1)} %slice.3), channel_id=1, source_target_pairs={{0,1},{1,2},{2,3},{3,4},{4,5},{5,6},{6,7},{7,8},{8,9},{9,10},{10,1... | collective-permute-start | bytes 196616 | tf_op jit(solution)/shard_map/ppermute | solution.py:586
  6.3 1.9 collective-permute-done.kh_ref.vh_ref.qh_ref
  8.2 1.9 collective-permute-start.1
  10.1 14.2 %local_terms.1 = (bf16[16,1,272,128]{3,2,1,0:T(8,128)(2,1)}, f32[8,128,128]{2,1,0:T(8,128)}, f32[16,128,256]{2,1,0:T(8,128)}) custom-call(bf16[128,4096]{1,0:T(8,128)(2,1)} %q_ref.1, bf16[128,4096]{1,0:T(8,128)(2,1)} %q_ref.1, bf16[8,4096]{1,0:T(8,128)(2,1)S(1)} %collective-permute-done.kh_ref.vh_ref.qh_ref, ...), custom_call_target="tpu_custom_call" | custom-call | tf_op jit(solution)/shard_map/local_terms/pallas_call | solution.py:220
  24.3 8.4 %all-to-all-start = ((bf16[16,272,128]{2,1,0:T(8,128)(2,1)}), bf16[16,272,128]{2,1,0:T(8,128)(2,1)S(1)}, u32[]{:S(2)}, u32[]{:S(2)}) async-start(bf16[16,272,128]{2,1,0:T(8,128)(2,1)} %bitcast.26), calls=%async_computation | async-start | bytes 2228224 | tf_op jit(solution)/shard_map/all_to_all | solution.py:594
  32.7 6.5 %reader_terms.1 = (f32[16,128,128]{2,1,0:T(8,128)}, f32[16,128,128]{2,1,0:T(8,128)}) custom-call(bf16[128,4096]{1,0:T(8,128)(2,1)} %q_ref.1, bf16[8,4096]{1,0:T(8,128)(2,1)S(1)} %collective-permute-done.kh_ref.vh_ref.qh_ref, f32[4,4096]{1,0:T(4,128)} %qw_ref.1, f32[8,128,128]{2,1,0:T(8,128)} %get-tuple-element.35.hat_ref, f32[8,2,128]{2,1,0:T(2,128)} %bitcast.28, ...), custom_call_target="tpu_custom_call" | custom-call | tf_op jit(solution)/shard_map/reader_terms/pallas_call | solution.py:268
  39.2 2.0 collective-permute-start.2
  41.2 5.3 %collective-permute-start.3 = (bf16[512,512]{1,0:T(8,128)(2,1)}, bf16[512,512]{1,0:T(8,128)(2,1)}, u32[]{:S(2)}, u32[]{:S(2)}) collective-permute-start(bf16[512,512]{1,0:T(8,128)(2,1)} %bitcast.4), channel_id=1, source_target_pairs={{0,0},{4,8},{8,4},{12,12},{1,1},{5,9},{9,5},{13,13},{2,2},{6,10},{... | collective-permute-start | bytes 1572872 | tf_op jit(solution)/shard_map/ppermute | solution.py:546
  48.2 13.7 %all-to-all-done.near_ref = bf16[16,272,128]{2,1,0:T(8,128)(2,1)S(1)} async-done(((bf16[16,272,128]{2,1,0:T(8,128)(2,1)}), bf16[16,272,128]{2,1,0:T(8,128)(2,1)S(1)}, u32[]{:S(2)}, u32[]{:S(2)}) %all-to-all-start) | async-done | bytes 1114144 | tf_op jit(solution)/shard_map/all_to_all | solution.py:594
  61.9 18.7 %collective-permute-start.4 = (bf16[16,272,128]{2,1,0:T(8,128)(2,1)S(1)}, bf16[16,272,128]{2,1,0:T(8,128)(2,1)S(1)}, u32[]{:S(2)}, u32[]{:S(2)}) collective-permute-start(bf16[16,272,128]{2,1,0:T(8,128)(2,1)S(1)} %all-to-all-done.near_ref), channel_id=1, source_target_pairs={{0,8},{8,0},{1,9},{9,1},{2,10},{10,2},{3,11},{11,3},{4,12},{12,4},... | collective-permute-start | bytes 3342344 | tf_op jit(solution)/shard_map/ppermute | solution.py:611
  80.6 2.4 %collective-permute-done.4.far_ref = bf16[16,272,128]{2,1,0:T(8,128)(2,1)S(1)} collective-permute-done((bf16[16,272,128]{2,1,0:T(8,128)(2,1)S(1)}, bf16[16,272,128]{2,1,0:T(8,128)(2,1)S(1)}, u32[]{:S(2)}, u32[]{:S(2)}) %collective-permute-start.4) | collective-permute-done | bytes 1114144 | tf_op jit(solution)/shard_map/ppermute | solution.py:611
  83.0 5.0 %scan_states.1 = bf16[32,64,128]{2,1,0:T(8,128)(2,1)} custom-call(s32[1]{0:T(128)} %bitcast.7.core_ref, bf16[16,272,128]{2,1,0:T(8,128)(2,1)S(1)} %all-to-all-done.near_ref, bf16[16,272,128]{2,1,0:T(8,128)(2,1)S(1)} %collective-permute-done.4.far_ref), custom_call_target="tpu_custom_call" | custom-call | tf_op jit(solution)/shard_map/scan_states/pallas_call | solution.py:316
  88.0 2.6 %all-to-all-start.1 = ((bf16[32,64,128]{2,1,0:T(8,128)(2,1)}), bf16[32,64,128]{2,1,0:T(8,128)(2,1)S(1)}, u32[]{:S(2)}, u32[]{:S(2)}) async-start(bf16[32,64,128]{2,1,0:T(8,128)(2,1)} %scan_states.1), calls=%async_computation.1 | async-start | bytes 1048576 | tf_op jit(solution)/shard_map/all_to_all | solution.py:614
  92.3 17.3 %collective-permute-done.6.refs_1_ = bf16[512,512]{1,0:T(8,128)(2,1)S(1)} collective-permute-done((bf16[512,512]{1,0:T(8,128)(2,1)}, bf16[512,512]{1,0:T(8,128)(2,1)S(1)}, u32[]{:S(2)}, u32[]{:S(2)}) %collective-permute-start.6) | collective-permute-done | bytes 524320 | tf_op jit(solution)/shard_map/ppermute | solution.py:553
  110.4 5.1 %all-to-all-done.1 = bf16[32,64,128]{2,1,0:T(8,128)(2,1)S(1)} async-done(((bf16[32,64,128]{2,1,0:T(8,128)(2,1)}), bf16[32,64,128]{2,1,0:T(8,128)(2,1)S(1)}, u32[]{:S(2)}, u32[]{:S(2)}) %all-to-all-start.1) | async-done | bytes 524320 | tf_op jit(solution)/shard_map/all_to_all | solution.py:614
  115.5 6.1 %mixer.1 = (bf16[128,2048]{1,0:T(8,128)(2,1)}, f32[16,128,128]{2,1,0:T(8,128)S(1)}, bf16[512,2048]{1,0:T(8,128)(2,1)}) custom-call(f32[16,128,128]{2,1,0:T(8,128)} %get-tuple-element.42.own_ref, f32[16,128,128]{2,1,0:T(8,128)} %get-tuple-element.43.reader_ref, bf16[2,2,8,64,128]{4,3,2,1,0:T(8,128)(2,1)S(1)} %bitcast.22, bf16[128,2048]{1,0:T(8,128)(2,1)} %gate_ref.1, ...), custom_call_target="tpu_custom_call" | custom-call | tf_op jit(solution)/shard_map/mixer/pallas_call | solution.py:433
  121.6 4.0 %all-to-all-start.2 = ((bf16[8,64,2048]{2,1,0:T(8,128)(2,1)}), bf16[8,64,2048]{2,1,0:T(8,128)(2,1)S(1)}, u32[]{:S(2)}, u32[]{:S(2)}) async-start(bf16[8,64,2048]{2,1,0:T(8,128)(2,1)} %bitcast.25), calls=%async_computation.2 | async-start | bytes 4194304 | tf_op jit(solution)/shard_map/all_to_all | solution.py:639
  126.5 3.5 %collective-permute-start.8 = (bf16[512,512]{1,0:T(8,128)(2,1)}, bf16[512,512]{1,0:T(8,128)(2,1)}, u32[]{:S(2)}, u32[]{:S(2)}) collective-permute-start(bf16[512,512]{1,0:T(8,128)(2,1)} %bitcast.4), channel_id=1, source_target_pairs={{0,4},{4,12},{8,0},{12,8},{1,5},{5,13},{9,1},{13,9},{2,6},{6,14},{... | collective-permute-start | bytes 1572872 | tf_op jit(solution)/shard_map/ppermute | solution.py:546
  130.0 24.9 %collective-permute-done.8.refs_2_ = bf16[512,512]{1,0:T(8,128)(2,1)} collective-permute-done((bf16[512,512]{1,0:T(8,128)(2,1)}, bf16[512,512]{1,0:T(8,128)(2,1)}, u32[]{:S(2)}, u32[]{:S(2)}) %collective-permute-start.8) | collective-permute-done | bytes 524320 | tf_op jit(solution)/shard_map/ppermute | solution.py:546
  157.3 5.3 %expert_in.1.activated_ref = bf16[512,512]{1,0:T(8,128)(2,1)S(1)} custom-call(s32[4]{0:T(128)S(1)} %pad_add_fusion.order_ref, bf16[512,2048]{1,0:T(8,128)(2,1)S(1)} %bitcast.20, bf16[512,1024]{1,0:T(8,128)(2,1)} %copy-done.3, bf16[512,1024]{1,0:T(8,128)(2,1)} %copy-done.4, bf16[512,1024]{1,0:T(8,128)(2,1)} %collective-permute-done.5.refs_2_, ...), custom_call_target="tpu_custom_call" | custom-call | tf_op jit(solution)/shard_map/expert_in/pallas_call | solution.py:494
  162.6 1.8 collective-permute-done.9.refs_3_
  164.4 3.5 %expert_out.1 = bf16[512,2048]{1,0:T(8,128)(2,1)S(1)} custom-call(s32[4]{0:T(128)S(1)} %pad_add_fusion.order_ref, bf16[512,512]{1,0:T(8,128)(2,1)S(1)} %expert_in.1.activated_ref, bf16[512,512]{1,0:T(8,128)(2,1)} %collective-permute-done.3.refs_0_, bf16[512,512]{1,0:T(8,128)(2,1)} %copy-done.5, bf16[512,512]{1,0:T(8,128)(2,1)} %collective-permute-done.8.refs_2_, ...), custom_call_target="tpu_custom_call" | custom-call | tf_op jit(solution)/shard_map/expert_out/pallas_call | solution.py:494
  168.0 31.5 %all_to_all.32 = bf16[8,64,2048]{2,1,0:T(8,128)(2,1)S(1)} all-to-all(bf16[8,64,2048]{2,1,0:T(8,128)(2,1)S(1)} %bitcast.19), channel_id=1, replica_groups=mesh['y'=2,'core'=2,'half'=2,'rest'=4] {'core','rest'}, dimensions={0} | all-to-all | bytes 4194304 | tf_op jit(solution)/shard_map/all_to_all | solution.py:641
  199.5 2.1 %combine.1 = bf16[128,2048]{1,0:T(8,128)(2,1)} custom-call(f32[512,128]{1,0:T(8,128)S(1)} %copy-done, bf16[512,2048]{1,0:T(8,128)(2,1)S(1)} %bitcast.21, f32[16,128,128]{2,1,0:T(8,128)S(1)} %get-tuple-element.59.middle_ref), custom_call_target="tpu_custom_call" | custom-call | tf_op jit(solution)/shard_map/combine/pallas_call | solution.py:530
  (25 shorter events, 8.3 us)
Async XLA Ops:
  1.5 6.7 %collective-permute-start = (bf16[8,4096]{1,0:T(8,128)(2,1)S(1)}, bf16[8,4096]{1,0:T(8,128)(2,1)S(1)}, u32[]{:S(2)}, u32[]{:S(2)}) collective-permute-start(bf16[8,4096]{1,0:T(8,128)(2,1)S(1)} %slice.3), channel_id=1, source_target_pairs={{0,1},{1,2},{2,3},{3,4},{4,5},{5,6},{6,7},{7,8},{8,9},{9,10},{10,1... | collective-permute-start | bytes 196616 | tf_op jit(solution)/shard_map/ppermute | solution.py:586
  8.2 24.5 %collective-permute-start.1 = (bf16[512,1024]{1,0:T(8,128)(2,1)}, bf16[512,1024]{1,0:T(8,128)(2,1)S(1)}, u32[]{:S(2)}, u32[]{:S(2)}) collective-permute-start(bf16[512,1024]{1,0:T(8,128)(2,1)} %bitcast.32), channel_id=1, source_target_pairs={{0,0},{4,8},{8,4},{12,12},{1,1},{5,9},{9,5},{13,13},{2,2},{6,10},{... | collective-permute-start | bytes 3145736 | tf_op jit(solution)/shard_map/ppermute | solution.py:546
  24.3 37.6 %all-to-all-start = ((bf16[16,272,128]{2,1,0:T(8,128)(2,1)}), bf16[16,272,128]{2,1,0:T(8,128)(2,1)S(1)}, u32[]{:S(2)}, u32[]{:S(2)}) async-start(bf16[16,272,128]{2,1,0:T(8,128)(2,1)} %bitcast.26), calls=%async_computation | async-start | bytes 2228224 | tf_op jit(solution)/shard_map/all_to_all | solution.py:594
  32.7 29.2 %copy-start.3 = (bf16[512,1024]{1,0:T(8,128)(2,1)}, bf16[512,1024]{1,0:T(8,128)(2,1)S(1)}, u32[]{:S(2)}) copy-start(bf16[512,1024]{1,0:T(8,128)(2,1)S(1)} %collective-permute-done.1.refs_0_) | copy-start | bytes 3145732
  39.2 76.3 %copy-start.1 = (f32[2048]{0:T(1024)S(1)}, f32[2048]{0:T(1024)}, u32[]{:S(2)}) copy-start(f32[2048]{0:T(1024)} %param.19) | copy-start | bytes 24580
  39.2 76.3 %copy-start.2 = (f32[128]{0:T(128)S(1)}, f32[128]{0:T(128)}, u32[]{:S(2)}) copy-start(f32[128]{0:T(128)} %param.18) | copy-start | bytes 1540
  39.2 22.7 %collective-permute-start.2 = (bf16[512,1024]{1,0:T(8,128)(2,1)S(1)}, bf16[512,1024]{1,0:T(8,128)(2,1)S(1)}, u32[]{:S(2)}, u32[]{:S(2)}) collective-permute-start(bf16[512,1024]{1,0:T(8,128)(2,1)S(1)} %collective-permute-done.1.refs_0_), channel_id=1, source_target_pairs={{0,16},{16,0},{1,17},{17,1},{2,18},{18,2},{3,19},{19,3},{4,20},{20... | collective-permute-start | bytes 3145736 | tf_op jit(solution)/shard_map/ppermute | solution.py:553
  41.2 7.0 %collective-permute-start.3 = (bf16[512,512]{1,0:T(8,128)(2,1)}, bf16[512,512]{1,0:T(8,128)(2,1)}, u32[]{:S(2)}, u32[]{:S(2)}) collective-permute-start(bf16[512,512]{1,0:T(8,128)(2,1)} %bitcast.4), channel_id=1, source_target_pairs={{0,0},{4,8},{8,4},{12,12},{1,1},{5,9},{9,5},{13,13},{2,2},{6,10},{... | collective-permute-start | bytes 1572872 | tf_op jit(solution)/shard_map/ppermute | solution.py:546
  61.9 53.6 %copy-start.4 = (bf16[512,1024]{1,0:T(8,128)(2,1)}, bf16[512,1024]{1,0:T(8,128)(2,1)S(1)}, u32[]{:S(2)}) copy-start(bf16[512,1024]{1,0:T(8,128)(2,1)S(1)} %collective-permute-done.2.refs_1_) | copy-start | bytes 3145732
  61.9 21.1 %collective-permute-start.4 = (bf16[16,272,128]{2,1,0:T(8,128)(2,1)S(1)}, bf16[16,272,128]{2,1,0:T(8,128)(2,1)S(1)}, u32[]{:S(2)}, u32[]{:S(2)}) collective-permute-start(bf16[16,272,128]{2,1,0:T(8,128)(2,1)S(1)} %all-to-all-done.near_ref), channel_id=1, source_target_pairs={{0,8},{8,0},{1,9},{9,1},{2,10},{10,2},{3,11},{11,3},{4,12},{12,4},... | collective-permute-start | bytes 3342344 | tf_op jit(solution)/shard_map/ppermute | solution.py:611
  80.6 29.8 %collective-permute-start.5 = (bf16[512,1024]{1,0:T(8,128)(2,1)}, bf16[512,1024]{1,0:T(8,128)(2,1)}, u32[]{:S(2)}, u32[]{:S(2)}) collective-permute-start(bf16[512,1024]{1,0:T(8,128)(2,1)} %bitcast.33), channel_id=1, source_target_pairs={{0,4},{4,12},{8,0},{12,8},{1,5},{5,13},{9,1},{13,9},{2,6},{6,14},{... | collective-permute-start | bytes 3145736 | tf_op jit(solution)/shard_map/ppermute | solution.py:546
  88.0 27.5 %all-to-all-start.1 = ((bf16[32,64,128]{2,1,0:T(8,128)(2,1)}), bf16[32,64,128]{2,1,0:T(8,128)(2,1)S(1)}, u32[]{:S(2)}, u32[]{:S(2)}) async-start(bf16[32,64,128]{2,1,0:T(8,128)(2,1)} %scan_states.1), calls=%async_computation.1 | async-start | bytes 1048576 | tf_op jit(solution)/shard_map/all_to_all | solution.py:614
  90.6 19.0 %collective-permute-start.6 = (bf16[512,512]{1,0:T(8,128)(2,1)}, bf16[512,512]{1,0:T(8,128)(2,1)S(1)}, u32[]{:S(2)}, u32[]{:S(2)}) collective-permute-start(bf16[512,512]{1,0:T(8,128)(2,1)} %collective-permute-done.3.refs_0_), channel_id=1, source_target_pairs={{0,16},{16,0},{1,17},{17,1},{2,18},{18,2},{3,19},{19,3},{4,20},{20... | collective-permute-start | bytes 1572872 | tf_op jit(solution)/shard_map/ppermute | solution.py:553
  109.6 0.8 copy-start.5
  121.6 35.7 %all-to-all-start.2 = ((bf16[8,64,2048]{2,1,0:T(8,128)(2,1)}), bf16[8,64,2048]{2,1,0:T(8,128)(2,1)S(1)}, u32[]{:S(2)}, u32[]{:S(2)}) async-start(bf16[8,64,2048]{2,1,0:T(8,128)(2,1)} %bitcast.25), calls=%async_computation.2 | async-start | bytes 4194304 | tf_op jit(solution)/shard_map/all_to_all | solution.py:639
  125.6 30.4 %collective-permute-start.7 = (bf16[512,1024]{1,0:T(8,128)(2,1)}, bf16[512,1024]{1,0:T(8,128)(2,1)}, u32[]{:S(2)}, u32[]{:S(2)}) collective-permute-start(bf16[512,1024]{1,0:T(8,128)(2,1)} %collective-permute-done.5.refs_2_), channel_id=1, source_target_pairs={{0,16},{16,0},{1,17},{17,1},{2,18},{18,2},{3,19},{19,3},{4,20},{20... | collective-permute-start | bytes 3145736 | tf_op jit(solution)/shard_map/ppermute | solution.py:553
  126.5 28.4 %collective-permute-start.8 = (bf16[512,512]{1,0:T(8,128)(2,1)}, bf16[512,512]{1,0:T(8,128)(2,1)}, u32[]{:S(2)}, u32[]{:S(2)}) collective-permute-start(bf16[512,512]{1,0:T(8,128)(2,1)} %bitcast.4), channel_id=1, source_target_pairs={{0,4},{4,12},{8,0},{12,8},{1,5},{5,13},{9,1},{13,9},{2,6},{6,14},{... | collective-permute-start | bytes 1572872 | tf_op jit(solution)/shard_map/ppermute | solution.py:546
  154.9 9.5 %collective-permute-start.9 = (bf16[512,512]{1,0:T(8,128)(2,1)}, bf16[512,512]{1,0:T(8,128)(2,1)}, u32[]{:S(2)}, u32[]{:S(2)}) collective-permute-start(bf16[512,512]{1,0:T(8,128)(2,1)} %collective-permute-done.8.refs_2_), channel_id=1, source_target_pairs={{0,16},{16,0},{1,17},{17,1},{2,18},{18,2},{3,19},{19,3},{4,20},{20... | collective-permute-start | bytes 1572872 | tf_op jit(solution)/shard_map/ppermute | solution.py:553
  167.9 31.6 %copy-start = (f32[512,128]{1,0:T(8,128)S(1)}, f32[512,128]{1,0:T(8,128)}, u32[]{:S(2)}) copy-start(f32[512,128]{1,0:T(8,128)} %get-tuple-element.50.gather_ref) | copy-start | bytes 786436

commit v3 on v2

--- a/solution.py
+++ b/solution.py
@@ -19,6 +19,7 @@
 GROUP = VALUE_HEAD_SET // HK
 HALO = 8
 STEP_KEYS = 2
+READER_KEYS = 2
 FADE_ROWS = 16
 
 f32 = jnp.float32
@@ -244,13 +245,23 @@
 
 
 def reader_kernel(
-    q_ref, qh_ref, qw_ref, hat_ref, decay_ref, fresh_ref, own_ref, reader_ref
+    q_ref,
+    qh_ref,
+    qw_ref,
+    hat_ref,
+    decay_ref,
+    fresh_ref,
+    gate_ref,
+    gain_ref,
+    own_ref,
+    reader_ref,
+    scale_ref,
 ):
     rows = q_ref.shape[0]
     queries = conv_silu(q_ref, qh_ref, qw_ref)
     row_ids, col_ids = square_ids(rows)
     masks = row_ids == col_ids, row_ids >= col_ids, row_ids <= col_ids
-    for key in range(STEP_KEYS):
+    for key in range(READER_KEYS):
         query = key_rows_hat(queries[:, key * DK : (key + 1) * DK]) * DK ** (-0.5)
         raw = three_pass_nt(halves(query), halves(hat_ref[key]))
         for member in range(GROUP):
@@ -259,28 +270,39 @@
             mixed = three_pass(fading * raw, fresh_ref[head])
             own_ref[head] = mixed[:, :DV]
             reader_ref[head] = jnp.exp(cum_col) * query - mixed[:, DV:]
-
-
-def reader_terms(mixed_qkv, halo, conv_weight, log_decay, hats, fresh):
-    rows = mixed_qkv.shape[0]
-    key_cols, step_heads = STEP_KEYS * DK, STEP_KEYS * GROUP
+            gate = gate_ref[:, head * DV : (head + 1) * DV].astype(f32)
+            scale_ref[head] = silu(gate) * gain_ref[...]
+
+
+def reader_terms(mixed_qkv, halo, conv_weight, log_decay, hats, fresh, out_gate, gain):
+    rows = out_gate.shape[0]
+    key_cols, step_heads = READER_KEYS * DK, READER_KEYS * GROUP
+    value_cols = step_heads * DV
     per_head = pl.BlockSpec((step_heads, rows, DK), lambda i: (i, 0, 0))
+    columns = pl.BlockSpec((rows, value_cols), lambda i: (0, i))
     return pl.pallas_call(
         reader_kernel,
-        grid=(HK // STEP_KEYS,),
+        grid=(HK // READER_KEYS,),
         in_specs=[pl.BlockSpec((tall, key_cols), lambda i: (0, i)) for tall in (rows, HALO, CONV)]
         + [
-            pl.BlockSpec((STEP_KEYS, rows, DK), lambda i: (i, 0, 0)),
-            pl.BlockSpec((STEP_KEYS, GROUP, rows), lambda i: (i, 0, 0)),
+            pl.BlockSpec((READER_KEYS, rows, DK), lambda i: (i, 0, 0)),
+            pl.BlockSpec((READER_KEYS, GROUP, rows), lambda i: (i, 0, 0)),
             pl.BlockSpec((step_heads, rows, DV + DK), lambda i: (i, 0, 0)),
+            columns,
+            pl.BlockSpec((1, DV), lambda i: (0, 0)),
         ],
-        out_specs=[per_head, per_head],
-        out_shape=[pltpu.HBM((VALUE_HEAD_SET, rows, DK), f32)] * 2,
+        out_specs=[per_head, per_head, per_head],
+        out_shape=[pltpu.HBM((VALUE_HEAD_SET, rows, DK), f32)] * 3,
         compiler_params=pltpu.CompilerParams(
             dimension_semantics=("arbitrary",), vmem_limit_bytes=24 << 20
         ),
         name="reader_terms",
-    )(*hbm(mixed_qkv), halo, *hbm(conv_weight, hats, log_decay, fresh))
+    )(
+        *hbm(mixed_qkv),
+        halo,
+        *hbm(conv_weight, hats, log_decay, fresh, out_gate),
+        gain[None],
+    )
 
 
 def scan_kernel(core_ref, near_ref, far_ref, start_ref, state_ref):
@@ -330,7 +352,7 @@
     )(core, near, far)
 
 
-def route_kernel(capacity, routes_ref, gates_ref, select_ref, gather_ref):
+def route_kernel(capacity, routes_ref, gates_ref, select_ref, high_ref, low_ref):
     rows = routes_ref.shape[1]
     experts = select_ref.shape[0] // capacity
     expert_ids = lax.broadcasted_iota(jnp.int32, (experts, rows), 0)
@@ -340,19 +362,20 @@
         named = routes_ref[choice : choice + 1, :] == expert_ids
         chosen = chosen | named
         gates = gates + jnp.where(named, gates_ref[choice : choice + 1, :], 0.0)
-    earlier = lax.broadcasted_iota(jnp.int32, (rows, rows), 0) < lax.broadcasted_iota(
-        jnp.int32, (rows, rows), 1
-    )
+    row_ids, col_ids = square_ids(rows)
     rank = dot(
-        jnp.where(chosen, 1.0, 0.0).astype(bf16), jnp.where(earlier, 1.0, 0.0).astype(bf16)
+        jnp.where(chosen, 1.0, 0.0).astype(bf16),
+        jnp.where(row_ids < col_ids, 1.0, 0.0).astype(bf16),
     )
     slot = jnp.where(chosen, rank, -1.0).astype(jnp.int32)
     slot_ids = lax.broadcasted_iota(jnp.int32, (capacity, rows), 0)
+    gathers = []
     for expert in range(experts):
         span = slice(expert * capacity, (expert + 1) * capacity)
         taken = slot_ids == slot[expert : expert + 1, :]
         select_ref[span, :] = jnp.where(taken, 1.0, 0.0).astype(bf16)
-        gather_ref[span, :] = jnp.where(taken, gates[expert : expert + 1, :], 0.0)
+        gathers.append(jnp.where(taken, gates[expert : expert + 1, :], 0.0))
+    high_ref[...], low_ref[...] = halves(jnp.concatenate(gathers, axis=0).T)
 
 
 def route_tables(routes, route_gates, experts, capacity):
@@ -361,149 +384,187 @@
     return pl.pallas_call(
         functools.partial(route_kernel, capacity),
         out_shape=[
-            jax.ShapeDtypeStruct((slots, rows), bf16),
-            jax.ShapeDtypeStruct((slots, rows), f32),
+            pltpu.HBM((slots, rows), bf16),
+            pltpu.HBM((rows, slots), bf16),
+            pltpu.HBM((rows, slots), bf16),
         ],
         name="route_tables",
     )(routes.T, route_gates.T)
 
 
 def mixer_kernel(
+    state_ref,
+    moe_gain_ref,
+    select_hbm,
+    own_hbm,
+    reader_hbm,
+    scale_hbm,
+    resid_hbm,
+    middle_hbm,
+    mixer_hbm,
+    rows_hbm,
+    select_ref,
+    middle_ref,
     own_ref,
     reader_ref,
-    state_ref,
-    gate_ref,
+    scale_ref,
     resid_ref,
-    head_gain_ref,
-    moe_gain_ref,
-    select_ref,
     mixer_ref,
-    middle_ref,
     rows_ref,
-    squares_ref,
+    in_sems,
+    mixer_sems,
+    rows_sems,
+    middle_sems,
+    select_sem,
 ):
-    step, heads = pl.program_id(0), own_ref.shape[0]
-    squares = jnp.where(step == 0, jnp.zeros_like(squares_ref), squares_ref[...])
-    for head in range(heads):
-        span = slice(head * DV, (head + 1) * DV)
-        if len(state_ref.shape) == 3:
-            state = state_ref[head]
-        else:
-            state = jnp.concatenate([state_ref[0, core, head] for core in range(2)], axis=0)
-        high, low = halves(reader_ref[head])
-        head_out = own_ref[head] + (dot_nt(high, state) + dot_nt(low, state))
-        scaled = (
-            head_out
-            * lax.rsqrt(jnp.mean(head_out * head_out, axis=1, keepdims=True) + 1e-06)
-            * head_gain_ref[...]
+    groups = in_sems.shape[0]
+    heads = VALUE_HEAD_SET // groups
+    loads, stores = [], []
+    for group in range(groups):
+        part, columns = pl.ds(group * heads, heads), pl.ds(group * heads * DV, heads * DV)
+        loads.append(
+            [
+                pltpu.make_async_copy(source, target, in_sems.at[group, place])
+                for place, (source, target) in enumerate(
+                    (
+                        (own_hbm.at[part], own_ref.at[part]),
+                        (reader_hbm.at[part], reader_ref.at[part]),
+                        (scale_hbm.at[part], scale_ref.at[part]),
+                        (resid_hbm.at[:, columns], resid_ref.at[:, columns]),
+                    )
+                )
+            ]
         )
-        mixed = (scaled * silu(gate_ref[:, span].astype(f32))).astype(bf16)
-        mixer_ref[:, span] = mixed
-        middle = resid_ref[:, span].astype(f32) + mixed.astype(f32)
-        middle_ref[step * heads + head] = middle
-        squares = squares + jnp.sum(middle * middle, axis=1, keepdims=True)
-    squares_ref[...] = squares
-
-    @pl.when(step == pl.num_programs(0) - 1)
-    def _():
-        scale = lax.rsqrt(squares / moe_gain_ref.shape[1] + 1e-06)
-        select = select_ref[...]
-        for head in range(VALUE_HEAD_SET):
+        for load in loads[-1]:
+            load.start()
+    select_load = pltpu.make_async_copy(select_hbm, select_ref, select_sem)
+    select_load.start()
+
+    squares = None
+    for group in range(groups):
+        for load in loads[group]:
+            load.wait()
+        for head in range(group * heads, (group + 1) * heads):
             span = slice(head * DV, (head + 1) * DV)
-            moe_input = (middle_ref[head] * scale * moe_gain_ref[:, span]).astype(bf16)
+            if len(state_ref.shape) == 3:
+                state = state_ref[head]
+            else:
+                block = state_ref.shape[2]
+                pieces = [state_ref[head // block, core, head % block] for core in range(2)]
+                state = jnp.concatenate(pieces, axis=0)
+            high, low = halves(reader_ref[head])
+            head_out = own_ref[head] + (dot_nt(high, state) + dot_nt(low, state))
+            spread = lax.rsqrt(jnp.mean(head_out * head_out, axis=1, keepdims=True) + 1e-06)
+            mixed = (head_out * spread * scale_ref[head]).astype(bf16)
+            mixer_ref[:, span] = mixed
+            middle = resid_ref[:, span].astype(f32) + mixed.astype(f32)
+            middle_ref[head] = middle
+            part = jnp.sum(middle * middle, axis=1, keepdims=True)
+            squares = part if squares is None else squares + part
+        columns = pl.ds(group * heads * DV, heads * DV)
+        part = pl.ds(group * heads, heads)
+        stores.append(
+            pltpu.make_async_copy(middle_ref.at[part], middle_hbm.at[part], middle_sems.at[group])
+        )
+        stores[-1].start()
+        stores.append(
+            pltpu.make_async_copy(
+                mixer_ref.at[:, columns], mixer_hbm.at[:, columns], mixer_sems.at[group]
+            )
+        )
+        stores[-1].start()
+
+    spread = lax.rsqrt(squares / resid_ref.shape[1] + 1e-06)
+    select_load.wait()
+    select = select_ref[...]
+    for group in range(groups):
+        for head in range(group * heads, (group + 1) * heads):
+            span = slice(head * DV, (head + 1) * DV)
+            moe_input = (middle_ref[head] * spread * moe_gain_ref[:, span]).astype(bf16)
             rows_ref[:, span] = dot(select, moe_input).astype(bf16)
-
-
-def mixer(own, reader, state, out_gate, resid, head_gain, moe_gain, select):
+        columns = pl.ds(group * heads * DV, heads * DV)
+        stores.append(
+            pltpu.make_async_copy(
+                rows_ref.at[:, columns], rows_hbm.at[:, columns], rows_sems.at[group]
+            )
+        )
+        stores[-1].start()
+    for store in stores:
+        store.wait()
+
+
+def mixer(own, reader, scale, resid, select, state, moe_gain):
     rows, width = resid.shape
-    heads = 4
-    per_head = pl.BlockSpec((heads, rows, DV), lambda i: (i, 0, 0))
-    columns = pl.BlockSpec((rows, heads * DV), lambda i: (0, i))
-    if state.ndim == 3:
-        state_spec = pl.BlockSpec((heads, DV, DK), lambda i: (i, 0, 0))
-    else:
-        block = state.shape[2] // heads
-        state_spec = pl.BlockSpec(
-            (1, 2, heads) + state.shape[3:], lambda i: (i // block, 0, i % block, 0, 0)
-        )
-
-    def whole(*shape):
-        return pl.BlockSpec(shape, lambda i: (0,) * len(shape))
-
+    slots, groups = select.shape[0], 4
+    local, remote = pl.BlockSpec(memory_space=pltpu.VMEM), pl.BlockSpec(memory_space=pltpu.HBM)
     return pl.pallas_call(
         mixer_kernel,
-        grid=(VALUE_HEAD_SET // heads,),
-        in_specs=[
-            per_head,
-            per_head,
-            state_spec,
-            columns,
-            columns,
-            whole(1, DV),
-            whole(1, width),
-            whole(*select.shape),
+        in_specs=[local] * 2 + [remote] * 5,
+        out_specs=[remote] * 3,
+        out_shape=[
+            pltpu.HBM((VALUE_HEAD_SET, rows, DV), f32),
+            pltpu.HBM((rows, width), bf16),
+            pltpu.HBM((slots, width), bf16),
         ],
-        out_specs=[
-            columns,
-            whole(VALUE_HEAD_SET, rows, DV),
-            whole(select.shape[0], width),
+        scratch_shapes=[pltpu.VMEM((slots, rows), bf16)]
+        + [pltpu.VMEM((VALUE_HEAD_SET, rows, DV), f32)] * 4
+        + [
+            pltpu.VMEM((rows, width), bf16),
+            pltpu.VMEM((rows, width), bf16),
+            pltpu.VMEM((slots, width), bf16),
+            pltpu.SemaphoreType.DMA((groups, 4)),
+            pltpu.SemaphoreType.DMA((groups,)),
+            pltpu.SemaphoreType.DMA((groups,)),
+            pltpu.SemaphoreType.DMA((groups,)),
+            pltpu.SemaphoreType.DMA,
         ],
-        out_shape=[
-            pltpu.HBM((rows, width), bf16),
-            jax.ShapeDtypeStruct((VALUE_HEAD_SET, rows, DV), f32),
-            pltpu.HBM((select.shape[0], width), bf16),
-        ],
-        scratch_shapes=[pltpu.VMEM((rows, 1), f32)],
-        compiler_params=pltpu.CompilerParams(
-            dimension_semantics=("arbitrary",), vmem_limit_bytes=24 << 20
-        ),
+        compiler_params=pltpu.CompilerParams(vmem_limit_bytes=24 << 20),
         name="mixer",
-    )(
-        *hbm(own, reader),
-        state,
-        *hbm(out_gate, resid),
-        head_gain[None],
-        moe_gain[None],
-        *hbm(select),
-    )
+    )(state, moe_gain[None], *hbm(select, own, reader, scale, resid))
+
+
+def start_loads(sources, buffer_ref, sems):
+    loads = [
+        pltpu.make_async_copy(source, buffer_ref.at[place], sems.at[place])
+        for place, source in enumerate(sources)
+    ]
+    for load in loads:
+        load.start()
+    return loads
 
 
 def expert_in_kernel(order_ref, rows_ref, *refs):
-    in_refs, result_ref = refs[:-1], refs[-1]
-    projected = None
-    for place, ref in enumerate(in_refs):
-        depth = ref.shape[0]
+    sources, (result_ref, buffer_ref, sems) = refs[:-3], refs[-3:]
+    depth, projected = buffer_ref.shape[1], None
+    for place, load in enumerate(start_loads(sources, buffer_ref, sems)):
         start = pl.multiple_of(order_ref[place] * depth, depth)
-        term = dot(rows_ref[:, pl.ds(start, depth)], ref[...])
+        load.wait()
+        term = dot(rows_ref[:, pl.ds(start, depth)], buffer_ref[place])
         projected = term if projected is None else projected + term
     result_ref[...] = (silu(projected[:, :MOE_H]) * projected[:, MOE_H:]).astype(bf16)
 
 
 def expert_out_kernel(order_ref, activated_ref, *refs):
-    out_refs, result_ref = refs[:-1], refs[-1]
-    activated = activated_ref[...]
-    for place, ref in enumerate(out_refs):
-        cols = ref.shape[1]
+    sources, (result_ref, buffer_ref, sems) = refs[:-3], refs[-3:]
+    cols, activated = buffer_ref.shape[2], activated_ref[...]
+    for place, load in enumerate(start_loads(sources, buffer_ref, sems)):
         start = pl.multiple_of(order_ref[place] * cols, cols)
-        result_ref[:, pl.ds(start, cols)] = dot(activated, ref[...]).astype(bf16)
+        load.wait()
+        result_ref[:, pl.ds(start, cols)] = dot(activated, buffer_ref[place]).astype(bf16)
 
 
 def expert_call(kernel, name, order, rows, parts, width):
-    count = rows.shape[0]
-    block = min(count, 256)
+    local, remote = pl.BlockSpec(memory_space=pltpu.VMEM), pl.BlockSpec(memory_space=pltpu.HBM)
     return pl.pallas_call(
         kernel,
-        grid_spec=pltpu.PrefetchScalarGridSpec(
-            num_scalar_prefetch=1,
-            grid=(count // block,),
-            in_specs=[pl.BlockSpec((block, rows.shape[1]), lambda i, order: (i, 0))]
-            + [pl.BlockSpec(part.shape, lambda i, order: (0, 0)) for part in parts],
-            out_specs=pl.BlockSpec((block, width), lambda i, order: (i, 0)),
-        ),
-        out_shape=jax.ShapeDtypeStruct((count, width), bf16),
-        compiler_params=pltpu.CompilerParams(
-            dimension_semantics=("arbitrary",), vmem_limit_bytes=24 << 20
-        ),
+        in_specs=[pl.BlockSpec(memory_space=pltpu.SMEM), local] + [remote] * len(parts),
+        out_specs=local,
+        out_shape=jax.ShapeDtypeStruct((rows.shape[0], width), bf16),
+        scratch_shapes=[
+            pltpu.VMEM((len(parts),) + parts[0].shape, bf16),
+            pltpu.SemaphoreType.DMA((len(parts),)),
+        ],
+        compiler_params=pltpu.CompilerParams(vmem_limit_bytes=24 << 20),
         name=name,
     )(order, rows, *hbm(*parts))
 
@@ -517,22 +578,22 @@
     return expert_call(expert_out_kernel, "expert_out", order, activated, parts, width)
 
 
-def combine_kernel(gather_ref, rows_ref, middle_ref, out_ref):
-    high, low = halves(gather_ref[...].T)
+def combine_kernel(high_ref, low_ref, middle_ref, rows_ref, out_ref):
+    high, low = high_ref[...], low_ref[...]
     for head in range(middle_ref.shape[0]):
         span = slice(head * DV, (head + 1) * DV)
         rows = rows_ref[:, span]
         out_ref[:, span] = (middle_ref[head] + (dot(high, rows) + dot(low, rows))).astype(bf16)
 
 
-def combine(gather, rows, middle):
+def combine(high, low, middle, rows):
     count, width = middle.shape[1], rows.shape[1]
     return pl.pallas_call(
         combine_kernel,
         out_shape=pltpu.HBM((count, width), bf16),
         compiler_params=pltpu.CompilerParams(vmem_limit_bytes=24 << 20),
         name="combine",
-    )(gather, rows, middle)
+    )(high, low, middle, rows)
 
 
 def after(value, earlier):
@@ -599,13 +660,13 @@
         tiled=True,
     )
     hats, in_first = tie((hats, in_first))
-    own, reader = reader_terms(mixed_qkv, halo, conv_weight, log_decay, hats, fresh)
-    select, gather = route_tables(routes, route_gates, experts, capacity)
-    in_first = along_y(after(in_first, own), y_count)
+    own, reader, scale = reader_terms(
+        mixed_qkv, halo, conv_weight, log_decay, hats, fresh, out_gate, head_gain
+    )
+    select, *gather = route_tables(routes, route_gates, experts, capacity)
+    in_first = along_y(in_first, y_count)
     out_first = across_halves(after(w_out[0], send), 0)
-    near, in_first, out_first, own, reader, select = tie(
-        (near, in_first, out_first, own, reader, select)
-    )
+    near, in_first, out_first, own, select = tie((near, in_first, out_first, own, select))
 
     in_second = across_halves(after(w_in[0], near), 1)
     far = lax.ppermute(near, "core", [(0, 1), (1, 0)])
@@ -619,8 +680,8 @@
     if part < part_rows or splits > 1:
         states = states[:, :, :, :part].transpose(0, 2, 1, 3, 4)
         states = states.reshape(VALUE_HEAD_SET, DV, DK)
-    mixer_out, middle, send_rows = mixer(
-        own, reader, states, out_gate, resid, head_gain, moe_gain, select
+    middle, mixer_out, send_rows = mixer(
+        own, reader, scale, resid, select, states, moe_gain
     )
     in_second = along_y(after(in_second, send_rows), y_count)
     out_second = across_halves(after(w_out[0], send_rows), 1)
@@ -638,7 +699,7 @@
     )
     activated = expert_in(order, exchange(send_rows), in_first + in_second)
     expert_rows = expert_out(order, activated, out_first + out_second, send_rows.shape[1])
-    return mixer_out, combine(gather, exchange(expert_rows), middle)
+    return mixer_out, combine(*gather, middle, exchange(expert_rows))
 
 
 def solution(mesh):

time: 203 us -> 198 us (0.975)
  starting transfers between devices: 54.8 us -> 49.7 us
  waiting for transfers between devices: 68.4 us -> 71.4 us
    ppermute x1, starting transfers between devices: 18.7 us -> 12.9 us  [shards(): far = lax.ppermute(near, 'core', [(0, 1), (1, 0)])]
    all_to_all x1, starting transfers between devices: 2.61 us -> 5.75 us  [shards(): lax.all_to_all(starts, every, split_axis=0, concat_axis=0, tiled=True)]
    pallas_call x5, Pallas kernels: 23 us -> 21 us  [the longest x2 7.94 us: expert_call(): pl.pallas_call(kernel, in_specs=[pl.BlockSpec(memory_space=pltpu.SMEM), l...]
where the time goes in v3:
time: 198 us; the launch traced here: 197 us
  waiting for transfers between devices  71.4 us (36%)
  starting transfers between devices  49.7 us (25%)
  Pallas kernels  42.4 us (21%)
  blocking collectives  30.5 us (15%)
    all_to_all x1, blocking collectives, shards(): return (mixer_out, combine(*gather, middle, exchange(expert_rows)))  30.5 us
    ppermute x4, waiting for transfers between devices, across_halves(): return lax.ppermute(value, ('core', 'half'), pairs)  26.9 us
    ppermute x4, waiting for transfers between devices, along_y(): moved.append(lax.ppermute(value, 'y', pairs))  19.8 us
    pallas_call x1, Pallas kernels, local_terms(): pl.pallas_call(functools.partial(local_kernel, splits, part, part_rows),...  14.2 us
    all_to_all x1, waiting for transfers between devices, shards(): lax.all_to_all(send.reshape(chips, -1, DK), ('y', 'half', 'rest'), split_...  13.7 us
    ppermute x1, starting transfers between devices, shards(): far = lax.ppermute(near, 'core', [(0, 1), (1, 0)])  12.9 us
    ppermute x4, starting transfers between devices, across_halves(): return lax.ppermute(value, ('core', 'half'), pairs)  8.85 us
    all_to_all x1, starting transfers between devices, shards(): lax.all_to_all(send.reshape(chips, -1, DK), ('y', 'half', 'rest'), split_...  8.46 us
  transfers between devices with their start and end apart: 13, of which 8 were waited for; matrix products, arithmetic and copies ran while one was open for 0% of the time, Pallas kernels for 16%

profile of v3, /device:TPU:0, one launch (start us, length us, event | category | flops | bytes accessed | tf_op | source)
XLA Modules:
  0.0 196.7 jit_solution(2165323822491185732)
XLA Ops:
  1.5 4.8 %collective-permute-start = (bf16[8,4096]{1,0:T(8,128)(2,1)S(1)}, bf16[8,4096]{1,0:T(8,128)(2,1)S(1)}, u32[]{:S(2)}, u32[]{:S(2)}) collective-permute-start(bf16[8,4096]{1,0:T(8,128)(2,1)S(1)} %slice.3), channel_id=1, source_target_pairs={{0,1},{1,2},{2,3},{3,4},{4,5},{5,6},{6,7},{7,8},{8,9},{9,10},{10,1... | collective-permute-start | bytes 196616 | tf_op jit(solution)/shard_map/ppermute | solution.py:647
  6.3 1.9 collective-permute-done.kh_ref.vh_ref.qh_ref
  8.2 1.9 collective-permute-start.1
  10.1 14.2 %local_terms.1 = (bf16[16,1,272,128]{3,2,1,0:T(8,128)(2,1)}, f32[8,128,128]{2,1,0:T(8,128)}, f32[16,128,256]{2,1,0:T(8,128)}) custom-call(bf16[128,4096]{1,0:T(8,128)(2,1)} %q_ref.1, bf16[128,4096]{1,0:T(8,128)(2,1)} %q_ref.1, bf16[8,4096]{1,0:T(8,128)(2,1)S(1)} %collective-permute-done.kh_ref.vh_ref.qh_ref, ...), custom_call_target="tpu_custom_call" | custom-call | tf_op jit(solution)/shard_map/local_terms/pallas_call | solution.py:221
  24.3 8.5 %all-to-all-start = ((bf16[16,272,128]{2,1,0:T(8,128)(2,1)}), bf16[16,272,128]{2,1,0:T(8,128)(2,1)S(1)}, u32[]{:S(2)}, u32[]{:S(2)}) async-start(bf16[16,272,128]{2,1,0:T(8,128)(2,1)} %bitcast.26), calls=%async_computation | async-start | bytes 2228224 | tf_op jit(solution)/shard_map/all_to_all | solution.py:655
  32.8 2.0 %collective-permute-start.2 = (bf16[512,1024]{1,0:T(8,128)(2,1)S(1)}, bf16[512,1024]{1,0:T(8,128)(2,1)S(1)}, u32[]{:S(2)}, u32[]{:S(2)}) collective-permute-start(bf16[512,1024]{1,0:T(8,128)(2,1)S(1)} %collective-permute-done.1.refs_0_), channel_id=1, source_target_pairs={{0,16},{16,0},{1,17},{17,1},{2,18},{18,2},{3,19},{19,3},{4,20},{20... | collective-permute-start | bytes 3145736 | tf_op jit(solution)/shard_map/ppermute | solution.py:614
  34.8 5.4 %collective-permute-start.3 = (bf16[512,512]{1,0:T(8,128)(2,1)}, bf16[512,512]{1,0:T(8,128)(2,1)}, u32[]{:S(2)}, u32[]{:S(2)}) collective-permute-start(bf16[512,512]{1,0:T(8,128)(2,1)} %bitcast.34), channel_id=1, source_target_pairs={{0,0},{4,8},{8,4},{12,12},{1,1},{5,9},{9,5},{13,13},{2,2},{6,10},{... | collective-permute-start | bytes 1572872 | tf_op jit(solution)/shard_map/ppermute | solution.py:607
  41.8 6.3 %reader_terms.1 = (f32[16,128,128]{2,1,0:T(8,128)}, f32[16,128,128]{2,1,0:T(8,128)}, f32[16,128,128]{2,1,0:T(8,128)}) custom-call(bf16[128,4096]{1,0:T(8,128)(2,1)} %q_ref.1, bf16[8,4096]{1,0:T(8,128)(2,1)S(1)} %collective-permute-done.kh_ref.vh_ref.qh_ref, f32[4,4096]{1,0:T(4,128)} %qw_ref.1, f32[8,128,128]{2,1,0:T(8,128)} %get-tuple-element.36.hat_ref, ...), custom_call_target="tpu_custom_call" | custom-call | tf_op jit(solution)/shard_map/reader_terms/pallas_call | solution.py:283
  48.2 13.7 %all-to-all-done.near_ref = bf16[16,272,128]{2,1,0:T(8,128)(2,1)S(1)} async-done(((bf16[16,272,128]{2,1,0:T(8,128)(2,1)}), bf16[16,272,128]{2,1,0:T(8,128)(2,1)S(1)}, u32[]{:S(2)}, u32[]{:S(2)}) %all-to-all-start) | async-done | bytes 1114144 | tf_op jit(solution)/shard_map/all_to_all | solution.py:655
  62.8 12.9 %collective-permute-start.4 = (bf16[16,272,128]{2,1,0:T(8,128)(2,1)S(1)}, bf16[16,272,128]{2,1,0:T(8,128)(2,1)S(1)}, u32[]{:S(2)}, u32[]{:S(2)}) collective-permute-start(bf16[16,272,128]{2,1,0:T(8,128)(2,1)S(1)} %all-to-all-done.near_ref), channel_id=1, source_target_pairs={{0,8},{8,0},{1,9},{9,1},{2,10},{10,2},{3,11},{11,3},{4,12},{12,4},... | collective-permute-start | bytes 3342344 | tf_op jit(solution)/shard_map/ppermute | solution.py:672
  75.7 2.4 %collective-permute-done.4.far_ref = bf16[16,272,128]{2,1,0:T(8,128)(2,1)S(1)} collective-permute-done((bf16[16,272,128]{2,1,0:T(8,128)(2,1)S(1)}, bf16[16,272,128]{2,1,0:T(8,128)(2,1)S(1)}, u32[]{:S(2)}, u32[]{:S(2)}) %collective-permute-start.4) | collective-permute-done | bytes 1114144 | tf_op jit(solution)/shard_map/ppermute | solution.py:672
  78.1 5.1 %scan_states.1 = bf16[32,64,128]{2,1,0:T(8,128)(2,1)} custom-call(s32[1]{0:T(128)} %bitcast.core_ref, bf16[16,272,128]{2,1,0:T(8,128)(2,1)S(1)} %all-to-all-done.near_ref, bf16[16,272,128]{2,1,0:T(8,128)(2,1)S(1)} %collective-permute-done.4.far_ref), custom_call_target="tpu_custom_call" | custom-call | tf_op jit(solution)/shard_map/scan_states/pallas_call | solution.py:338
  83.2 5.7 %all-to-all-start.1 = ((bf16[32,64,128]{2,1,0:T(8,128)(2,1)}), bf16[32,64,128]{2,1,0:T(8,128)(2,1)S(1)}, u32[]{:S(2)}, u32[]{:S(2)}) async-start(bf16[32,64,128]{2,1,0:T(8,128)(2,1)} %scan_states.1), calls=%async_computation.1 | async-start | bytes 1048576 | tf_op jit(solution)/shard_map/all_to_all | solution.py:675
  89.0 1.8 collective-permute-start.6
  90.8 17.3 %collective-permute-done.6.refs_1_ = bf16[512,512]{1,0:T(8,128)(2,1)S(1)} collective-permute-done((bf16[512,512]{1,0:T(8,128)(2,1)}, bf16[512,512]{1,0:T(8,128)(2,1)S(1)}, u32[]{:S(2)}, u32[]{:S(2)}) %collective-permute-start.6) | collective-permute-done | bytes 524320 | tf_op jit(solution)/shard_map/ppermute | solution.py:614
  108.1 5.1 %all-to-all-done.1 = bf16[32,64,128]{2,1,0:T(8,128)(2,1)S(1)} async-done(((bf16[32,64,128]{2,1,0:T(8,128)(2,1)}), bf16[32,64,128]{2,1,0:T(8,128)(2,1)S(1)}, u32[]{:S(2)}, u32[]{:S(2)}) %all-to-all-start.1) | async-done | bytes 524320 | tf_op jit(solution)/shard_map/all_to_all | solution.py:675
  113.2 5.0 %mixer.1 = (f32[16,128,128]{2,1,0:T(8,128)}, bf16[128,2048]{1,0:T(8,128)(2,1)}, bf16[512,2048]{1,0:T(8,128)(2,1)}) custom-call(bf16[2,2,8,64,128]{4,3,2,1,0:T(8,128)(2,1)S(1)} %bitcast.22, f32[1,2048]{1,0:T(1,128)S(1)} %bitcast.23, bf16[512,128]{1,0:T(8,128)(2,1)} %get-tuple-element.44.select_hbm, f32[16,128,128]{2,1,0:T(8,128)} %get-tuple-element.45.own_hbm, ...), custom_call_target="tpu_custom_call" | custom-call | tf_op jit(solution)/shard_map/mixer/pallas_call | solution.py:500
  118.2 3.6 %all-to-all-start.2 = ((bf16[8,64,2048]{2,1,0:T(8,128)(2,1)}), bf16[8,64,2048]{2,1,0:T(8,128)(2,1)S(1)}, u32[]{:S(2)}, u32[]{:S(2)}) async-start(bf16[8,64,2048]{2,1,0:T(8,128)(2,1)} %bitcast.25), calls=%async_computation.2 | async-start | bytes 4194304 | tf_op jit(solution)/shard_map/all_to_all | solution.py:700
  124.2 26.9 %collective-permute-done.8.refs_2_ = bf16[512,512]{1,0:T(8,128)(2,1)} collective-permute-done((bf16[512,512]{1,0:T(8,128)(2,1)}, bf16[512,512]{1,0:T(8,128)(2,1)}, u32[]{:S(2)}, u32[]{:S(2)}) %collective-permute-start.8) | collective-permute-done | bytes 524320 | tf_op jit(solution)/shard_map/ppermute | solution.py:607
  153.5 4.6 %expert_in.1.activated_ref = bf16[512,512]{1,0:T(8,128)(2,1)S(1)} custom-call(s32[4]{0:T(128)S(1)} %pad_add_fusion.order_ref, bf16[512,2048]{1,0:T(8,128)(2,1)S(1)} %bitcast.20, bf16[512,1024]{1,0:T(8,128)(2,1)} %copy-done.5, bf16[512,1024]{1,0:T(8,128)(2,1)} %copy-done.6, bf16[512,1024]{1,0:T(8,128)(2,1)} %copy-done.7, ...), custom_call_target="tpu_custom_call" | custom-call | tf_op jit(solution)/shard_map/expert_in/pallas_call | solution.py:558
  158.1 2.5 %collective-permute-done.9.refs_3_ = bf16[512,512]{1,0:T(8,128)(2,1)} collective-permute-done((bf16[512,512]{1,0:T(8,128)(2,1)}, bf16[512,512]{1,0:T(8,128)(2,1)}, u32[]{:S(2)}, u32[]{:S(2)}) %collective-permute-start.9) | collective-permute-done | bytes 524320 | tf_op jit(solution)/shard_map/ppermute | solution.py:614
  160.6 3.4 %expert_out.1 = bf16[512,2048]{1,0:T(8,128)(2,1)S(1)} custom-call(s32[4]{0:T(128)S(1)} %pad_add_fusion.order_ref, bf16[512,512]{1,0:T(8,128)(2,1)S(1)} %expert_in.1.activated_ref, bf16[512,512]{1,0:T(8,128)(2,1)} %collective-permute-done.3.refs_0_, bf16[512,512]{1,0:T(8,128)(2,1)} %copy-done.8, bf16[512,512]{1,0:T(8,128)(2,1)} %collective-permute-done.8.refs_2_, ...), custom_call_target="tpu_custom_call" | custom-call | tf_op jit(solution)/shard_map/expert_out/pallas_call | solution.py:558
  164.0 30.5 %all_to_all.32 = bf16[8,64,2048]{2,1,0:T(8,128)(2,1)S(1)} all-to-all(bf16[8,64,2048]{2,1,0:T(8,128)(2,1)S(1)} %bitcast.19), channel_id=1, replica_groups=mesh['y'=2,'core'=2,'half'=2,'rest'=4] {'core','rest'}, dimensions={0} | all-to-all | bytes 4194304 | tf_op jit(solution)/shard_map/all_to_all | solution.py:702
  194.6 2.1 %combine.1 = bf16[128,2048]{1,0:T(8,128)(2,1)} custom-call(bf16[128,512]{1,0:T(8,128)(2,1)S(1)} %copy-done.1, bf16[128,512]{1,0:T(8,128)(2,1)S(1)} %copy-done.2, f32[16,128,128]{2,1,0:T(8,128)S(1)} %copy-done, bf16[512,2048]{1,0:T(8,128)(2,1)S(1)} %bitcast.21), custom_call_target="tpu_custom_call" | custom-call | tf_op jit(solution)/shard_map/combine/pallas_call | solution.py:591
  (31 shorter events, 8.3 us)
Async XLA Ops:
  1.5 6.7 %collective-permute-start = (bf16[8,4096]{1,0:T(8,128)(2,1)S(1)}, bf16[8,4096]{1,0:T(8,128)(2,1)S(1)}, u32[]{:S(2)}, u32[]{:S(2)}) collective-permute-start(bf16[8,4096]{1,0:T(8,128)(2,1)S(1)} %slice.3), channel_id=1, source_target_pairs={{0,1},{1,2},{2,3},{3,4},{4,5},{5,6},{6,7},{7,8},{8,9},{9,10},{10,1... | collective-permute-start | bytes 196616 | tf_op jit(solution)/shard_map/ppermute | solution.py:647
  8.2 24.5 %collective-permute-start.1 = (bf16[512,1024]{1,0:T(8,128)(2,1)}, bf16[512,1024]{1,0:T(8,128)(2,1)S(1)}, u32[]{:S(2)}, u32[]{:S(2)}) collective-permute-start(bf16[512,1024]{1,0:T(8,128)(2,1)} %bitcast.32), channel_id=1, source_target_pairs={{0,0},{4,8},{8,4},{12,12},{1,1},{5,9},{9,5},{13,13},{2,2},{6,10},{... | collective-permute-start | bytes 3145736 | tf_op jit(solution)/shard_map/ppermute | solution.py:607
  10.1 31.7 %copy-start.4 = (f32[128]{0:T(128)S(1)}, f32[128]{0:T(128)}, u32[]{:S(2)}) copy-start(f32[128]{0:T(128)} %param.18) | copy-start | bytes 1540
  24.3 37.6 %all-to-all-start = ((bf16[16,272,128]{2,1,0:T(8,128)(2,1)}), bf16[16,272,128]{2,1,0:T(8,128)(2,1)S(1)}, u32[]{:S(2)}, u32[]{:S(2)}) async-start(bf16[16,272,128]{2,1,0:T(8,128)(2,1)} %bitcast.26), calls=%async_computation | async-start | bytes 2228224 | tf_op jit(solution)/shard_map/all_to_all | solution.py:655
  32.8 15.4 %copy-start.5 = (bf16[512,1024]{1,0:T(8,128)(2,1)}, bf16[512,1024]{1,0:T(8,128)(2,1)S(1)}, u32[]{:S(2)}) copy-start(bf16[512,1024]{1,0:T(8,128)(2,1)S(1)} %collective-permute-done.1.refs_0_) | copy-start | bytes 3145732
  32.8 29.1 %collective-permute-start.2 = (bf16[512,1024]{1,0:T(8,128)(2,1)S(1)}, bf16[512,1024]{1,0:T(8,128)(2,1)S(1)}, u32[]{:S(2)}, u32[]{:S(2)}) collective-permute-start(bf16[512,1024]{1,0:T(8,128)(2,1)S(1)} %collective-permute-done.1.refs_0_), channel_id=1, source_target_pairs={{0,16},{16,0},{1,17},{17,1},{2,18},{18,2},{3,19},{19,3},{4,20},{20... | collective-permute-start | bytes 3145736 | tf_op jit(solution)/shard_map/ppermute | solution.py:614
  34.8 13.4 %collective-permute-start.3 = (bf16[512,512]{1,0:T(8,128)(2,1)}, bf16[512,512]{1,0:T(8,128)(2,1)}, u32[]{:S(2)}, u32[]{:S(2)}) collective-permute-start(bf16[512,512]{1,0:T(8,128)(2,1)} %bitcast.34), channel_id=1, source_target_pairs={{0,0},{4,8},{8,4},{12,12},{1,1},{5,9},{9,5},{13,13},{2,2},{6,10},{... | collective-permute-start | bytes 1572872 | tf_op jit(solution)/shard_map/ppermute | solution.py:607
  48.1 65.0 %copy-start.3 = (f32[2048]{0:T(1024)S(1)}, f32[2048]{0:T(1024)}, u32[]{:S(2)}) copy-start(f32[2048]{0:T(1024)} %param.19) | copy-start | bytes 24580
  61.9 1.0 copy-start.6
  62.8 15.3 %collective-permute-start.4 = (bf16[16,272,128]{2,1,0:T(8,128)(2,1)S(1)}, bf16[16,272,128]{2,1,0:T(8,128)(2,1)S(1)}, u32[]{:S(2)}, u32[]{:S(2)}) collective-permute-start(bf16[16,272,128]{2,1,0:T(8,128)(2,1)S(1)} %all-to-all-done.near_ref), channel_id=1, source_target_pairs={{0,8},{8,0},{1,9},{9,1},{2,10},{10,2},{3,11},{11,3},{4,12},{12,4},... | collective-permute-start | bytes 3342344 | tf_op jit(solution)/shard_map/ppermute | solution.py:672
  75.7 32.3 %collective-permute-start.5 = (bf16[512,1024]{1,0:T(8,128)(2,1)}, bf16[512,1024]{1,0:T(8,128)(2,1)S(1)}, u32[]{:S(2)}, u32[]{:S(2)}) collective-permute-start(bf16[512,1024]{1,0:T(8,128)(2,1)} %bitcast.33), channel_id=1, source_target_pairs={{0,4},{4,12},{8,0},{12,8},{1,5},{5,13},{9,1},{13,9},{2,6},{6,14},{... | collective-permute-start | bytes 3145736 | tf_op jit(solution)/shard_map/ppermute | solution.py:607
  83.2 30.0 %all-to-all-start.1 = ((bf16[32,64,128]{2,1,0:T(8,128)(2,1)}), bf16[32,64,128]{2,1,0:T(8,128)(2,1)S(1)}, u32[]{:S(2)}, u32[]{:S(2)}) async-start(bf16[32,64,128]{2,1,0:T(8,128)(2,1)} %scan_states.1), calls=%async_computation.1 | async-start | bytes 1048576 | tf_op jit(solution)/shard_map/all_to_all | solution.py:675
  89.0 19.1 %collective-permute-start.6 = (bf16[512,512]{1,0:T(8,128)(2,1)}, bf16[512,512]{1,0:T(8,128)(2,1)S(1)}, u32[]{:S(2)}, u32[]{:S(2)}) collective-permute-start(bf16[512,512]{1,0:T(8,128)(2,1)} %collective-permute-done.3.refs_0_), channel_id=1, source_target_pairs={{0,16},{16,0},{1,17},{17,1},{2,18},{18,2},{3,19},{19,3},{4,20},{20... | collective-permute-start | bytes 1572872 | tf_op jit(solution)/shard_map/ppermute | solution.py:614
  108.1 10.1 %copy-start.8 = (bf16[512,512]{1,0:T(8,128)(2,1)}, bf16[512,512]{1,0:T(8,128)(2,1)S(1)}, u32[]{:S(2)}) copy-start(bf16[512,512]{1,0:T(8,128)(2,1)S(1)} %collective-permute-done.6.refs_1_) | copy-start | bytes 1572868
  108.1 13.8 %copy-start.7 = (bf16[512,1024]{1,0:T(8,128)(2,1)}, bf16[512,1024]{1,0:T(8,128)(2,1)S(1)}, u32[]{:S(2)}) copy-start(bf16[512,1024]{1,0:T(8,128)(2,1)S(1)} %collective-permute-done.5.refs_2_) | copy-start | bytes 3145732
  118.2 35.3 %all-to-all-start.2 = ((bf16[8,64,2048]{2,1,0:T(8,128)(2,1)}), bf16[8,64,2048]{2,1,0:T(8,128)(2,1)S(1)}, u32[]{:S(2)}, u32[]{:S(2)}) async-start(bf16[8,64,2048]{2,1,0:T(8,128)(2,1)} %bitcast.25), calls=%async_computation.2 | async-start | bytes 4194304 | tf_op jit(solution)/shard_map/all_to_all | solution.py:700
  121.8 30.1 %collective-permute-start.7 = (bf16[512,1024]{1,0:T(8,128)(2,1)S(1)}, bf16[512,1024]{1,0:T(8,128)(2,1)}, u32[]{:S(2)}, u32[]{:S(2)}) collective-permute-start(bf16[512,1024]{1,0:T(8,128)(2,1)S(1)} %collective-permute-done.5.refs_2_), channel_id=1, source_target_pairs={{0,16},{16,0},{1,17},{17,1},{2,18},{18,2},{3,19},{19,3},{4,20},{20... | collective-permute-start | bytes 3145736 | tf_op jit(solution)/shard_map/ppermute | solution.py:614
  122.6 28.5 %collective-permute-start.8 = (bf16[512,512]{1,0:T(8,128)(2,1)}, bf16[512,512]{1,0:T(8,128)(2,1)}, u32[]{:S(2)}, u32[]{:S(2)}) collective-permute-start(bf16[512,512]{1,0:T(8,128)(2,1)} %bitcast.35), channel_id=1, source_target_pairs={{0,4},{4,12},{8,0},{12,8},{1,5},{5,13},{9,1},{13,9},{2,6},{6,14},{... | collective-permute-start | bytes 1572872 | tf_op jit(solution)/shard_map/ppermute | solution.py:607
  151.1 9.5 %collective-permute-start.9 = (bf16[512,512]{1,0:T(8,128)(2,1)}, bf16[512,512]{1,0:T(8,128)(2,1)}, u32[]{:S(2)}, u32[]{:S(2)}) collective-permute-start(bf16[512,512]{1,0:T(8,128)(2,1)} %collective-permute-done.8.refs_2_), channel_id=1, source_target_pairs={{0,16},{16,0},{1,17},{17,1},{2,18},{18,2},{3,19},{19,3},{4,20},{20... | collective-permute-start | bytes 1572872 | tf_op jit(solution)/shard_map/ppermute | solution.py:614
  164.0 30.6 %copy-start = (f32[16,128,128]{2,1,0:T(8,128)S(1)}, f32[16,128,128]{2,1,0:T(8,128)}, u32[]{:S(2)}) copy-start(f32[16,128,128]{2,1,0:T(8,128)} %get-tuple-element.51.middle_ref) | copy-start | bytes 3145732
  164.0 30.6 %copy-start.1 = (bf16[128,512]{1,0:T(8,128)(2,1)S(1)}, bf16[128,512]{1,0:T(8,128)(2,1)}, u32[]{:S(2)}) copy-start(bf16[128,512]{1,0:T(8,128)(2,1)} %get-tuple-element.49.high_ref) | copy-start | bytes 393220
  164.0 30.6 %copy-start.2 = (bf16[128,512]{1,0:T(8,128)(2,1)S(1)}, bf16[128,512]{1,0:T(8,128)(2,1)}, u32[]{:S(2)}) copy-start(bf16[128,512]{1,0:T(8,128)(2,1)} %get-tuple-element.50.low_ref) | copy-start | bytes 393220

commit v4 on v3

--- a/solution.py
+++ b/solution.py
@@ -18,7 +18,7 @@
 TOK_DEV = 128
 GROUP = VALUE_HEAD_SET // HK
 HALO = 8
-STEP_KEYS = 2
+STEP_KEYS = 4
 READER_KEYS = 2
 FADE_ROWS = 16
 
@@ -644,10 +644,9 @@
     beta, log_decay = (value.reshape(HK, GROUP, rows) for value in (beta, log_decay))
     tie = lax.optimization_barrier
 
-    halo = lax.ppermute(
-        mixed_qkv[rows - HALO :], every, [(source, source + 1) for source in range(count - 1)]
-    )
-    in_first = across_halves(after(w_in[0], halo), 0)
+    rim = mixed_qkv[rows - HALO :]
+    halo = lax.ppermute(rim, every, [(source, source + 1) for source in range(count - 1)])
+    in_first = across_halves(after(w_in[0], rim), 0)
     send, hats, fresh = local_terms(
         mixed_qkv, halo, conv_weight, beta, log_decay, splits, part, part_rows
     )

time: 198 us -> 193 us (0.975)
  waiting for transfers between devices: 71.4 us -> 76.7 us
  Pallas kernels: 42.4 us -> 37.6 us
  starting transfers between devices: 49.7 us -> 47.2 us
    ppermute x4, waiting for transfers between devices: 19.8 us -> 27.9 us  [along_y(): moved.append(lax.ppermute(value, 'y', pairs))]
    pallas_call x1, Pallas kernels: 14.2 us -> 9.41 us  [local_terms(): pl.pallas_call(functools.partial(local_kernel, splits, part, part_rows),...]
    all_to_all x1, waiting for transfers between devices: 13.7 us -> 10.3 us  [shards(): lax.all_to_all(send.reshape(chips, -1, DK), ('y', 'half', 'rest'), split_...]
    all_to_all x1, waiting for transfers between devices: 5.11 us -> 7.54 us  [shards(): lax.all_to_all(starts, every, split_axis=0, concat_axis=0, tiled=True)]
    all_to_all x1, starting transfers between devices: 5.75 us -> 3.53 us  [shards(): lax.all_to_all(starts, every, split_axis=0, concat_axis=0, tiled=True)]
  transfers between devices with their start and end apart: 13 -> 13, of which waited for: 8 -> 8; matrix products, arithmetic and copies ran while one was open for 0% -> 0% of each run, Pallas kernels for 16% -> 14%
where the time goes in v4:
time: 193 us; the launch traced here: 192 us
  waiting for transfers between devices  76.7 us (40%)
  starting transfers between devices  47.2 us (24%)
  Pallas kernels  37.6 us (19%)
  blocking collectives  29.1 us (15%)
    all_to_all x1, blocking collectives, shards(): return (mixer_out, combine(*gather, middle, exchange(expert_rows)))  29.1 us
    ppermute x4, waiting for transfers between devices, along_y(): moved.append(lax.ppermute(value, 'y', pairs))  27.9 us
    ppermute x4, waiting for transfers between devices, across_halves(): return lax.ppermute(value, ('core', 'half'), pairs)  27.1 us
    ppermute x1, starting transfers between devices, shards(): far = lax.ppermute(near, 'core', [(0, 1), (1, 0)])  13.4 us
    all_to_all x1, waiting for transfers between devices, shards(): lax.all_to_all(send.reshape(chips, -1, DK), ('y', 'half', 'rest'), split_...  10.3 us
    pallas_call x1, Pallas kernels, local_terms(): pl.pallas_call(functools.partial(local_kernel, splits, part, part_rows),...  9.41 us
    ppermute x4, starting transfers between devices, across_halves(): return lax.ppermute(value, ('core', 'half'), pairs)  8.42 us
    pallas_call x2, Pallas kernels, expert_call(): pl.pallas_call(kernel, in_specs=[pl.BlockSpec(memory_space=pltpu.SMEM), l...  7.94 us
  transfers between devices with their start and end apart: 13, of which 8 were waited for; matrix products, arithmetic and copies ran while one was open for 0% of the time, Pallas kernels for 14%

profile of v4, /device:TPU:0, one launch (start us, length us, event | category | flops | bytes accessed | tf_op | source)
XLA Modules:
  0.0 192.3 jit_solution(5678839634062997273)
XLA Ops:
  1.5 4.8 %collective-permute-start = (bf16[8,4096]{1,0:T(8,128)(2,1)S(1)}, bf16[8,4096]{1,0:T(8,128)(2,1)S(1)}, u32[]{:S(2)}, u32[]{:S(2)}) collective-permute-start(bf16[8,4096]{1,0:T(8,128)(2,1)S(1)} %slice.3), channel_id=1, source_target_pairs={{0,1},{1,2},{2,3},{3,4},{4,5},{5,6},{6,7},{7,8},{8,9},{9,10},{10,1... | collective-permute-start | bytes 196616 | tf_op jit(solution)/shard_map/ppermute | solution.py:648
  6.3 1.9 collective-permute-start.1
  8.2 9.4 %local_terms.1 = (bf16[16,1,272,128]{3,2,1,0:T(8,128)(2,1)}, f32[8,128,128]{2,1,0:T(8,128)}, f32[16,128,256]{2,1,0:T(8,128)}) custom-call(bf16[128,4096]{1,0:T(8,128)(2,1)} %q_ref.1, bf16[128,4096]{1,0:T(8,128)(2,1)} %q_ref.1, bf16[8,4096]{1,0:T(8,128)(2,1)S(1)} %collective-permute-done.kh_ref.vh_ref.qh_ref, ...), custom_call_target="tpu_custom_call" | custom-call | tf_op jit(solution)/shard_map/local_terms/pallas_call | solution.py:221
  17.6 7.7 %all-to-all-start = ((bf16[16,272,128]{2,1,0:T(8,128)(2,1)}), bf16[16,272,128]{2,1,0:T(8,128)(2,1)S(1)}, u32[]{:S(2)}, u32[]{:S(2)}) async-start(bf16[16,272,128]{2,1,0:T(8,128)(2,1)} %bitcast.26), calls=%async_computation | async-start | bytes 2228224 | tf_op jit(solution)/shard_map/all_to_all | solution.py:654
  25.4 2.0 %collective-permute-start.2 = (bf16[512,1024]{1,0:T(8,128)(2,1)S(1)}, bf16[512,1024]{1,0:T(8,128)(2,1)S(1)}, u32[]{:S(2)}, u32[]{:S(2)}) collective-permute-start(bf16[512,1024]{1,0:T(8,128)(2,1)S(1)} %collective-permute-done.1.refs_0_), channel_id=1, source_target_pairs={{0,16},{16,0},{1,17},{17,1},{2,18},{18,2},{3,19},{19,3},{4,20},{20... | collective-permute-start | bytes 3145736 | tf_op jit(solution)/shard_map/ppermute | solution.py:614
  27.4 5.4 %collective-permute-start.3 = (bf16[512,512]{1,0:T(8,128)(2,1)}, bf16[512,512]{1,0:T(8,128)(2,1)}, u32[]{:S(2)}, u32[]{:S(2)}) collective-permute-start(bf16[512,512]{1,0:T(8,128)(2,1)} %bitcast.34), channel_id=1, source_target_pairs={{0,0},{4,8},{8,4},{12,12},{1,1},{5,9},{9,5},{13,13},{2,2},{6,10},{... | collective-permute-start | bytes 1572872 | tf_op jit(solution)/shard_map/ppermute | solution.py:607
  34.4 6.3 %reader_terms.1 = (f32[16,128,128]{2,1,0:T(8,128)}, f32[16,128,128]{2,1,0:T(8,128)}, f32[16,128,128]{2,1,0:T(8,128)}) custom-call(bf16[128,4096]{1,0:T(8,128)(2,1)} %q_ref.1, bf16[8,4096]{1,0:T(8,128)(2,1)S(1)} %collective-permute-done.kh_ref.vh_ref.qh_ref, f32[4,4096]{1,0:T(4,128)} %qw_ref.1, f32[8,128,128]{2,1,0:T(8,128)} %get-tuple-element.36.hat_ref, ...), custom_call_target="tpu_custom_call" | custom-call | tf_op jit(solution)/shard_map/reader_terms/pallas_call | solution.py:283
  40.8 8.1 %collective-permute-done.2.refs_1_ = bf16[512,1024]{1,0:T(8,128)(2,1)S(1)} collective-permute-done((bf16[512,1024]{1,0:T(8,128)(2,1)S(1)}, bf16[512,1024]{1,0:T(8,128)(2,1)S(1)}, u32[]{:S(2)}, u32[]{:S(2)}) %collective-permute-start.2) | collective-permute-done | bytes 1048608 | tf_op jit(solution)/shard_map/ppermute | solution.py:614
  48.9 10.3 %all-to-all-done.near_ref = bf16[16,272,128]{2,1,0:T(8,128)(2,1)S(1)} async-done(((bf16[16,272,128]{2,1,0:T(8,128)(2,1)}), bf16[16,272,128]{2,1,0:T(8,128)(2,1)S(1)}, u32[]{:S(2)}, u32[]{:S(2)}) %all-to-all-start) | async-done | bytes 1114144 | tf_op jit(solution)/shard_map/all_to_all | solution.py:654
  59.2 13.4 %collective-permute-start.4 = (bf16[16,272,128]{2,1,0:T(8,128)(2,1)S(1)}, bf16[16,272,128]{2,1,0:T(8,128)(2,1)S(1)}, u32[]{:S(2)}, u32[]{:S(2)}) collective-permute-start(bf16[16,272,128]{2,1,0:T(8,128)(2,1)S(1)} %all-to-all-done.near_ref), channel_id=1, source_target_pairs={{0,8},{8,0},{1,9},{9,1},{2,10},{10,2},{3,11},{11,3},{4,12},{12,4},... | collective-permute-start | bytes 3342344 | tf_op jit(solution)/shard_map/ppermute | solution.py:671
  72.6 2.4 %collective-permute-done.4.far_ref = bf16[16,272,128]{2,1,0:T(8,128)(2,1)S(1)} collective-permute-done((bf16[16,272,128]{2,1,0:T(8,128)(2,1)S(1)}, bf16[16,272,128]{2,1,0:T(8,128)(2,1)S(1)}, u32[]{:S(2)}, u32[]{:S(2)}) %collective-permute-start.4) | collective-permute-done | bytes 1114144 | tf_op jit(solution)/shard_map/ppermute | solution.py:671
  75.0 5.1 %scan_states.1 = bf16[32,64,128]{2,1,0:T(8,128)(2,1)} custom-call(s32[1]{0:T(128)} %bitcast.core_ref, bf16[16,272,128]{2,1,0:T(8,128)(2,1)S(1)} %all-to-all-done.near_ref, bf16[16,272,128]{2,1,0:T(8,128)(2,1)S(1)} %collective-permute-done.4.far_ref), custom_call_target="tpu_custom_call" | custom-call | tf_op jit(solution)/shard_map/scan_states/pallas_call | solution.py:338
  80.1 3.5 %all-to-all-start.1 = ((bf16[32,64,128]{2,1,0:T(8,128)(2,1)}), bf16[32,64,128]{2,1,0:T(8,128)(2,1)S(1)}, u32[]{:S(2)}, u32[]{:S(2)}) async-start(bf16[32,64,128]{2,1,0:T(8,128)(2,1)} %scan_states.1), calls=%async_computation.1 | async-start | bytes 1048576 | tf_op jit(solution)/shard_map/all_to_all | solution.py:674
  83.6 1.8 collective-permute-start.6
  85.5 17.3 %collective-permute-done.6.refs_1_ = bf16[512,512]{1,0:T(8,128)(2,1)S(1)} collective-permute-done((bf16[512,512]{1,0:T(8,128)(2,1)}, bf16[512,512]{1,0:T(8,128)(2,1)S(1)}, u32[]{:S(2)}, u32[]{:S(2)}) %collective-permute-start.6) | collective-permute-done | bytes 524320 | tf_op jit(solution)/shard_map/ppermute | solution.py:614
  102.7 7.5 %all-to-all-done.1 = bf16[32,64,128]{2,1,0:T(8,128)(2,1)S(1)} async-done(((bf16[32,64,128]{2,1,0:T(8,128)(2,1)}), bf16[32,64,128]{2,1,0:T(8,128)(2,1)S(1)}, u32[]{:S(2)}, u32[]{:S(2)}) %all-to-all-start.1) | async-done | bytes 524320 | tf_op jit(solution)/shard_map/all_to_all | solution.py:674
  110.3 5.0 %mixer.1 = (f32[16,128,128]{2,1,0:T(8,128)}, bf16[128,2048]{1,0:T(8,128)(2,1)}, bf16[512,2048]{1,0:T(8,128)(2,1)}) custom-call(bf16[2,2,8,64,128]{4,3,2,1,0:T(8,128)(2,1)S(1)} %bitcast.22, f32[1,2048]{1,0:T(1,128)S(1)} %bitcast.23, bf16[512,128]{1,0:T(8,128)(2,1)} %get-tuple-element.44.select_hbm, f32[16,128,128]{2,1,0:T(8,128)} %get-tuple-element.45.own_hbm, ...), custom_call_target="tpu_custom_call" | custom-call | tf_op jit(solution)/shard_map/mixer/pallas_call | solution.py:500
  115.3 3.6 %all-to-all-start.2 = ((bf16[8,64,2048]{2,1,0:T(8,128)(2,1)}), bf16[8,64,2048]{2,1,0:T(8,128)(2,1)S(1)}, u32[]{:S(2)}, u32[]{:S(2)}) async-start(bf16[8,64,2048]{2,1,0:T(8,128)(2,1)} %bitcast.25), calls=%async_computation.2 | async-start | bytes 4194304 | tf_op jit(solution)/shard_map/all_to_all | solution.py:699
  121.1 27.1 %collective-permute-done.8.refs_2_ = bf16[512,512]{1,0:T(8,128)(2,1)} collective-permute-done((bf16[512,512]{1,0:T(8,128)(2,1)}, bf16[512,512]{1,0:T(8,128)(2,1)}, u32[]{:S(2)}, u32[]{:S(2)}) %collective-permute-start.8) | collective-permute-done | bytes 524320 | tf_op jit(solution)/shard_map/ppermute | solution.py:607
  150.6 4.6 %expert_in.1.activated_ref = bf16[512,512]{1,0:T(8,128)(2,1)S(1)} custom-call(s32[4]{0:T(128)S(1)} %pad_add_fusion.order_ref, bf16[512,2048]{1,0:T(8,128)(2,1)S(1)} %bitcast.20, bf16[512,1024]{1,0:T(8,128)(2,1)} %copy-done.5, bf16[512,1024]{1,0:T(8,128)(2,1)} %copy-done.6, bf16[512,1024]{1,0:T(8,128)(2,1)} %copy-done.7, ...), custom_call_target="tpu_custom_call" | custom-call | tf_op jit(solution)/shard_map/expert_in/pallas_call | solution.py:558
  155.2 2.5 %collective-permute-done.9.refs_3_ = bf16[512,512]{1,0:T(8,128)(2,1)} collective-permute-done((bf16[512,512]{1,0:T(8,128)(2,1)}, bf16[512,512]{1,0:T(8,128)(2,1)}, u32[]{:S(2)}, u32[]{:S(2)}) %collective-permute-start.9) | collective-permute-done | bytes 524320 | tf_op jit(solution)/shard_map/ppermute | solution.py:614
  157.7 3.4 %expert_out.1 = bf16[512,2048]{1,0:T(8,128)(2,1)S(1)} custom-call(s32[4]{0:T(128)S(1)} %pad_add_fusion.order_ref, bf16[512,512]{1,0:T(8,128)(2,1)S(1)} %expert_in.1.activated_ref, bf16[512,512]{1,0:T(8,128)(2,1)} %collective-permute-done.3.refs_0_, bf16[512,512]{1,0:T(8,128)(2,1)} %copy-done.8, bf16[512,512]{1,0:T(8,128)(2,1)} %collective-permute-done.8.refs_2_, ...), custom_call_target="tpu_custom_call" | custom-call | tf_op jit(solution)/shard_map/expert_out/pallas_call | solution.py:558
  161.1 29.1 %all_to_all.32 = bf16[8,64,2048]{2,1,0:T(8,128)(2,1)S(1)} all-to-all(bf16[8,64,2048]{2,1,0:T(8,128)(2,1)S(1)} %bitcast.19), channel_id=1, replica_groups=mesh['y'=2,'core'=2,'half'=2,'rest'=4] {'core','rest'}, dimensions={0} | all-to-all | bytes 4194304 | tf_op jit(solution)/shard_map/all_to_all | solution.py:701
  190.2 2.1 %combine.1 = bf16[128,2048]{1,0:T(8,128)(2,1)} custom-call(bf16[128,512]{1,0:T(8,128)(2,1)S(1)} %copy-done.1, bf16[128,512]{1,0:T(8,128)(2,1)S(1)} %copy-done.2, f32[16,128,128]{2,1,0:T(8,128)S(1)} %copy-done, bf16[512,2048]{1,0:T(8,128)(2,1)S(1)} %bitcast.21), custom_call_target="tpu_custom_call" | custom-call | tf_op jit(solution)/shard_map/combine/pallas_call | solution.py:591
  (31 shorter events, 7.1 us)
Async XLA Ops:
  1.5 6.7 %collective-permute-start = (bf16[8,4096]{1,0:T(8,128)(2,1)S(1)}, bf16[8,4096]{1,0:T(8,128)(2,1)S(1)}, u32[]{:S(2)}, u32[]{:S(2)}) collective-permute-start(bf16[8,4096]{1,0:T(8,128)(2,1)S(1)} %slice.3), channel_id=1, source_target_pairs={{0,1},{1,2},{2,3},{3,4},{4,5},{5,6},{6,7},{7,8},{8,9},{9,10},{10,1... | collective-permute-start | bytes 196616 | tf_op jit(solution)/shard_map/ppermute | solution.py:648
  6.3 19.0 %collective-permute-start.1 = (bf16[512,1024]{1,0:T(8,128)(2,1)}, bf16[512,1024]{1,0:T(8,128)(2,1)S(1)}, u32[]{:S(2)}, u32[]{:S(2)}) collective-permute-start(bf16[512,1024]{1,0:T(8,128)(2,1)} %bitcast.32), channel_id=1, source_target_pairs={{0,0},{4,8},{8,4},{12,12},{1,1},{5,9},{9,5},{13,13},{2,2},{6,10},{... | collective-permute-start | bytes 3145736 | tf_op jit(solution)/shard_map/ppermute | solution.py:607
  8.2 26.2 %copy-start.4 = (f32[128]{0:T(128)S(1)}, f32[128]{0:T(128)}, u32[]{:S(2)}) copy-start(f32[128]{0:T(128)} %param.18) | copy-start | bytes 1540
  17.6 41.6 %all-to-all-start = ((bf16[16,272,128]{2,1,0:T(8,128)(2,1)}), bf16[16,272,128]{2,1,0:T(8,128)(2,1)S(1)}, u32[]{:S(2)}, u32[]{:S(2)}) async-start(bf16[16,272,128]{2,1,0:T(8,128)(2,1)} %bitcast.26), calls=%async_computation | async-start | bytes 2228224 | tf_op jit(solution)/shard_map/all_to_all | solution.py:654
  25.4 15.4 %copy-start.5 = (bf16[512,1024]{1,0:T(8,128)(2,1)}, bf16[512,1024]{1,0:T(8,128)(2,1)S(1)}, u32[]{:S(2)}) copy-start(bf16[512,1024]{1,0:T(8,128)(2,1)S(1)} %collective-permute-done.1.refs_0_) | copy-start | bytes 3145732
  25.4 23.6 %collective-permute-start.2 = (bf16[512,1024]{1,0:T(8,128)(2,1)S(1)}, bf16[512,1024]{1,0:T(8,128)(2,1)S(1)}, u32[]{:S(2)}, u32[]{:S(2)}) collective-permute-start(bf16[512,1024]{1,0:T(8,128)(2,1)S(1)} %collective-permute-done.1.refs_0_), channel_id=1, source_target_pairs={{0,16},{16,0},{1,17},{17,1},{2,18},{18,2},{3,19},{19,3},{4,20},{20... | collective-permute-start | bytes 3145736 | tf_op jit(solution)/shard_map/ppermute | solution.py:614
  27.4 13.4 %collective-permute-start.3 = (bf16[512,512]{1,0:T(8,128)(2,1)}, bf16[512,512]{1,0:T(8,128)(2,1)}, u32[]{:S(2)}, u32[]{:S(2)}) collective-permute-start(bf16[512,512]{1,0:T(8,128)(2,1)} %bitcast.34), channel_id=1, source_target_pairs={{0,0},{4,8},{8,4},{12,12},{1,1},{5,9},{9,5},{13,13},{2,2},{6,10},{... | collective-permute-start | bytes 1572872 | tf_op jit(solution)/shard_map/ppermute | solution.py:607
  40.8 69.5 %copy-start.3 = (f32[2048]{0:T(1024)S(1)}, f32[2048]{0:T(1024)}, u32[]{:S(2)}) copy-start(f32[2048]{0:T(1024)} %param.19) | copy-start | bytes 24580
  48.9 10.3 %copy-start.6 = (bf16[512,1024]{1,0:T(8,128)(2,1)}, bf16[512,1024]{1,0:T(8,128)(2,1)S(1)}, u32[]{:S(2)}) copy-start(bf16[512,1024]{1,0:T(8,128)(2,1)S(1)} %collective-permute-done.2.refs_1_) | copy-start | bytes 3145732
  59.2 15.8 %collective-permute-start.4 = (bf16[16,272,128]{2,1,0:T(8,128)(2,1)S(1)}, bf16[16,272,128]{2,1,0:T(8,128)(2,1)S(1)}, u32[]{:S(2)}, u32[]{:S(2)}) collective-permute-start(bf16[16,272,128]{2,1,0:T(8,128)(2,1)S(1)} %all-to-all-done.near_ref), channel_id=1, source_target_pairs={{0,8},{8,0},{1,9},{9,1},{2,10},{10,2},{3,11},{11,3},{4,12},{12,4},... | collective-permute-start | bytes 3342344 | tf_op jit(solution)/shard_map/ppermute | solution.py:671
  72.6 30.1 %collective-permute-start.5 = (bf16[512,1024]{1,0:T(8,128)(2,1)}, bf16[512,1024]{1,0:T(8,128)(2,1)S(1)}, u32[]{:S(2)}, u32[]{:S(2)}) collective-permute-start(bf16[512,1024]{1,0:T(8,128)(2,1)} %bitcast.33), channel_id=1, source_target_pairs={{0,4},{4,12},{8,0},{12,8},{1,5},{5,13},{9,1},{13,9},{2,6},{6,14},{... | collective-permute-start | bytes 3145736 | tf_op jit(solution)/shard_map/ppermute | solution.py:607
  80.1 30.2 %all-to-all-start.1 = ((bf16[32,64,128]{2,1,0:T(8,128)(2,1)}), bf16[32,64,128]{2,1,0:T(8,128)(2,1)S(1)}, u32[]{:S(2)}, u32[]{:S(2)}) async-start(bf16[32,64,128]{2,1,0:T(8,128)(2,1)} %scan_states.1), calls=%async_computation.1 | async-start | bytes 1048576 | tf_op jit(solution)/shard_map/all_to_all | solution.py:674
  83.6 19.1 %collective-permute-start.6 = (bf16[512,512]{1,0:T(8,128)(2,1)}, bf16[512,512]{1,0:T(8,128)(2,1)S(1)}, u32[]{:S(2)}, u32[]{:S(2)}) collective-permute-start(bf16[512,512]{1,0:T(8,128)(2,1)} %collective-permute-done.3.refs_0_), channel_id=1, source_target_pairs={{0,16},{16,0},{1,17},{17,1},{2,18},{18,2},{3,19},{19,3},{4,20},{20... | collective-permute-start | bytes 1572872 | tf_op jit(solution)/shard_map/ppermute | solution.py:614
  102.7 12.6 %copy-start.8 = (bf16[512,512]{1,0:T(8,128)(2,1)}, bf16[512,512]{1,0:T(8,128)(2,1)S(1)}, u32[]{:S(2)}) copy-start(bf16[512,512]{1,0:T(8,128)(2,1)S(1)} %collective-permute-done.6.refs_1_) | copy-start | bytes 1572868
  102.7 16.2 %copy-start.7 = (bf16[512,1024]{1,0:T(8,128)(2,1)}, bf16[512,1024]{1,0:T(8,128)(2,1)S(1)}, u32[]{:S(2)}) copy-start(bf16[512,1024]{1,0:T(8,128)(2,1)S(1)} %collective-permute-done.5.refs_2_) | copy-start | bytes 3145732
  115.3 35.3 %all-to-all-start.2 = ((bf16[8,64,2048]{2,1,0:T(8,128)(2,1)}), bf16[8,64,2048]{2,1,0:T(8,128)(2,1)S(1)}, u32[]{:S(2)}, u32[]{:S(2)}) async-start(bf16[8,64,2048]{2,1,0:T(8,128)(2,1)} %bitcast.25), calls=%async_computation.2 | async-start | bytes 4194304 | tf_op jit(solution)/shard_map/all_to_all | solution.py:699
  118.9 30.2 %collective-permute-start.7 = (bf16[512,1024]{1,0:T(8,128)(2,1)S(1)}, bf16[512,1024]{1,0:T(8,128)(2,1)}, u32[]{:S(2)}, u32[]{:S(2)}) collective-permute-start(bf16[512,1024]{1,0:T(8,128)(2,1)S(1)} %collective-permute-done.5.refs_2_), channel_id=1, source_target_pairs={{0,16},{16,0},{1,17},{17,1},{2,18},{18,2},{3,19},{19,3},{4,20},{20... | collective-permute-start | bytes 3145736 | tf_op jit(solution)/shard_map/ppermute | solution.py:614
  119.9 28.3 %collective-permute-start.8 = (bf16[512,512]{1,0:T(8,128)(2,1)}, bf16[512,512]{1,0:T(8,128)(2,1)}, u32[]{:S(2)}, u32[]{:S(2)}) collective-permute-start(bf16[512,512]{1,0:T(8,128)(2,1)} %bitcast.35), channel_id=1, source_target_pairs={{0,4},{4,12},{8,0},{12,8},{1,5},{5,13},{9,1},{13,9},{2,6},{6,14},{... | collective-permute-start | bytes 1572872 | tf_op jit(solution)/shard_map/ppermute | solution.py:607
  148.2 9.5 %collective-permute-start.9 = (bf16[512,512]{1,0:T(8,128)(2,1)}, bf16[512,512]{1,0:T(8,128)(2,1)}, u32[]{:S(2)}, u32[]{:S(2)}) collective-permute-start(bf16[512,512]{1,0:T(8,128)(2,1)} %collective-permute-done.8.refs_2_), channel_id=1, source_target_pairs={{0,16},{16,0},{1,17},{17,1},{2,18},{18,2},{3,19},{19,3},{4,20},{20... | collective-permute-start | bytes 1572872 | tf_op jit(solution)/shard_map/ppermute | solution.py:614
  161.1 29.1 %copy-start = (f32[16,128,128]{2,1,0:T(8,128)S(1)}, f32[16,128,128]{2,1,0:T(8,128)}, u32[]{:S(2)}) copy-start(f32[16,128,128]{2,1,0:T(8,128)} %get-tuple-element.51.middle_ref) | copy-start | bytes 3145732
  161.1 29.1 %copy-start.1 = (bf16[128,512]{1,0:T(8,128)(2,1)S(1)}, bf16[128,512]{1,0:T(8,128)(2,1)}, u32[]{:S(2)}) copy-start(bf16[128,512]{1,0:T(8,128)(2,1)} %get-tuple-element.49.high_ref) | copy-start | bytes 393220
  161.1 29.1 %copy-start.2 = (bf16[128,512]{1,0:T(8,128)(2,1)S(1)}, bf16[128,512]{1,0:T(8,128)(2,1)}, u32[]{:S(2)}) copy-start(bf16[128,512]{1,0:T(8,128)(2,1)} %get-tuple-element.50.low_ref) | copy-start | bytes 393220

commit v5 on v4

--- a/solution.py
+++ b/solution.py
@@ -19,7 +19,7 @@
 GROUP = VALUE_HEAD_SET // HK
 HALO = 8
 STEP_KEYS = 4
-READER_KEYS = 2
+READER_KEYS = 4
 FADE_ROWS = 16
 
 f32 = jnp.float32
@@ -578,19 +578,37 @@
     return expert_call(expert_out_kernel, "expert_out", order, activated, parts, width)
 
 
-def combine_kernel(high_ref, low_ref, middle_ref, rows_ref, out_ref):
+def combine_kernel(high_ref, low_ref, middle_ref, rows_ref, out_hbm, out_ref, sems):
     high, low = high_ref[...], low_ref[...]
-    for head in range(middle_ref.shape[0]):
-        span = slice(head * DV, (head + 1) * DV)
-        rows = rows_ref[:, span]
-        out_ref[:, span] = (middle_ref[head] + (dot(high, rows) + dot(low, rows))).astype(bf16)
+    groups = sems.shape[0]
+    heads, stores = middle_ref.shape[0] // groups, []
+    for group in range(groups):
+        for head in range(group * heads, (group + 1) * heads):
+            span = slice(head * DV, (head + 1) * DV)
+            rows = rows_ref[:, span]
+            summed = dot(high, rows) + dot(low, rows)
+            out_ref[:, span] = (middle_ref[head] + summed).astype(bf16)
+        columns = pl.ds(group * heads * DV, heads * DV)
+        stores.append(
+            pltpu.make_async_copy(out_ref.at[:, columns], out_hbm.at[:, columns], sems.at[group])
+        )
+        stores[-1].start()
+    for store in stores:
+        store.wait()
 
 
 def combine(high, low, middle, rows):
     count, width = middle.shape[1], rows.shape[1]
+    groups = 4
     return pl.pallas_call(
         combine_kernel,
+        in_specs=[pl.BlockSpec(memory_space=pltpu.VMEM)] * 4,
+        out_specs=pl.BlockSpec(memory_space=pltpu.HBM),
         out_shape=pltpu.HBM((count, width), bf16),
+        scratch_shapes=[
+            pltpu.VMEM((count, width), bf16),
+            pltpu.SemaphoreType.DMA((groups,)),
+        ],
         compiler_params=pltpu.CompilerParams(vmem_limit_bytes=24 << 20),
         name="combine",
     )(high, low, middle, rows)

time: 193 us -> 193 us (level)
  no operation moved by 1% of the time
where the time goes in v5:
time: 193 us; the launch traced here: 192 us
  waiting for transfers between devices  77.2 us (40%)
  starting transfers between devices  47.2 us (24%)
  Pallas kernels  36.9 us (19%)
  blocking collectives  29.1 us (15%)
    all_to_all x1, blocking collectives, shards(): return (mixer_out, combine(*gather, middle, exchange(expert_rows)))  29.1 us
    ppermute x4, waiting for transfers between devices, along_y(): moved.append(lax.ppermute(value, 'y', pairs))  28.5 us
    ppermute x4, waiting for transfers between devices, across_halves(): return lax.ppermute(value, ('core', 'half'), pairs)  27.1 us
    ppermute x1, starting transfers between devices, shards(): far = lax.ppermute(near, 'core', [(0, 1), (1, 0)])  13.4 us
    all_to_all x1, waiting for transfers between devices, shards(): lax.all_to_all(send.reshape(chips, -1, DK), ('y', 'half', 'rest'), split_...  10.3 us
    pallas_call x1, Pallas kernels, local_terms(): pl.pallas_call(functools.partial(local_kernel, splits, part, part_rows),...  9.41 us
    ppermute x4, starting transfers between devices, across_halves(): return lax.ppermute(value, ('core', 'half'), pairs)  8.42 us
    pallas_call x2, Pallas kernels, expert_call(): pl.pallas_call(kernel, in_specs=[pl.BlockSpec(memory_space=pltpu.SMEM), l...  7.94 us
  transfers between devices with their start and end apart: 13, of which 8 were waited for; matrix products, arithmetic and copies ran while one was open for 0% of the time, Pallas kernels for 14%

profile of v5, /device:TPU:0, one launch (start us, length us, event | category | flops | bytes accessed | tf_op | source)
XLA Modules:
  0.0 192.2 jit_solution(10517170256489605766)
XLA Ops:
  1.5 4.8 %collective-permute-start = (bf16[8,4096]{1,0:T(8,128)(2,1)S(1)}, bf16[8,4096]{1,0:T(8,128)(2,1)S(1)}, u32[]{:S(2)}, u32[]{:S(2)}) collective-permute-start(bf16[8,4096]{1,0:T(8,128)(2,1)S(1)} %slice.3), channel_id=1, source_target_pairs={{0,1},{1,2},{2,3},{3,4},{4,5},{5,6},{6,7},{7,8},{8,9},{9,10},{10,1... | collective-permute-start | bytes 196616 | tf_op jit(solution)/shard_map/ppermute | solution.py:666
  6.3 1.9 collective-permute-start.1
  8.2 9.4 %local_terms.1 = (bf16[16,1,272,128]{3,2,1,0:T(8,128)(2,1)}, f32[8,128,128]{2,1,0:T(8,128)}, f32[16,128,256]{2,1,0:T(8,128)}) custom-call(bf16[128,4096]{1,0:T(8,128)(2,1)} %q_ref.1, bf16[128,4096]{1,0:T(8,128)(2,1)} %q_ref.1, bf16[8,4096]{1,0:T(8,128)(2,1)S(1)} %collective-permute-done.kh_ref.vh_ref.qh_ref, ...), custom_call_target="tpu_custom_call" | custom-call | tf_op jit(solution)/shard_map/local_terms/pallas_call | solution.py:221
  17.6 7.7 %all-to-all-start = ((bf16[16,272,128]{2,1,0:T(8,128)(2,1)}), bf16[16,272,128]{2,1,0:T(8,128)(2,1)S(1)}, u32[]{:S(2)}, u32[]{:S(2)}) async-start(bf16[16,272,128]{2,1,0:T(8,128)(2,1)} %bitcast.26), calls=%async_computation | async-start | bytes 2228224 | tf_op jit(solution)/shard_map/all_to_all | solution.py:672
  25.4 2.0 %collective-permute-start.2 = (bf16[512,1024]{1,0:T(8,128)(2,1)S(1)}, bf16[512,1024]{1,0:T(8,128)(2,1)S(1)}, u32[]{:S(2)}, u32[]{:S(2)}) collective-permute-start(bf16[512,1024]{1,0:T(8,128)(2,1)S(1)} %collective-permute-done.1.refs_0_), channel_id=1, source_target_pairs={{0,16},{16,0},{1,17},{17,1},{2,18},{18,2},{3,19},{19,3},{4,20},{20... | collective-permute-start | bytes 3145736 | tf_op jit(solution)/shard_map/ppermute | solution.py:632
  27.4 5.4 %collective-permute-start.3 = (bf16[512,512]{1,0:T(8,128)(2,1)}, bf16[512,512]{1,0:T(8,128)(2,1)}, u32[]{:S(2)}, u32[]{:S(2)}) collective-permute-start(bf16[512,512]{1,0:T(8,128)(2,1)} %bitcast.34), channel_id=1, source_target_pairs={{0,0},{4,8},{8,4},{12,12},{1,1},{5,9},{9,5},{13,13},{2,2},{6,10},{... | collective-permute-start | bytes 1572872 | tf_op jit(solution)/shard_map/ppermute | solution.py:625
  34.4 5.8 %reader_terms.1 = (f32[16,128,128]{2,1,0:T(8,128)}, f32[16,128,128]{2,1,0:T(8,128)}, f32[16,128,128]{2,1,0:T(8,128)}) custom-call(bf16[128,4096]{1,0:T(8,128)(2,1)} %q_ref.1, bf16[8,4096]{1,0:T(8,128)(2,1)S(1)} %collective-permute-done.kh_ref.vh_ref.qh_ref, f32[4,4096]{1,0:T(4,128)} %qw_ref.1, f32[8,128,128]{2,1,0:T(8,128)} %get-tuple-element.36.hat_ref, ...), custom_call_target="tpu_custom_call" | custom-call | tf_op jit(solution)/shard_map/reader_terms/pallas_call | solution.py:283
  40.3 8.7 %collective-permute-done.2.refs_1_ = bf16[512,1024]{1,0:T(8,128)(2,1)S(1)} collective-permute-done((bf16[512,1024]{1,0:T(8,128)(2,1)S(1)}, bf16[512,1024]{1,0:T(8,128)(2,1)S(1)}, u32[]{:S(2)}, u32[]{:S(2)}) %collective-permute-start.2) | collective-permute-done | bytes 1048608 | tf_op jit(solution)/shard_map/ppermute | solution.py:632
  48.9 10.3 %all-to-all-done.near_ref = bf16[16,272,128]{2,1,0:T(8,128)(2,1)S(1)} async-done(((bf16[16,272,128]{2,1,0:T(8,128)(2,1)}), bf16[16,272,128]{2,1,0:T(8,128)(2,1)S(1)}, u32[]{:S(2)}, u32[]{:S(2)}) %all-to-all-start) | async-done | bytes 1114144 | tf_op jit(solution)/shard_map/all_to_all | solution.py:672
  59.2 13.4 %collective-permute-start.4 = (bf16[16,272,128]{2,1,0:T(8,128)(2,1)S(1)}, bf16[16,272,128]{2,1,0:T(8,128)(2,1)S(1)}, u32[]{:S(2)}, u32[]{:S(2)}) collective-permute-start(bf16[16,272,128]{2,1,0:T(8,128)(2,1)S(1)} %all-to-all-done.near_ref), channel_id=1, source_target_pairs={{0,8},{8,0},{1,9},{9,1},{2,10},{10,2},{3,11},{11,3},{4,12},{12,4},... | collective-permute-start | bytes 3342344 | tf_op jit(solution)/shard_map/ppermute | solution.py:689
  72.6 2.4 %collective-permute-done.4.far_ref = bf16[16,272,128]{2,1,0:T(8,128)(2,1)S(1)} collective-permute-done((bf16[16,272,128]{2,1,0:T(8,128)(2,1)S(1)}, bf16[16,272,128]{2,1,0:T(8,128)(2,1)S(1)}, u32[]{:S(2)}, u32[]{:S(2)}) %collective-permute-start.4) | collective-permute-done | bytes 1114144 | tf_op jit(solution)/shard_map/ppermute | solution.py:689
  75.0 5.1 %scan_states.1 = bf16[32,64,128]{2,1,0:T(8,128)(2,1)} custom-call(s32[1]{0:T(128)} %bitcast.core_ref, bf16[16,272,128]{2,1,0:T(8,128)(2,1)S(1)} %all-to-all-done.near_ref, bf16[16,272,128]{2,1,0:T(8,128)(2,1)S(1)} %collective-permute-done.4.far_ref), custom_call_target="tpu_custom_call" | custom-call | tf_op jit(solution)/shard_map/scan_states/pallas_call | solution.py:338
  80.1 3.5 %all-to-all-start.1 = ((bf16[32,64,128]{2,1,0:T(8,128)(2,1)}), bf16[32,64,128]{2,1,0:T(8,128)(2,1)S(1)}, u32[]{:S(2)}, u32[]{:S(2)}) async-start(bf16[32,64,128]{2,1,0:T(8,128)(2,1)} %scan_states.1), calls=%async_computation.1 | async-start | bytes 1048576 | tf_op jit(solution)/shard_map/all_to_all | solution.py:692
  83.6 1.8 collective-permute-start.6
  85.5 17.3 %collective-permute-done.6.refs_1_ = bf16[512,512]{1,0:T(8,128)(2,1)S(1)} collective-permute-done((bf16[512,512]{1,0:T(8,128)(2,1)}, bf16[512,512]{1,0:T(8,128)(2,1)S(1)}, u32[]{:S(2)}, u32[]{:S(2)}) %collective-permute-start.6) | collective-permute-done | bytes 524320 | tf_op jit(solution)/shard_map/ppermute | solution.py:632
  102.7 7.5 %all-to-all-done.1 = bf16[32,64,128]{2,1,0:T(8,128)(2,1)S(1)} async-done(((bf16[32,64,128]{2,1,0:T(8,128)(2,1)}), bf16[32,64,128]{2,1,0:T(8,128)(2,1)S(1)}, u32[]{:S(2)}, u32[]{:S(2)}) %all-to-all-start.1) | async-done | bytes 524320 | tf_op jit(solution)/shard_map/all_to_all | solution.py:692
  110.3 5.0 %mixer.1 = (f32[16,128,128]{2,1,0:T(8,128)}, bf16[128,2048]{1,0:T(8,128)(2,1)}, bf16[512,2048]{1,0:T(8,128)(2,1)}) custom-call(bf16[2,2,8,64,128]{4,3,2,1,0:T(8,128)(2,1)S(1)} %bitcast.22, f32[1,2048]{1,0:T(1,128)S(1)} %bitcast.23, bf16[512,128]{1,0:T(8,128)(2,1)} %get-tuple-element.44.select_hbm, f32[16,128,128]{2,1,0:T(8,128)} %get-tuple-element.45.own_hbm, ...), custom_call_target="tpu_custom_call" | custom-call | tf_op jit(solution)/shard_map/mixer/pallas_call | solution.py:500
  115.3 3.6 %all-to-all-start.2 = ((bf16[8,64,2048]{2,1,0:T(8,128)(2,1)}), bf16[8,64,2048]{2,1,0:T(8,128)(2,1)S(1)}, u32[]{:S(2)}, u32[]{:S(2)}) async-start(bf16[8,64,2048]{2,1,0:T(8,128)(2,1)} %bitcast.25), calls=%async_computation.2 | async-start | bytes 4194304 | tf_op jit(solution)/shard_map/all_to_all | solution.py:717
  121.1 27.1 %collective-permute-done.8.refs_2_ = bf16[512,512]{1,0:T(8,128)(2,1)} collective-permute-done((bf16[512,512]{1,0:T(8,128)(2,1)}, bf16[512,512]{1,0:T(8,128)(2,1)}, u32[]{:S(2)}, u32[]{:S(2)}) %collective-permute-start.8) | collective-permute-done | bytes 524320 | tf_op jit(solution)/shard_map/ppermute | solution.py:625
  150.6 4.6 %expert_in.1.activated_ref = bf16[512,512]{1,0:T(8,128)(2,1)S(1)} custom-call(s32[4]{0:T(128)S(1)} %pad_add_fusion.order_ref, bf16[512,2048]{1,0:T(8,128)(2,1)S(1)} %bitcast.20, bf16[512,1024]{1,0:T(8,128)(2,1)} %copy-done.5, bf16[512,1024]{1,0:T(8,128)(2,1)} %copy-done.6, bf16[512,1024]{1,0:T(8,128)(2,1)} %copy-done.7, ...), custom_call_target="tpu_custom_call" | custom-call | tf_op jit(solution)/shard_map/expert_in/pallas_call | solution.py:558
  155.2 2.5 %collective-permute-done.9.refs_3_ = bf16[512,512]{1,0:T(8,128)(2,1)} collective-permute-done((bf16[512,512]{1,0:T(8,128)(2,1)}, bf16[512,512]{1,0:T(8,128)(2,1)}, u32[]{:S(2)}, u32[]{:S(2)}) %collective-permute-start.9) | collective-permute-done | bytes 524320 | tf_op jit(solution)/shard_map/ppermute | solution.py:632
  157.7 3.4 %expert_out.1 = bf16[512,2048]{1,0:T(8,128)(2,1)S(1)} custom-call(s32[4]{0:T(128)S(1)} %pad_add_fusion.order_ref, bf16[512,512]{1,0:T(8,128)(2,1)S(1)} %expert_in.1.activated_ref, bf16[512,512]{1,0:T(8,128)(2,1)} %collective-permute-done.3.refs_0_, bf16[512,512]{1,0:T(8,128)(2,1)} %copy-done.8, bf16[512,512]{1,0:T(8,128)(2,1)} %collective-permute-done.8.refs_2_, ...), custom_call_target="tpu_custom_call" | custom-call | tf_op jit(solution)/shard_map/expert_out/pallas_call | solution.py:558
  161.1 29.1 %all_to_all.32 = bf16[8,64,2048]{2,1,0:T(8,128)(2,1)S(1)} all-to-all(bf16[8,64,2048]{2,1,0:T(8,128)(2,1)S(1)} %bitcast.19), channel_id=1, replica_groups=mesh['y'=2,'core'=2,'half'=2,'rest'=4] {'core','rest'}, dimensions={0} | all-to-all | bytes 4194304 | tf_op jit(solution)/shard_map/all_to_all | solution.py:719
  190.2 2.0 %combine.1 = bf16[128,2048]{1,0:T(8,128)(2,1)} custom-call(bf16[128,512]{1,0:T(8,128)(2,1)S(1)} %copy-done.1, bf16[128,512]{1,0:T(8,128)(2,1)S(1)} %copy-done.2, f32[16,128,128]{2,1,0:T(8,128)S(1)} %copy-done, bf16[512,2048]{1,0:T(8,128)(2,1)S(1)} %bitcast.21), custom_call_target="tpu_custom_call" | custom-call | tf_op jit(solution)/shard_map/combine/pallas_call | solution.py:603
  (31 shorter events, 7.1 us)
Async XLA Ops:
  1.5 6.7 %collective-permute-start = (bf16[8,4096]{1,0:T(8,128)(2,1)S(1)}, bf16[8,4096]{1,0:T(8,128)(2,1)S(1)}, u32[]{:S(2)}, u32[]{:S(2)}) collective-permute-start(bf16[8,4096]{1,0:T(8,128)(2,1)S(1)} %slice.3), channel_id=1, source_target_pairs={{0,1},{1,2},{2,3},{3,4},{4,5},{5,6},{6,7},{7,8},{8,9},{9,10},{10,1... | collective-permute-start | bytes 196616 | tf_op jit(solution)/shard_map/ppermute | solution.py:666
  6.3 19.0 %collective-permute-start.1 = (bf16[512,1024]{1,0:T(8,128)(2,1)}, bf16[512,1024]{1,0:T(8,128)(2,1)S(1)}, u32[]{:S(2)}, u32[]{:S(2)}) collective-permute-start(bf16[512,1024]{1,0:T(8,128)(2,1)} %bitcast.32), channel_id=1, source_target_pairs={{0,0},{4,8},{8,4},{12,12},{1,1},{5,9},{9,5},{13,13},{2,2},{6,10},{... | collective-permute-start | bytes 3145736 | tf_op jit(solution)/shard_map/ppermute | solution.py:625
  8.2 26.2 %copy-start.4 = (f32[128]{0:T(128)S(1)}, f32[128]{0:T(128)}, u32[]{:S(2)}) copy-start(f32[128]{0:T(128)} %param.18) | copy-start | bytes 1540
  17.6 41.6 %all-to-all-start = ((bf16[16,272,128]{2,1,0:T(8,128)(2,1)}), bf16[16,272,128]{2,1,0:T(8,128)(2,1)S(1)}, u32[]{:S(2)}, u32[]{:S(2)}) async-start(bf16[16,272,128]{2,1,0:T(8,128)(2,1)} %bitcast.26), calls=%async_computation | async-start | bytes 2228224 | tf_op jit(solution)/shard_map/all_to_all | solution.py:672
  25.4 14.9 %copy-start.5 = (bf16[512,1024]{1,0:T(8,128)(2,1)}, bf16[512,1024]{1,0:T(8,128)(2,1)S(1)}, u32[]{:S(2)}) copy-start(bf16[512,1024]{1,0:T(8,128)(2,1)S(1)} %collective-permute-done.1.refs_0_) | copy-start | bytes 3145732
  25.4 23.6 %collective-permute-start.2 = (bf16[512,1024]{1,0:T(8,128)(2,1)S(1)}, bf16[512,1024]{1,0:T(8,128)(2,1)S(1)}, u32[]{:S(2)}, u32[]{:S(2)}) collective-permute-start(bf16[512,1024]{1,0:T(8,128)(2,1)S(1)} %collective-permute-done.1.refs_0_), channel_id=1, source_target_pairs={{0,16},{16,0},{1,17},{17,1},{2,18},{18,2},{3,19},{19,3},{4,20},{20... | collective-permute-start | bytes 3145736 | tf_op jit(solution)/shard_map/ppermute | solution.py:632
  27.4 12.9 %collective-permute-start.3 = (bf16[512,512]{1,0:T(8,128)(2,1)}, bf16[512,512]{1,0:T(8,128)(2,1)}, u32[]{:S(2)}, u32[]{:S(2)}) collective-permute-start(bf16[512,512]{1,0:T(8,128)(2,1)} %bitcast.34), channel_id=1, source_target_pairs={{0,0},{4,8},{8,4},{12,12},{1,1},{5,9},{9,5},{13,13},{2,2},{6,10},{... | collective-permute-start | bytes 1572872 | tf_op jit(solution)/shard_map/ppermute | solution.py:625
  40.2 70.0 %copy-start.3 = (f32[2048]{0:T(1024)S(1)}, f32[2048]{0:T(1024)}, u32[]{:S(2)}) copy-start(f32[2048]{0:T(1024)} %param.19) | copy-start | bytes 24580
  48.9 10.3 %copy-start.6 = (bf16[512,1024]{1,0:T(8,128)(2,1)}, bf16[512,1024]{1,0:T(8,128)(2,1)S(1)}, u32[]{:S(2)}) copy-start(bf16[512,1024]{1,0:T(8,128)(2,1)S(1)} %collective-permute-done.2.refs_1_) | copy-start | bytes 3145732
  59.2 15.8 %collective-permute-start.4 = (bf16[16,272,128]{2,1,0:T(8,128)(2,1)S(1)}, bf16[16,272,128]{2,1,0:T(8,128)(2,1)S(1)}, u32[]{:S(2)}, u32[]{:S(2)}) collective-permute-start(bf16[16,272,128]{2,1,0:T(8,128)(2,1)S(1)} %all-to-all-done.near_ref), channel_id=1, source_target_pairs={{0,8},{8,0},{1,9},{9,1},{2,10},{10,2},{3,11},{11,3},{4,12},{12,4},... | collective-permute-start | bytes 3342344 | tf_op jit(solution)/shard_map/ppermute | solution.py:689
  72.6 30.1 %collective-permute-start.5 = (bf16[512,1024]{1,0:T(8,128)(2,1)}, bf16[512,1024]{1,0:T(8,128)(2,1)S(1)}, u32[]{:S(2)}, u32[]{:S(2)}) collective-permute-start(bf16[512,1024]{1,0:T(8,128)(2,1)} %bitcast.33), channel_id=1, source_target_pairs={{0,4},{4,12},{8,0},{12,8},{1,5},{5,13},{9,1},{13,9},{2,6},{6,14},{... | collective-permute-start | bytes 3145736 | tf_op jit(solution)/shard_map/ppermute | solution.py:625
  80.1 30.2 %all-to-all-start.1 = ((bf16[32,64,128]{2,1,0:T(8,128)(2,1)}), bf16[32,64,128]{2,1,0:T(8,128)(2,1)S(1)}, u32[]{:S(2)}, u32[]{:S(2)}) async-start(bf16[32,64,128]{2,1,0:T(8,128)(2,1)} %scan_states.1), calls=%async_computation.1 | async-start | bytes 1048576 | tf_op jit(solution)/shard_map/all_to_all | solution.py:692
  83.6 19.1 %collective-permute-start.6 = (bf16[512,512]{1,0:T(8,128)(2,1)}, bf16[512,512]{1,0:T(8,128)(2,1)S(1)}, u32[]{:S(2)}, u32[]{:S(2)}) collective-permute-start(bf16[512,512]{1,0:T(8,128)(2,1)} %collective-permute-done.3.refs_0_), channel_id=1, source_target_pairs={{0,16},{16,0},{1,17},{17,1},{2,18},{18,2},{3,19},{19,3},{4,20},{20... | collective-permute-start | bytes 1572872 | tf_op jit(solution)/shard_map/ppermute | solution.py:632
  102.7 12.6 %copy-start.8 = (bf16[512,512]{1,0:T(8,128)(2,1)}, bf16[512,512]{1,0:T(8,128)(2,1)S(1)}, u32[]{:S(2)}) copy-start(bf16[512,512]{1,0:T(8,128)(2,1)S(1)} %collective-permute-done.6.refs_1_) | copy-start | bytes 1572868
  102.7 16.2 %copy-start.7 = (bf16[512,1024]{1,0:T(8,128)(2,1)}, bf16[512,1024]{1,0:T(8,128)(2,1)S(1)}, u32[]{:S(2)}) copy-start(bf16[512,1024]{1,0:T(8,128)(2,1)S(1)} %collective-permute-done.5.refs_2_) | copy-start | bytes 3145732
  115.3 35.3 %all-to-all-start.2 = ((bf16[8,64,2048]{2,1,0:T(8,128)(2,1)}), bf16[8,64,2048]{2,1,0:T(8,128)(2,1)S(1)}, u32[]{:S(2)}, u32[]{:S(2)}) async-start(bf16[8,64,2048]{2,1,0:T(8,128)(2,1)} %bitcast.25), calls=%async_computation.2 | async-start | bytes 4194304 | tf_op jit(solution)/shard_map/all_to_all | solution.py:717
  118.9 30.2 %collective-permute-start.7 = (bf16[512,1024]{1,0:T(8,128)(2,1)S(1)}, bf16[512,1024]{1,0:T(8,128)(2,1)}, u32[]{:S(2)}, u32[]{:S(2)}) collective-permute-start(bf16[512,1024]{1,0:T(8,128)(2,1)S(1)} %collective-permute-done.5.refs_2_), channel_id=1, source_target_pairs={{0,16},{16,0},{1,17},{17,1},{2,18},{18,2},{3,19},{19,3},{4,20},{20... | collective-permute-start | bytes 3145736 | tf_op jit(solution)/shard_map/ppermute | solution.py:632
  119.9 28.3 %collective-permute-start.8 = (bf16[512,512]{1,0:T(8,128)(2,1)}, bf16[512,512]{1,0:T(8,128)(2,1)}, u32[]{:S(2)}, u32[]{:S(2)}) collective-permute-start(bf16[512,512]{1,0:T(8,128)(2,1)} %bitcast.35), channel_id=1, source_target_pairs={{0,4},{4,12},{8,0},{12,8},{1,5},{5,13},{9,1},{13,9},{2,6},{6,14},{... | collective-permute-start | bytes 1572872 | tf_op jit(solution)/shard_map/ppermute | solution.py:625
  148.2 9.5 %collective-permute-start.9 = (bf16[512,512]{1,0:T(8,128)(2,1)}, bf16[512,512]{1,0:T(8,128)(2,1)}, u32[]{:S(2)}, u32[]{:S(2)}) collective-permute-start(bf16[512,512]{1,0:T(8,128)(2,1)} %collective-permute-done.8.refs_2_), channel_id=1, source_target_pairs={{0,16},{16,0},{1,17},{17,1},{2,18},{18,2},{3,19},{19,3},{4,20},{20... | collective-permute-start | bytes 1572872 | tf_op jit(solution)/shard_map/ppermute | solution.py:632
  161.1 29.1 %copy-start = (f32[16,128,128]{2,1,0:T(8,128)S(1)}, f32[16,128,128]{2,1,0:T(8,128)}, u32[]{:S(2)}) copy-start(f32[16,128,128]{2,1,0:T(8,128)} %get-tuple-element.51.middle_ref) | copy-start | bytes 3145732
  161.1 29.1 %copy-start.1 = (bf16[128,512]{1,0:T(8,128)(2,1)S(1)}, bf16[128,512]{1,0:T(8,128)(2,1)}, u32[]{:S(2)}) copy-start(bf16[128,512]{1,0:T(8,128)(2,1)} %get-tuple-element.49.high_ref) | copy-start | bytes 393220
  161.1 29.1 %copy-start.2 = (bf16[128,512]{1,0:T(8,128)(2,1)S(1)}, bf16[128,512]{1,0:T(8,128)(2,1)}, u32[]{:S(2)}) copy-start(bf16[128,512]{1,0:T(8,128)(2,1)} %get-tuple-element.50.low_ref) | copy-start | bytes 393220
